TPU v7x, 32 devices: a whole 2x2x4 slice. The times are simulated.
32 devices in a mesh: dp: 8 (over y, x, core), expert: 4 (over z).
Axes of the slice: x: 2, y: 2, z: 4, core: 2. Of those that a mesh axis runs over, the one named last changes fastest.
Arguments:
- tokens: bfloat16 [4, 32, 256, 768], P(None, ('dp', 'expert')), may hold values from -6 to 6
- cotangent: bfloat16 [4, 32, 256, 768], P(None, ('dp', 'expert')), may hold values from -6 to 6
- segments: int32 [4, 32, 256], P(None, ('dp', 'expert')), may hold values from 0 to 2, never falling along the last dimension, each value on 1 to 128 neighbouring positions
- routes: int32 [4, 32, 256, 2], P(None, ('dp', 'expert')), may hold values from 0 to 15, as said below
- slots: int32 [4, 32, 256, 2], P(None, ('dp', 'expert')), may hold values from 0 to 39, as said below
- norm1_gain: bfloat16 [768], P('dp'), may hold values from 0.5 to 1.5
- w_query: bfloat16 [768, 768], P('dp'), may hold values from -0.21875 to 0.21875
- w_key: bfloat16 [768, 768], P('dp'), may hold values from -0.21875 to 0.21875
- w_value: bfloat16 [768, 768], P('dp'), may hold values from -0.21875 to 0.21875
- w_out: bfloat16 [768, 768], P('dp'), may hold values from -0.625 to 0.625
- norm2_gain: bfloat16 [768], P('dp'), may hold values from 0.5 to 1.5
- w_router: bfloat16 [768, 16], P('dp'), may hold values from -0.15625 to 0.15625
- shared_gate: bfloat16 [768, 2048], P('dp'), may hold values from -0.21875 to 0.21875
- shared_up: bfloat16 [768, 2048], P('dp'), may hold values from -0.21875 to 0.21875
- shared_down: bfloat16 [2048, 768], P('dp'), may hold values from -0.25 to 0.25
- expert_gate: bfloat16 [16, 768, 2048], P('expert', 'dp'), may hold values from -0.21875 to 0.21875
- expert_up: bfloat16 [16, 768, 2048], P('expert', 'dp'), may hold values from -0.21875 to 0.21875
- expert_down: bfloat16 [16, 2048, 768], P('expert', 'dp'), may hold values from -2 to 2
Outputs:
- layer_out: bfloat16 [4, 32, 256, 768], P(None, ('dp', 'expert'))
- grad_tokens: float32 [4, 32, 256, 768], P(None, ('dp', 'expert'))
- grad_norm1_gain: float32 [768], P('dp')
- grad_w_query: float32 [768, 768], P('dp')
- grad_w_key: float32 [768, 768], P('dp')
- grad_w_value: float32 [768, 768], P('dp')
- grad_w_out: float32 [768, 768], P('dp')
- grad_norm2_gain: float32 [768], P('dp')
- grad_w_router: float32 [768, 16], P('dp')
- grad_shared_gate: float32 [768, 2048], P('dp')
- grad_shared_up: float32 [768, 2048], P('dp')
- grad_shared_down: float32 [2048, 768], P('dp')
- grad_expert_gate: float32 [16, 768, 2048], P('expert', 'dp')
- grad_expert_up: float32 [16, 768, 2048], P('expert', 'dp')
- grad_expert_down: float32 [16, 2048, 768], P('expert', 'dp')
Inputs may be any that keep to these rules, and one draw needn't show every extreme that they name: `routes`: each token names 2 different experts. Within one sequence of one micro-batch every expert is named by at most 40 of the token choices, and some expert by exactly 40; every expert is named somewhere. Within one sequence of one micro-batch the choices that name one expert hold different slots, numbered 0 upward without gaps.
All inputs are finite; a program needn't handle non-finite values.
Results may differ from a plain program's by a relative error of at most 0.023.
Values may be sent and summed in bfloat16 or wider, within the bound.
No kernel may reach another device: no remote copies, remote signals or barrier semaphores. Data moves between devices by JAX's collectives and lax.ppermute only.
A program may use at most 384 MiB of HBM per device.

v0:
```python
import math

import jax
import jax.numpy as jnp
from jax import lax
from jax.sharding import PartitionSpec as P

HEAD_DIM = 64
CAP = 40


epsilon = 1e-06


def rotate(field, head_count, head_width, direction):
    length = field.shape[0]
    half_width = head_width // 2
    frequency = jnp.exp(-jnp.log(10000.0) * jnp.arange(half_width, dtype=jnp.float32) / half_width)
    angles = jnp.arange(length, dtype=jnp.float32)[:, None] * frequency[None, :]
    cosine = jnp.cos(angles)[:, None, :]
    sine_part = direction * jnp.sin(angles)[:, None, :]
    shaped = field.reshape(length, head_count, head_width)
    first = shaped[..., :half_width]
    second = shaped[..., half_width:]
    turned = jnp.concatenate(
        [first * cosine - second * sine_part, second * cosine + first * sine_part], axis=-1
    )
    return turned.reshape(length, head_count * head_width)


def silu_slope(value):
    sigma = jax.nn.sigmoid(value)
    return sigma * (1.0 + value * (1.0 - sigma))


def norm_back(grad_in, unit_rows, inverse, gain_value):
    scaled = grad_in * gain_value
    return inverse * (scaled - unit_rows * jnp.mean(scaled * unit_rows, axis=-1, keepdims=True))


def on_device(
    tokens,
    cotangent,
    segments,
    routes,
    slots,
    norm1_gain,
    w_query,
    w_key,
    w_value,
    w_out,
    norm2_gain,
    w_router,
    shared_gate,
    shared_up,
    shared_down,
    expert_gate,
    expert_up,
    expert_down,
):
    micro_count = tokens.shape[0]
    length = tokens.shape[2]
    model_width = tokens.shape[3]
    owners = lax.axis_size("expert")
    local_experts = expert_gate.shape[0]
    expert_count = owners * local_experts
    capacity = CAP
    head_width = HEAD_DIM
    head_count = model_width // head_width
    score_scale = 1.0 / math.sqrt(head_width)
    gathered = (
        lax.all_gather(norm1_gain, "dp", axis=0, tiled=True),
        lax.all_gather(w_query, "dp", axis=0, tiled=True),
        lax.all_gather(w_key, "dp", axis=0, tiled=True),
        lax.all_gather(w_value, "dp", axis=0, tiled=True),
        lax.all_gather(w_out, "dp", axis=0, tiled=True),
        lax.all_gather(norm2_gain, "dp", axis=0, tiled=True),
        lax.all_gather(w_router, "dp", axis=0, tiled=True),
        lax.all_gather(shared_gate, "dp", axis=0, tiled=True),
        lax.all_gather(shared_up, "dp", axis=0, tiled=True),
        lax.all_gather(shared_down, "dp", axis=0, tiled=True),
        lax.all_gather(expert_gate, "dp", axis=1, tiled=True),
        lax.all_gather(expert_up, "dp", axis=1, tiled=True),
        lax.all_gather(expert_down, "dp", axis=1, tiled=True),
    )
    (
        gain_first,
        query_weight,
        key_weight,
        value_weight,
        output_weight,
        gain_second,
        router_weight,
        common_gate,
        common_up,
        common_down,
        pool_gate,
        pool_up,
        pool_down,
    ) = gathered
    positions = jnp.arange(length, dtype=jnp.int32)
    causal = positions[:, None] >= positions[None, :]
    token_ids = jnp.repeat(positions, routes.shape[3])
    outputs = []
    saved = []
    for micro_index in range(micro_count):
        token_rows = tokens[micro_index, 0].astype(jnp.float32)
        segment_ids = segments[micro_index, 0]
        route_ids = routes[micro_index, 0]
        slot_ids = slots[micro_index, 0]
        allowed = causal & (segment_ids[:, None] == segment_ids[None, :])
        inverse_one = lax.rsqrt(jnp.mean(token_rows * token_rows, axis=-1, keepdims=True) + epsilon)
        normed = (token_rows * inverse_one * gain_first.astype(jnp.float32)).astype(jnp.bfloat16)
        query_pre = jnp.dot(normed, query_weight, preferred_element_type=jnp.float32)
        key_pre = jnp.dot(normed, key_weight, preferred_element_type=jnp.float32)
        value_pre = jnp.dot(normed, value_weight, preferred_element_type=jnp.float32)
        queries = (
            rotate(query_pre, head_count, head_width, 1.0)
            .astype(jnp.bfloat16)
            .reshape(length, head_count, head_width)
        )
        key_rows = (
            rotate(key_pre, head_count, head_width, 1.0)
            .astype(jnp.bfloat16)
            .reshape(length, head_count, head_width)
        )
        values = value_pre.astype(jnp.bfloat16).reshape(length, head_count, head_width)
        scores = (
            jnp.einsum("qhd,khd->hqk", queries, key_rows, preferred_element_type=jnp.float32)
            * score_scale
        )
        scores = jnp.where(allowed[None], scores, -1e30)
        row_max = jnp.max(scores, axis=-1, keepdims=True)
        expo_rows = jnp.exp(scores - row_max)
        row_total = jnp.sum(expo_rows, axis=-1, keepdims=True)
        attn_probs = expo_rows / row_total
        logsum = row_max + jnp.log(row_total)
        attended = (
            jnp.einsum(
                "hqk,khd->qhd",
                attn_probs.astype(jnp.bfloat16),
                values,
                preferred_element_type=jnp.float32,
            )
            .reshape(length, model_width)
            .astype(jnp.bfloat16)
        )
        hidden = token_rows + jnp.dot(attended, output_weight, preferred_element_type=jnp.float32)
        inverse_two = lax.rsqrt(jnp.mean(hidden * hidden, axis=-1, keepdims=True) + epsilon)
        mixed_in = (hidden * inverse_two * gain_second.astype(jnp.float32)).astype(jnp.bfloat16)
        router = jax.nn.softmax(
            jnp.dot(mixed_in, router_weight, preferred_element_type=jnp.float32), axis=-1
        )
        gate_values = jnp.take_along_axis(router, route_ids, axis=1)
        common_g = jnp.dot(mixed_in, common_gate, preferred_element_type=jnp.float32)
        common_u = jnp.dot(mixed_in, common_up, preferred_element_type=jnp.float32)
        shared_inner = (jax.nn.silu(common_g) * common_u).astype(jnp.bfloat16)
        shared_out = jnp.dot(shared_inner, common_down, preferred_element_type=jnp.float32)
        flat_slots = (route_ids * capacity + slot_ids).reshape(-1)
        holder = jnp.zeros((expert_count * capacity,), jnp.int32).at[flat_slots].set(token_ids)
        filled = jnp.zeros((expert_count * capacity,), jnp.float32).at[flat_slots].set(1.0)
        send_rows = jnp.where(
            filled[:, None] > 0.0, jnp.take(mixed_in, holder, axis=0), jnp.zeros((), jnp.bfloat16)
        )
        send_rows = send_rows.reshape(owners, local_experts, capacity, model_width)
        arrived = lax.all_to_all(send_rows, "expert", split_axis=0, concat_axis=0, tiled=True)
        pool_g = jnp.einsum(
            "slcd,ldf->slcf", arrived, pool_gate, preferred_element_type=jnp.float32
        )
        pool_u = jnp.einsum("slcd,ldf->slcf", arrived, pool_up, preferred_element_type=jnp.float32)
        pool_inner = (jax.nn.silu(pool_g) * pool_u).astype(jnp.bfloat16)
        pool_result = jnp.einsum(
            "slcf,lfd->slcd", pool_inner, pool_down, preferred_element_type=jnp.float32
        ).astype(jnp.bfloat16)
        returned = lax.all_to_all(pool_result, "expert", split_axis=0, concat_axis=0, tiled=True)
        picked = jnp.take(returned.reshape(-1, model_width), flat_slots, axis=0)
        picked = picked.reshape(length, route_ids.shape[1], model_width).astype(jnp.float32)
        mixture = jnp.sum(gate_values[:, :, None] * picked, axis=1)
        outputs.append((hidden + shared_out + mixture).astype(jnp.bfloat16))
        saved.append(
            (
                token_rows,
                inverse_one,
                normed,
                queries,
                key_rows,
                values,
                allowed,
                logsum,
                attended,
                hidden,
                inverse_two,
                mixed_in,
                router,
                gate_values,
                route_ids,
                common_g,
                common_u,
                shared_inner,
                flat_slots,
                holder,
                arrived,
                pool_g,
                pool_u,
                picked,
            )
        )
    gathered = (
        lax.all_gather(norm1_gain, "dp", axis=0, tiled=True),
        lax.all_gather(w_query, "dp", axis=0, tiled=True),
        lax.all_gather(w_key, "dp", axis=0, tiled=True),
        lax.all_gather(w_value, "dp", axis=0, tiled=True),
        lax.all_gather(w_out, "dp", axis=0, tiled=True),
        lax.all_gather(norm2_gain, "dp", axis=0, tiled=True),
        lax.all_gather(w_router, "dp", axis=0, tiled=True),
        lax.all_gather(shared_gate, "dp", axis=0, tiled=True),
        lax.all_gather(shared_up, "dp", axis=0, tiled=True),
        lax.all_gather(shared_down, "dp", axis=0, tiled=True),
        lax.all_gather(expert_gate, "dp", axis=1, tiled=True),
        lax.all_gather(expert_up, "dp", axis=1, tiled=True),
        lax.all_gather(expert_down, "dp", axis=1, tiled=True),
    )
    (
        gain_first,
        query_weight,
        key_weight,
        value_weight,
        output_weight,
        gain_second,
        router_weight,
        common_gate,
        common_up,
        common_down,
        pool_gate,
        pool_up,
        pool_down,
    ) = gathered
    grad_sums = [jnp.zeros(piece.shape, jnp.float32) for piece in gathered]
    expert_ids = jnp.arange(expert_count, dtype=jnp.int32)
    grad_inputs = []
    for micro_index in range(micro_count):
        (
            token_rows,
            inverse_one,
            normed,
            queries,
            key_rows,
            values,
            allowed,
            logsum,
            attended,
            hidden,
            inverse_two,
            mixed_in,
            router,
            gate_values,
            route_ids,
            common_g,
            common_u,
            shared_inner,
            flat_slots,
            holder,
            arrived,
            pool_g,
            pool_u,
            picked,
        ) = saved[micro_index]
        grad_rows = cotangent[micro_index, 0].astype(jnp.float32)
        d_gate = jnp.sum(grad_rows[:, None, :] * picked, axis=-1)
        slot_gates = (
            jnp.zeros((expert_count * capacity,), jnp.float32)
            .at[flat_slots]
            .set(gate_values.reshape(-1))
        )
        back_rows = (slot_gates[:, None] * jnp.take(grad_rows, holder, axis=0)).astype(jnp.bfloat16)
        back_rows = back_rows.reshape(owners, local_experts, capacity, model_width)
        d_result = lax.all_to_all(back_rows, "expert", split_axis=0, concat_axis=0, tiled=True)
        pool_inner = (jax.nn.silu(pool_g) * pool_u).astype(jnp.bfloat16)
        grad_sums[12] = grad_sums[12] + jnp.einsum(
            "slcf,slcd->lfd", pool_inner, d_result, preferred_element_type=jnp.float32
        )
        d_pool_inner = jnp.einsum(
            "slcd,lfd->slcf", d_result, pool_down, preferred_element_type=jnp.float32
        )
        d_pool_g = (d_pool_inner * pool_u * silu_slope(pool_g)).astype(jnp.bfloat16)
        d_pool_u = (d_pool_inner * jax.nn.silu(pool_g)).astype(jnp.bfloat16)
        grad_sums[10] = grad_sums[10] + jnp.einsum(
            "slcd,slcf->ldf", arrived, d_pool_g, preferred_element_type=jnp.float32
        )
        grad_sums[11] = grad_sums[11] + jnp.einsum(
            "slcd,slcf->ldf", arrived, d_pool_u, preferred_element_type=jnp.float32
        )
        d_send = (
            jnp.einsum("slcf,ldf->slcd", d_pool_g, pool_gate, preferred_element_type=jnp.float32)
            + jnp.einsum("slcf,ldf->slcd", d_pool_u, pool_up, preferred_element_type=jnp.float32)
        ).astype(jnp.bfloat16)
        d_back = lax.all_to_all(d_send, "expert", split_axis=0, concat_axis=0, tiled=True)
        d_picked = jnp.take(d_back.reshape(-1, model_width), flat_slots, axis=0)
        d_mixed = jnp.sum(
            d_picked.reshape(length, route_ids.shape[1], model_width).astype(jnp.float32), axis=1
        )
        chosen = (route_ids[:, :, None] == expert_ids[None, None, :]).astype(jnp.float32)
        d_router = jnp.sum(d_gate[:, :, None] * chosen, axis=1)
        d_logits = (
            router * (d_router - jnp.sum(router * d_router, axis=-1, keepdims=True))
        ).astype(jnp.bfloat16)
        grad_sums[6] = grad_sums[6] + jnp.einsum(
            "nd,ne->de", mixed_in, d_logits, preferred_element_type=jnp.float32
        )
        d_mixed = d_mixed + jnp.einsum(
            "ne,de->nd", d_logits, router_weight, preferred_element_type=jnp.float32
        )
        d_shared = grad_rows.astype(jnp.bfloat16)
        grad_sums[9] = grad_sums[9] + jnp.einsum(
            "nf,nd->fd", shared_inner, d_shared, preferred_element_type=jnp.float32
        )
        d_common_inner = jnp.einsum(
            "nd,fd->nf", d_shared, common_down, preferred_element_type=jnp.float32
        )
        d_common_g = (d_common_inner * common_u * silu_slope(common_g)).astype(jnp.bfloat16)
        d_common_u = (d_common_inner * jax.nn.silu(common_g)).astype(jnp.bfloat16)
        grad_sums[7] = grad_sums[7] + jnp.einsum(
            "nd,nf->df", mixed_in, d_common_g, preferred_element_type=jnp.float32
        )
        grad_sums[8] = grad_sums[8] + jnp.einsum(
            "nd,nf->df", mixed_in, d_common_u, preferred_element_type=jnp.float32
        )
        d_mixed = d_mixed + jnp.einsum(
            "nf,df->nd", d_common_g, common_gate, preferred_element_type=jnp.float32
        )
        d_mixed = d_mixed + jnp.einsum(
            "nf,df->nd", d_common_u, common_up, preferred_element_type=jnp.float32
        )
        unit_two = hidden * inverse_two
        grad_sums[5] = grad_sums[5] + jnp.sum(d_mixed * unit_two, axis=0)
        d_hidden = grad_rows + norm_back(
            d_mixed, unit_two, inverse_two, gain_second.astype(jnp.float32)
        )
        d_branch = d_hidden.astype(jnp.bfloat16)
        grad_sums[4] = grad_sums[4] + jnp.einsum(
            "nd,ne->de", attended, d_branch, preferred_element_type=jnp.float32
        )
        d_attended = jnp.einsum(
            "ne,de->nd", d_branch, output_weight, preferred_element_type=jnp.float32
        )
        d_attended = d_attended.astype(jnp.bfloat16).reshape(length, head_count, head_width)
        scores = (
            jnp.einsum("qhd,khd->hqk", queries, key_rows, preferred_element_type=jnp.float32)
            * score_scale
        )
        scores = jnp.where(allowed[None], scores, -1e30)
        attn_probs = jnp.exp(scores - logsum)
        d_probs = jnp.einsum("qhd,khd->hqk", d_attended, values, preferred_element_type=jnp.float32)
        d_scores = (
            attn_probs * (d_probs - jnp.sum(attn_probs * d_probs, axis=-1, keepdims=True))
        ).astype(jnp.bfloat16)
        d_queries = (
            jnp.einsum("hqk,khd->qhd", d_scores, key_rows, preferred_element_type=jnp.float32)
            * score_scale
        )
        d_keys = (
            jnp.einsum("hqk,qhd->khd", d_scores, queries, preferred_element_type=jnp.float32)
            * score_scale
        )
        d_values = jnp.einsum(
            "hqk,qhd->khd",
            attn_probs.astype(jnp.bfloat16),
            d_attended,
            preferred_element_type=jnp.float32,
        )
        d_query_pre = rotate(
            d_queries.reshape(length, model_width), head_count, head_width, -1.0
        ).astype(jnp.bfloat16)
        d_key_pre = rotate(
            d_keys.reshape(length, model_width), head_count, head_width, -1.0
        ).astype(jnp.bfloat16)
        d_value_pre = d_values.reshape(length, model_width).astype(jnp.bfloat16)
        grad_sums[1] = grad_sums[1] + jnp.einsum(
            "nd,ne->de", normed, d_query_pre, preferred_element_type=jnp.float32
        )
        grad_sums[2] = grad_sums[2] + jnp.einsum(
            "nd,ne->de", normed, d_key_pre, preferred_element_type=jnp.float32
        )
        grad_sums[3] = grad_sums[3] + jnp.einsum(
            "nd,ne->de", normed, d_value_pre, preferred_element_type=jnp.float32
        )
        d_normed = jnp.einsum(
            "ne,de->nd", d_query_pre, query_weight, preferred_element_type=jnp.float32
        )
        d_normed = d_normed + jnp.einsum(
            "ne,de->nd", d_key_pre, key_weight, preferred_element_type=jnp.float32
        )
        d_normed = d_normed + jnp.einsum(
            "ne,de->nd", d_value_pre, value_weight, preferred_element_type=jnp.float32
        )
        unit_one = token_rows * inverse_one
        grad_sums[0] = grad_sums[0] + jnp.sum(d_normed * unit_one, axis=0)
        grad_inputs.append(
            d_hidden + norm_back(d_normed, unit_one, inverse_one, gain_first.astype(jnp.float32))
        )
    layer_out = jnp.stack(outputs)[:, None]
    grad_tokens = jnp.stack(grad_inputs)[:, None]
    reduced = (
        lax.psum_scatter(
            grad_sums[0].astype(jnp.bfloat16), "dp", scatter_dimension=0, tiled=True
        ).astype(jnp.float32),
        lax.psum_scatter(
            grad_sums[1].astype(jnp.bfloat16), "dp", scatter_dimension=0, tiled=True
        ).astype(jnp.float32),
        lax.psum_scatter(
            grad_sums[2].astype(jnp.bfloat16), "dp", scatter_dimension=0, tiled=True
        ).astype(jnp.float32),
        lax.psum_scatter(
            grad_sums[3].astype(jnp.bfloat16), "dp", scatter_dimension=0, tiled=True
        ).astype(jnp.float32),
        lax.psum_scatter(
            grad_sums[4].astype(jnp.bfloat16), "dp", scatter_dimension=0, tiled=True
        ).astype(jnp.float32),
        lax.psum_scatter(
            grad_sums[5].astype(jnp.bfloat16), "dp", scatter_dimension=0, tiled=True
        ).astype(jnp.float32),
        lax.psum_scatter(
            grad_sums[6].astype(jnp.bfloat16), "dp", scatter_dimension=0, tiled=True
        ).astype(jnp.float32),
        lax.psum_scatter(
            grad_sums[7].astype(jnp.bfloat16), "dp", scatter_dimension=0, tiled=True
        ).astype(jnp.float32),
        lax.psum_scatter(
            grad_sums[8].astype(jnp.bfloat16), "dp", scatter_dimension=0, tiled=True
        ).astype(jnp.float32),
        lax.psum_scatter(
            grad_sums[9].astype(jnp.bfloat16), "dp", scatter_dimension=0, tiled=True
        ).astype(jnp.float32),
        lax.psum_scatter(
            grad_sums[10].astype(jnp.bfloat16), "dp", scatter_dimension=1, tiled=True
        ).astype(jnp.float32),
        lax.psum_scatter(
            grad_sums[11].astype(jnp.bfloat16), "dp", scatter_dimension=1, tiled=True
        ).astype(jnp.float32),
        lax.psum_scatter(
            grad_sums[12].astype(jnp.bfloat16), "dp", scatter_dimension=1, tiled=True
        ).astype(jnp.float32),
    )
    dense_parts = (
        lax.psum(reduced[0].astype(jnp.bfloat16), "expert").astype(jnp.float32),
        lax.psum(reduced[1].astype(jnp.bfloat16), "expert").astype(jnp.float32),
        lax.psum(reduced[2].astype(jnp.bfloat16), "expert").astype(jnp.float32),
        lax.psum(reduced[3].astype(jnp.bfloat16), "expert").astype(jnp.float32),
        lax.psum(reduced[4].astype(jnp.bfloat16), "expert").astype(jnp.float32),
        lax.psum(reduced[5].astype(jnp.bfloat16), "expert").astype(jnp.float32),
        lax.psum(reduced[6].astype(jnp.bfloat16), "expert").astype(jnp.float32),
        lax.psum(reduced[7].astype(jnp.bfloat16), "expert").astype(jnp.float32),
        lax.psum(reduced[8].astype(jnp.bfloat16), "expert").astype(jnp.float32),
        lax.psum(reduced[9].astype(jnp.bfloat16), "expert").astype(jnp.float32),
    )
    pool_parts = (reduced[10], reduced[11], reduced[12])
    return (
        layer_out,
        grad_tokens,
        dense_parts[0],
        dense_parts[1],
        dense_parts[2],
        dense_parts[3],
        dense_parts[4],
        dense_parts[5],
        dense_parts[6],
        dense_parts[7],
        dense_parts[8],
        dense_parts[9],
        pool_parts[0],
        pool_parts[1],
        pool_parts[2],
    )


def solution(mesh):
    placed = (
        P(None, ("dp", "expert"), None, None),
        P(None, ("dp", "expert"), None, None),
        P(None, ("dp", "expert"), None),
        P(None, ("dp", "expert"), None, None),
        P(None, ("dp", "expert"), None, None),
        P("dp"),
        P("dp", None),
        P("dp", None),
        P("dp", None),
        P("dp", None),
        P("dp"),
        P("dp", None),
        P("dp", None),
        P("dp", None),
        P("dp", None),
        P("expert", "dp", None),
        P("expert", "dp", None),
        P("expert", "dp", None),
    )
    return jax.shard_map(
        on_device,
        mesh=mesh,
        in_specs=placed,
        out_specs=(
            P(None, ("dp", "expert"), None, None),
            P(None, ("dp", "expert"), None, None),
            P("dp"),
            P("dp", None),
            P("dp", None),
            P("dp", None),
            P("dp", None),
            P("dp"),
            P("dp", None),
            P("dp", None),
            P("dp", None),
            P("dp", None),
            P("expert", "dp", None),
            P("expert", "dp", None),
            P("expert", "dp", None),
        ),
        check_vma=False,
    )
```

profile of v0, /device:TPU:0, one launch (start us, length us, event | category | flops | bytes accessed | tf_op | source)
XLA Modules:
  0.0 1592.0 jit_solution(10842968683469041927)
XLA Ops:
  47.4 15.6 all-reduce.5
  197.7 64.1 %all-gather.28.cloned.1.call-done = bf16[4,768,2048]{2,1,0:T(8,128)(2,1)} async-done(((bf16[4,96,2048]{2,1,0:T(8,128)(2,1)}), bf16[4,768,2048]{2,1,0:T(8,128)(2,1)}) %all-gather.28.cloned.1.call-update) | async-done | bytes 12582928 | tf_op jit(solution)/shard_map/all_gather | solution.py:83
  261.7 12.9 fusion.69
  274.6 61.0 %all-gather.30.cloned.1.call-done = bf16[4,2048,768]{2,1,0:T(8,128)(2,1)} async-done(((bf16[4,256,768]{2,1,0:T(8,128)(2,1)}), bf16[4,2048,768]{2,1,0:T(8,128)(2,1)}) %all-gather.30.cloned.1.call-update) | async-done | bytes 12582928 | tf_op jit(solution)/shard_map/all_gather | solution.py:84
  352.8 16.9 %all-gather.24.cloned.1.call-done = bf16[2048,768]{1,0:T(8,128)(2,1)} async-done(((bf16[256,768]{1,0:T(8,128)(2,1)}), bf16[2048,768]{1,0:T(8,128)(2,1)}) %all-gather.24.cloned.1.call-update) | async-done | bytes 3145744 | tf_op jit(solution)/shard_map/all_gather | solution.py:81
  374.2 29.7 %all-gather.22.cloned.1.call-done = bf16[768,2048]{1,0:T(8,128)(2,1)} async-done(((bf16[96,2048]{1,0:T(8,128)(2,1)}), bf16[768,2048]{1,0:T(8,128)(2,1)}) %all-gather.22.cloned.1.call-update) | async-done | bytes 3145744 | tf_op jit(solution)/shard_map/all_gather | solution.py:80
  426.8 11.1 all-gather.20.cloned.1.call-done
  451.2 13.7 fusion.55
  501.8 11.8 all-to-all-done.13
  624.3 12.7 fusion.63
  655.1 12.0 fusion.75
  699.7 11.3 fusion.81
  783.3 13.7 fusion.52
  822.6 13.8 fusion.58
  836.4 10.6 fusion.23
  863.4 14.5 fusion.61
  1043.4 14.1 fusion.99
  1059.2 12.4 fusion.101
  1082.0 16.8 %reduce-scatter.16.cloned.1.call-done = bf16[96,768]{1,0:T(8,128)(2,1)} async-done(((bf16[768,768]{1,0:T(8,128)(2,1)}), bf16[96,768]{1,0:T(8,128)(2,1)}) %reduce-scatter.16.cloned.1.call-update) | async-done | bytes 147472 | tf_op jit(solution)/shard_map/reduce_scatter | solution.py:410
  1098.7 40.3 %reduce-scatter.18.cloned.1.call-done = bf16[96,768]{1,0:T(8,128)(2,1)} async-done(((bf16[768,768]{1,0:T(8,128)(2,1)}), bf16[96,768]{1,0:T(8,128)(2,1)}) %reduce-scatter.18.cloned.1.call-update) | async-done | bytes 147472 | tf_op jit(solution)/shard_map/reduce_scatter | solution.py:413
  1139.1 40.3 %reduce-scatter.20.cloned.1.call-done = bf16[96,768]{1,0:T(8,128)(2,1)} async-done(((bf16[768,768]{1,0:T(8,128)(2,1)}), bf16[96,768]{1,0:T(8,128)(2,1)}) %reduce-scatter.20.cloned.1.call-update) | async-done | bytes 147472 | tf_op jit(solution)/shard_map/reduce_scatter | solution.py:416
  1179.7 29.8 %fusion.2 = bf16[4,768,2048]{2,1,0:T(8,128)(2,1)} fusion(f32[4,768,2048,1]{2,1,0,3:T(8,128)} %fusion.99, f32[4,768,2048,1]{2,1,0,3:T(8,128)} %fusion.101, f32[4,768,2048,1]{2,1,0,3:T(8,128)} %fusion.103, bf16[4,4,40,768]{3,2,1,0:T(8,128)(2,1)} %all-to-all-done.6, bf16[4,4,40,2048]{3,2,0,1:T(8,128)(2,1)S(1)} %copy-done.67), kind=kOutput, calls=%fused_computation.41 | convolution fusion | flops 2038431744 | bytes 91684864 | tf_op jit(solution)/shard_map/slcd,slcf->ldf/dot_general | solution.py:287
  1209.6 14.0 fusion.92
  1244.3 30.3 %fusion.1 = bf16[4,768,2048]{2,1,0:T(8,128)(2,1)} fusion(f32[4,768,2048,1]{2,1,0,3:T(8,128)} %fusion.92, f32[4,768,2048,1]{2,1,0,3:T(8,128)} %fusion.94, f32[4,768,2048,1]{2,1,0,3:T(8,128)} %fusion.96, bf16[4,4,40,768]{3,2,1,0:T(8,128)(2,1)} %all-to-all-done.6, bf16[4,4,40,2048]{3,2,0,1:T(8,128)(2,1)S(1)} %copy-done.70), kind=kOutput, calls=%fused_computation.37 | convolution fusion | flops 2038431744 | bytes 91684864 | tf_op jit(solution)/shard_map/slcd,slcf->ldf/dot_general | solution.py:290
  1276.3 11.7 fusion.248
  1288.1 11.6 fusion.251
  1299.7 16.3 %fusion.254 = f32[4,2048,768,1]{2,1,3,0:T(8,128)} fusion(bf16[4,4,40,2048]{3,2,0,1:T(8,128)(2,1)S(1)} %copy-done.172, bf16[4,4,40,768]{3,2,1,0:T(8,128)(2,1)} %all-to-all-done.8), kind=kOutput, calls=%fused_computation.391 | convolution fusion | flops 2013265920 | bytes 28770304 | tf_op jit(solution)/shard_map/slcf,slcd->lfd/dot_general | solution.py:279
  1315.9 31.7 %fusion = bf16[4,2048,768]{2,1,0:T(8,128)(2,1)} fusion(f32[4,2048,768,1]{2,1,3,0:T(8,128)} %fusion.248, f32[4,2048,768,1]{2,1,3,0:T(8,128)} %fusion.251, f32[4,2048,768,1]{2,1,3,0:T(8,128)} %fusion.254, bf16[4,4,40,2048]{3,2,0,1:T(8,128)(2,1)S(1)} %copy-done.69, bf16[4,4,40,768]{3,2,1,0:T(8,128)(2,1)} %all-to-all-done.14), kind=kOutput, calls=%fused_computation.33 | convolution fusion | flops 2038431744 | bytes 91684864 | tf_op jit(solution)/shard_map/slcf,slcd->lfd/dot_general | solution.py:279
  1379.3 14.9 all-reduce.4
  1396.7 12.7 all-reduce.6
  1444.7 41.1 %reduce-scatter.30.cloned.1.call-done = bf16[4,96,2048]{2,1,0:T(8,128)(2,1)} async-done(((bf16[4,768,2048]{2,1,0:T(8,128)(2,1)}), bf16[4,96,2048]{2,1,0:T(8,128)(2,1)}) %reduce-scatter.30.cloned.1.call-update) | async-done | bytes 1572880 | tf_op jit(solution)/shard_map/reduce_scatter | solution.py:437
  1489.2 92.4 %reduce-scatter.32.cloned.1.call-done = bf16[4,256,768]{2,1,0:T(8,128)(2,1)} async-done(((bf16[4,2048,768]{2,1,0:T(8,128)(2,1)}), bf16[4,256,768]{2,1,0:T(8,128)(2,1)}) %reduce-scatter.32.cloned.1.call-update) | async-done | bytes 1572880 | tf_op jit(solution)/shard_map/reduce_scatter | solution.py:440
  (1372 shorter events, 815.0 us)
Async XLA Ops:
  7.2 107.5 %all-gather.14.cloned.1.call-start = ((), (), s32[]{:S(2)}) async-start(), calls=%async_computation.28 | async-start | bytes 1327104 | tf_op jit(solution)/shard_map/all_gather | solution.py:73
  7.9 108.3 %all-gather.16.cloned.1.call-start = ((), (), s32[]{:S(2)}) async-start(), calls=%async_computation.29 | async-start | bytes 1327104 | tf_op jit(solution)/shard_map/all_gather | solution.py:74
  8.7 122.2 %all-gather.12.cloned.1.call-start = ((), (), s32[]{:S(2)}) async-start(), calls=%async_computation.27 | async-start | bytes 1327104 | tf_op jit(solution)/shard_map/all_gather | solution.py:75
  9.4 129.5 %all-gather.18.cloned.1.call-start = ((), (), s32[]{:S(2)}) async-start(), calls=%async_computation.30 | async-start | bytes 1327104 | tf_op jit(solution)/shard_map/all_gather | solution.py:76
  10.0 177.9 %all-gather.26.cloned.1.call-start = ((), (), s32[]{:S(2)}) async-start(), calls=%async_computation.34 | async-start | bytes 14155776 | tf_op jit(solution)/shard_map/all_gather | solution.py:82
  10.6 251.1 %all-gather.28.cloned.1.call-start = ((), (), s32[]{:S(2)}) async-start(), calls=%async_computation.35 | async-start | bytes 14155776 | tf_op jit(solution)/shard_map/all_gather | solution.py:83
  11.2 324.5 %all-gather.30.cloned.1.call-start = ((), (), s32[]{:S(2)}) async-start(), calls=%async_computation.36 | async-start | bytes 14155776 | tf_op jit(solution)/shard_map/all_gather | solution.py:84
  11.9 357.9 %all-gather.24.cloned.1.call-start = ((), (), s32[]{:S(2)}) async-start(), calls=%async_computation.33 | async-start | bytes 3538944 | tf_op jit(solution)/shard_map/all_gather | solution.py:81
  12.7 391.2 %all-gather.22.cloned.1.call-start = ((), (), s32[]{:S(2)}) async-start(), calls=%async_computation.32 | async-start | bytes 3538944 | tf_op jit(solution)/shard_map/all_gather | solution.py:80
  13.4 424.4 %all-gather.20.cloned.1.call-start = ((), (), s32[]{:S(2)}) async-start(), calls=%async_computation.31 | async-start | bytes 3538944 | tf_op jit(solution)/shard_map/all_gather | solution.py:79
  150.0 29.9 %all-to-all-start.4 = ((bf16[4,4,40,768]{3,2,1,0:T(8,128)(2,1)}), bf16[4,4,40,768]{3,2,1,0:T(8,128)(2,1)}, u32[]{:S(2)}, u32[]{:S(2)}) async-start(bf16[4,4,40,768]{3,2,1,0:T(8,128)(2,1)} %bitcast.917), calls=%async_computation.4 | async-start | bytes 1966080 | tf_op jit(solution)/shard_map/all_to_all | solution.py:166
  344.3 63.8 %all-to-all-start.5 = ((bf16[4,4,40,768]{3,2,1,0:T(8,128)(2,1)}), bf16[4,4,40,768]{3,2,1,0:T(8,128)(2,1)S(1)}, u32[]{:S(2)}, u32[]{:S(2)}) async-start(bf16[4,4,40,768]{3,2,1,0:T(8,128)(2,1)} %copy.222), calls=%async_computation.5 | async-start | bytes 1966080 | tf_op jit(solution)/shard_map/all_to_all | solution.py:175
  421.8 29.4 %all-to-all-start.12 = ((bf16[4,4,40,768]{3,2,1,0:T(8,128)(2,1)}), bf16[4,4,40,768]{3,2,1,0:T(8,128)(2,1)}, u32[]{:S(2)}, u32[]{:S(2)}) async-start(bf16[4,4,40,768]{3,2,1,0:T(8,128)(2,1)} %bitcast.112), calls=%async_computation.12 | async-start | bytes 1966080 | tf_op jit(solution)/shard_map/all_to_all | solution.py:277
  485.5 28.1 %all-to-all-start.13 = ((bf16[4,4,40,768]{3,2,1,0:T(8,128)(2,1)}), bf16[4,4,40,768]{3,2,1,0:T(8,128)(2,1)S(1)}, u32[]{:S(2)}, u32[]{:S(2)}) async-start(bf16[4,4,40,768]{3,2,1,0:T(8,128)(2,1)} %copy.247), calls=%async_computation.13 | async-start | bytes 1966080 | tf_op jit(solution)/shard_map/all_to_all | solution.py:297
  489.0 592.9 %reduce-scatter.22.cloned.1.call-start = ((), (), s32[]{:S(2)}) async-start(), calls=%async_computation.41 | async-start | bytes 3538944 | tf_op jit(solution)/shard_map/reduce_scatter | solution.py:425
  553.5 528.4 %reduce-scatter.24.cloned.1.call-start = ((), (), s32[]{:S(2)}) async-start(), calls=%async_computation.42 | async-start | bytes 3538944 | tf_op jit(solution)/shard_map/reduce_scatter | solution.py:428
  584.6 28.0 %all-to-all-start.6 = ((bf16[4,4,40,768]{3,2,1,0:T(8,128)(2,1)}), bf16[4,4,40,768]{3,2,1,0:T(8,128)(2,1)}, u32[]{:S(2)}, u32[]{:S(2)}) async-start(bf16[4,4,40,768]{3,2,1,0:T(8,128)(2,1)} %bitcast.918), calls=%async_computation.6 | async-start | bytes 1966080 | tf_op jit(solution)/shard_map/all_to_all | solution.py:166
  588.8 493.2 %reduce-scatter.26.cloned.1.call-start = ((), (), s32[]{:S(2)}) async-start(), calls=%async_computation.43 | async-start | bytes 3538944 | tf_op jit(solution)/shard_map/reduce_scatter | solution.py:431
  612.5 27.9 %all-to-all-start.2 = ((bf16[4,4,40,768]{3,2,1,0:T(8,128)(2,1)}), bf16[4,4,40,768]{3,2,1,0:T(8,128)(2,1)S(1)}, u32[]{:S(2)}, u32[]{:S(2)}) async-start(bf16[4,4,40,768]{3,2,1,0:T(8,128)(2,1)} %bitcast.40), calls=%async_computation.2 | async-start | bytes 1966080 | tf_op jit(solution)/shard_map/all_to_all | solution.py:166
  750.9 28.2 %all-to-all-start.14 = ((bf16[4,4,40,768]{3,2,1,0:T(8,128)(2,1)}), bf16[4,4,40,768]{3,2,1,0:T(8,128)(2,1)}, u32[]{:S(2)}, u32[]{:S(2)}) async-start(bf16[4,4,40,768]{3,2,1,0:T(8,128)(2,1)} %bitcast.919), calls=%async_computation.14 | async-start | bytes 1966080 | tf_op jit(solution)/shard_map/all_to_all | solution.py:277
  779.1 38.3 %all-to-all-start.10 = ((bf16[4,4,40,768]{3,2,1,0:T(8,128)(2,1)}), bf16[4,4,40,768]{3,2,1,0:T(8,128)(2,1)}, u32[]{:S(2)}, u32[]{:S(2)}) async-start(bf16[4,4,40,768]{3,2,1,0:T(8,128)(2,1)} %bitcast.99), calls=%async_computation.10 | async-start | bytes 1966080 | tf_op jit(solution)/shard_map/all_to_all | solution.py:277
  817.4 40.5 %all-to-all-start.8 = ((bf16[4,4,40,768]{3,2,1,0:T(8,128)(2,1)}), bf16[4,4,40,768]{3,2,1,0:T(8,128)(2,1)}, u32[]{:S(2)}, u32[]{:S(2)}) async-start(bf16[4,4,40,768]{3,2,1,0:T(8,128)(2,1)} %bitcast.920), calls=%async_computation.8 | async-start | bytes 1966080 | tf_op jit(solution)/shard_map/all_to_all | solution.py:277
  857.9 28.2 %all-to-all-start.15 = ((bf16[4,4,40,768]{3,2,1,0:T(8,128)(2,1)}), bf16[4,4,40,768]{3,2,1,0:T(8,128)(2,1)S(1)}, u32[]{:S(2)}, u32[]{:S(2)}) async-start(bf16[4,4,40,768]{3,2,1,0:T(8,128)(2,1)} %copy.255), calls=%async_computation.15 | async-start | bytes 1966080 | tf_op jit(solution)/shard_map/all_to_all | solution.py:297
  917.1 164.9 %reduce-scatter.14.cloned.1.call-start = ((), (), s32[]{:S(2)}) async-start(), calls=%async_computation.37 | async-start | bytes 1327104 | tf_op jit(solution)/shard_map/reduce_scatter | solution.py:407
  1023.4 75.3 %reduce-scatter.16.cloned.1.call-start = ((), (), s32[]{:S(2)}) async-start(), calls=%async_computation.38 | async-start | bytes 1327104 | tf_op jit(solution)/shard_map/reduce_scatter | solution.py:410
  1031.4 107.7 %reduce-scatter.18.cloned.1.call-start = ((), (), s32[]{:S(2)}) async-start(), calls=%async_computation.39 | async-start | bytes 1327104 | tf_op jit(solution)/shard_map/reduce_scatter | solution.py:413
  1038.1 141.3 %reduce-scatter.20.cloned.1.call-start = ((), (), s32[]{:S(2)}) async-start(), calls=%async_computation.40 | async-start | bytes 1327104 | tf_op jit(solution)/shard_map/reduce_scatter | solution.py:416
  1043.4 314.8 %reduce-scatter.34.cloned.1.call-start = ((), (), s32[]{:S(2)}) async-start(), calls=%async_computation.47 | async-start | bytes 221184
  1059.1 371.6 %all-reduce.10.cloned.1.call-start = ((), (), s32[]{:S(2)}) async-start(), calls=%async_computation.48 | async-start | bytes 3538944 | tf_op jit(solution)/shard_map/psum | solution.py:446
  1179.4 261.8 %reduce-scatter.28.cloned.1.call-start = ((), (), s32[]{:S(2)}) async-start(), calls=%async_computation.44 | async-start | bytes 14155776 | tf_op jit(solution)/shard_map/reduce_scatter | solution.py:434
  1209.5 276.2 %reduce-scatter.30.cloned.1.call-start = ((), (), s32[]{:S(2)}) async-start(), calls=%async_computation.45 | async-start | bytes 14155776 | tf_op jit(solution)/shard_map/reduce_scatter | solution.py:437
  1274.6 307.0 %reduce-scatter.32.cloned.1.call-start = ((), (), s32[]{:S(2)}) async-start(), calls=%async_computation.46 | async-start | bytes 14155776 | tf_op jit(solution)/shard_map/reduce_scatter | solution.py:440
  (440 other events, 4426.5 us)
Sparse Core Ops, SparseCore 0:
  9.9 26.6 all-gather.13
  38.4 23.9 all-gather.15
  64.3 24.0 all-gather.11
  90.1 23.9 all-gather.17
  115.9 71.9 all-gather.25
  189.7 71.9 all-gather.27
  263.6 71.9 all-gather.29
  337.5 32.2 all-gather.23
  371.7 32.1 all-gather.21
  405.6 32.1 all-gather.19
  553.6 44.1 reduce-scatter.21
  601.1 46.0 reduce-scatter.23
  650.6 46.0 reduce-scatter.25
  1023.5 34.8 reduce-scatter.13
  1062.0 36.6 reduce-scatter.15
  1102.4 36.6 reduce-scatter.17
  1142.7 36.6 reduce-scatter.19
  1182.9 33.6 reduce-scatter.33
  1219.5 75.7 all-reduce.9
  1298.6 91.2 reduce-scatter.27
  1393.5 92.2 reduce-scatter.29
  1489.3 92.2 reduce-scatter.31
where the time goes:
time: 1600 us; the launch traced here: 1590 us
  matrix products  631 us (39%)
  waiting for transfers between devices  487 us (30%)
  local copies, waits for them, and re-layouts  209 us (13%)
  other arithmetic  121 us (8%)
  starting transfers between devices  72 us (4%)
  blocking collectives  51.5 us (3%)
  between operations  21.2 us (1%)
    reduce_scatter x1, waiting for transfers between devices, on_device(): lax.psum_scatter(grad_sums[12].astype(jnp.bfloat16), 'dp', scatter_dimens...  92.4 us
    dot_general x4, matrix products, on_device(): jnp.einsum('slcf,slcd->lfd', pool_inner, d_result, preferred_element_type...  71.3 us
    dot_general x4, matrix products, on_device(): jnp.einsum('slcd,slcf->ldf', arrived, d_pool_g, preferred_element_type=jn...  66.6 us
    dot_general x4, matrix products, on_device(): jnp.einsum('slcd,slcf->ldf', arrived, d_pool_u, preferred_element_type=jn...  64.9 us
    all_gather x1, waiting for transfers between devices, on_device(): lax.all_gather(expert_up, 'dp', axis=1, tiled=True)  64.1 us
    all_gather x1, waiting for transfers between devices, on_device(): lax.all_gather(expert_down, 'dp', axis=1, tiled=True)  61 us
    dot_general x4, matrix products, on_device(): jnp.einsum('slcd,lfd->slcf', d_result, pool_down, preferred_element_type=...  55.7 us
    dot_general x4, matrix products, on_device(): jnp.einsum('slcd,ldf->slcf', arrived, pool_up, preferred_element_type=jnp...  48.9 us
  transfers between devices with their start and end apart: 38, of which 23 were waited for; matrix products, arithmetic and copies ran while one was open for 53% of the time, Pallas kernels for 0%

commit v1 on v0

v1 whole, which is shorter than its diff:
```python
import functools
import math

import jax
import jax.numpy as jnp
from jax import lax
from jax.experimental import pallas as pl
from jax.experimental.pallas import tpu as pltpu
from jax.sharding import PartitionSpec as P

HEAD_DIM = 64
PAIR = 2 * HEAD_DIM
CAP = 40
LANES = 128
EPSILON = 1e-06
F32 = jnp.float32
BF16 = jnp.bfloat16
NN = (((1,), (0,)), ((), ()))
NT = (((1,), (1,)), ((), ()))
TN = (((0,), (0,)), ((), ()))
VMEM_BYTES = 60 * 1024 * 1024
ANY = pl.BlockSpec(memory_space=pl.ANY)


def mm(left, right, dims):
    return lax.dot_general(left, right, dims, preferred_element_type=F32)


def iota(shape, axis):
    return lax.broadcasted_iota(jnp.int32, shape, axis)


def first_step(i):
    return i ^ (2 if i % 2 == 0 else 4)


def second_step(i):
    return i ^ (4 if i % 2 == 0 else 2)


def core_step(i):
    return i ^ 1


def send(field, step):
    return lax.ppermute(field, "dp", [(i, step(i)) for i in range(8)])


def place_kernel(where, *refs):
    pieces, (out, held, came, left) = refs[:8], refs[8:]
    loads = [pltpu.make_async_copy(pieces[k], held.at[k], came.at[k]) for k in range(8)]
    stores = [pltpu.make_async_copy(held.at[k], out.at[where[k]], left.at[k]) for k in range(8)]
    for load in loads:
        load.start()
    for load, store in zip(loads, stores):
        load.wait()
        store.start()
    for store in stores:
        store.wait()


def gather_rows(part):
    count = lax.axis_size("dp")
    if count != 8:
        return lax.all_gather(part, "dp", axis=0)
    near = send(part, first_step)
    side = send(part, second_step)
    far = send(near, second_step)
    mine = [part, near, side, far]
    pieces = mine + [send(piece, core_step) for piece in mine]
    index = lax.axis_index("dp")
    even = jnp.array([0, 2, 4, 6], jnp.int32)
    odd = jnp.array([0, 4, 2, 6], jnp.int32)
    own = jnp.where(index % 2 == 0, even, odd)
    other = jnp.where(index % 2 == 0, odd, even)
    where = jnp.concatenate([index ^ own, (index ^ 1) ^ other]).astype(jnp.int32)
    size = part.size * part.dtype.itemsize * 8
    return pl.pallas_call(
        place_kernel,
        out_shape=jax.ShapeDtypeStruct((8,) + part.shape, part.dtype),
        in_specs=[pl.BlockSpec(memory_space=pltpu.SMEM)] + [ANY] * 8,
        out_specs=ANY,
        scratch_shapes=[
            pltpu.VMEM((8,) + part.shape, part.dtype),
            pltpu.SemaphoreType.DMA((8,)),
            pltpu.SemaphoreType.DMA((8,)),
        ],
        cost_estimate=pl.CostEstimate(flops=0, bytes_accessed=2 * size, transcendentals=0),
        name="place",
    )(where, *pieces)


def scatter_rows(field):
    count = lax.axis_size("dp")
    if count != 8:
        return lax.psum_scatter(field, "dp", scatter_dimension=0, tiled=False)
    index = lax.axis_index("dp")
    core, x, y = index % 2, (index // 2) % 2, index // 4
    take = functools.partial(lax.dynamic_index_in_dim, keepdims=False)
    blocks = field.reshape((4, 2) + field.shape[1:])
    came = send(take(blocks, 1 - core, 1), core_step)
    total = (take(blocks, core, 1).astype(F32) + came.astype(F32)).astype(BF16)
    one, two = jnp.where(core == 0, x, y), jnp.where(core == 0, y, x)

    def at(first, second):
        return take(total, jnp.where(core == 0, second * 2 + first, first * 2 + second), 0)

    came = send(jnp.stack([at(1 - one, two), at(1 - one, 1 - two)]), first_step).astype(F32)
    keep = (at(one, two).astype(F32) + came[0]).astype(BF16)
    pass_on = (at(one, 1 - two).astype(F32) + came[1]).astype(BF16)
    return (keep.astype(F32) + send(pass_on, second_step).astype(F32)).astype(BF16)


def place_of(flat, rows):
    at = iota((rows, flat.shape[1]), 0)
    held = jnp.logical_or(flat[0:1, :] == at, flat[1:2, :] == at)
    return jnp.where(held, 1.0, 0.0).astype(BF16)


def put_rows(sent, outs):
    at = 0
    for out in outs:
        for expert in range(out.shape[0]):
            out[expert, 0] = sent[at : at + CAP].astype(BF16)
            at += CAP


def dispatch_kernel(flat_ref, field_ref, *outs):
    rows = len(outs) * outs[0].shape[0] * CAP
    put_rows(mm(place_of(flat_ref[0], rows), field_ref[0], NN), outs)


def swap_halves(field):
    low = iota(field.shape, 1) % HEAD_DIM < HEAD_DIM // 2
    ahead = pltpu.roll(field, PAIR - HEAD_DIM // 2, 1)
    behind = pltpu.roll(field, HEAD_DIM // 2, 1)
    return jnp.where(low, ahead, behind)


def turn(field, cosine, sine):
    return field * cosine + swap_halves(field) * sine


def allowed_of(column_ref, row_ref):
    length = row_ref.shape[2]
    square = (length, length)
    return jnp.logical_and(iota(square, 0) >= iota(square, 1), column_ref[0] == row_ref[0])


def inverse_rms(field):
    return lax.rsqrt(jnp.mean(field * field, axis=-1, keepdims=True) + EPSILON)


def forward_kernel(
    experts, tokens_ref, column_ref, row_ref, flat_ref, weight_ref, gain_one_ref, gain_two_ref, cosine_ref, sine_ref,
    hidden_ref, mixed_ref, attended_ref, qkv_ref, logsum_ref, router_ref, *outs,
):
    width = tokens_ref.shape[2]
    x = tokens_ref[0].astype(F32)
    normed = (x * inverse_rms(x) * gain_one_ref[...]).astype(BF16)
    allowed = allowed_of(column_ref, row_ref)
    cosine, sine = cosine_ref[...], sine_ref[...]
    low = iota((x.shape[0], PAIR), 1) < HEAD_DIM
    lane = iota((x.shape[0], LANES), 1)
    logsum = jnp.zeros((x.shape[0], LANES), F32)
    for pair in range(width // PAIR):
        at = slice(pair * PAIR, (pair + 1) * PAIR)
        query = turn(mm(normed, weight_ref[:, at], NN), cosine, sine).astype(BF16) * BF16(0.125)
        key = turn(mm(normed, weight_ref[:, width + at.start : width + at.stop], NN), cosine, sine).astype(BF16)
        value = mm(normed, weight_ref[:, 2 * width + at.start : 2 * width + at.stop], NN).astype(BF16)
        qkv_ref[0, :, at] = query
        qkv_ref[0, :, width + at.start : width + at.stop] = key
        qkv_ref[0, :, 2 * width + at.start : 2 * width + at.stop] = value
        both = []
        for half in range(2):
            mine = low if half == 0 else jnp.logical_not(low)
            scores = jnp.where(allowed, mm(jnp.where(mine, query, BF16(0.0)), key, NT), -1e30)
            peak = jnp.max(scores, axis=-1, keepdims=True)
            expo = jnp.exp(scores - peak)
            total = jnp.sum(expo, axis=-1, keepdims=True)
            logsum = jnp.where(lane == 2 * pair + half, peak + jnp.log(total), logsum)
            both.append(mm((expo * (1.0 / total)).astype(BF16), value, NN))
        attended_ref[0, :, at] = jnp.where(low, both[0], both[1]).astype(BF16)
    logsum_ref[0] = logsum
    hidden = x + mm(attended_ref[0], weight_ref[:, 3 * width : 4 * width], NN)
    hidden_ref[0] = hidden
    mixed = (hidden * inverse_rms(hidden) * gain_two_ref[...]).astype(BF16)
    mixed_ref[0] = mixed
    logits = jnp.where(lane < experts, mm(mixed, weight_ref[:, 4 * width :], NN), -1e30)
    expo = jnp.exp(logits - jnp.max(logits, axis=-1, keepdims=True))
    router_ref[0] = expo / jnp.sum(expo, axis=-1, keepdims=True)
    put_rows(mm(place_of(flat_ref[0], experts * CAP), mixed, NN), outs)


def get_rows(pieces, held_ref):
    at = 0
    for piece in pieces:
        for expert in range(piece.shape[0]):
            held_ref[at : at + CAP, :] = piece[expert, 0].astype(F32)
            at += CAP
    return held_ref[...].astype(BF16)


def backward_kernel(
    experts, count, tokens_ref, grad_ref, column_ref, row_ref, flat_ref, routes_ref, weight_ref, gain_one_ref, gain_two_ref,
    cosine_ref, sine_ref, hidden_ref, mixed_ref, attended_ref, qkv_ref, logsum_ref, router_ref, shared_ref, d_mixed_ref, *refs,
):
    returned, d_back = refs[:count], refs[count : 2 * count]
    out_ref, grad_tokens_ref, grad_weight_ref, held_ref, sum_ref, gains_ref, d_qkv_ref = refs[2 * count :]
    width = tokens_ref.shape[2]
    step = pl.program_id(0)

    @pl.when(step == 0)
    def _():
        sum_ref[...] = jnp.zeros_like(sum_ref)
        gains_ref[...] = jnp.zeros_like(gains_ref)

    length = tokens_ref.shape[1]
    lane = iota((length, LANES), 1)
    grad = grad_ref[0].astype(F32)
    hidden = hidden_ref[0]
    mixed = mixed_ref[0]
    router = router_ref[0]
    flat = flat_ref[0]
    rows = experts * CAP
    at_row = iota((rows, length), 0)
    came = get_rows(returned, held_ref)
    layer = hidden + shared_ref[0]
    d_router = jnp.zeros((length, LANES), F32)
    for choice in range(2):
        place = jnp.where(flat[choice : choice + 1, :] == at_row, 1.0, 0.0).astype(BF16)
        picked = mm(place, came, TN)
        chosen = lane == routes_ref[0, :, choice : choice + 1]
        gate = jnp.sum(jnp.where(chosen, router, 0.0), axis=-1, keepdims=True)
        layer = layer + gate * picked
        d_gate = jnp.sum(grad * picked, axis=-1, keepdims=True)
        d_router = d_router + jnp.where(chosen, d_gate, 0.0)
    out_ref[0] = layer.astype(BF16)
    d_logits = (router * (d_router - jnp.sum(router * d_router, axis=-1, keepdims=True))).astype(BF16)
    sum_ref[:, 4 * width :] += mm(mixed, d_logits, TN)
    came = get_rows(d_back, held_ref)
    d_mixed = d_mixed_ref[0] + mm(place_of(flat, rows), came, TN) + mm(d_logits, weight_ref[:, 4 * width :], NT)

    inverse_two = inverse_rms(hidden)
    unit_two = hidden * inverse_two
    gains_ref[1:2, :] += jnp.sum(d_mixed * unit_two, axis=0, keepdims=True)
    scaled = d_mixed * gain_two_ref[...]
    d_hidden = grad + inverse_two * (scaled - unit_two * jnp.mean(scaled * unit_two, axis=-1, keepdims=True))
    d_branch = d_hidden.astype(BF16)
    sum_ref[:, 3 * width : 4 * width] += mm(attended_ref[0], d_branch, TN)
    d_attended = mm(d_branch, weight_ref[:, 3 * width : 4 * width], NT).astype(BF16)

    allowed = allowed_of(column_ref, row_ref)
    cosine, sine = cosine_ref[...], -sine_ref[...]
    low = iota((length, PAIR), 1) < HEAD_DIM
    logsum = logsum_ref[0]
    for pair in range(width // PAIR):
        at = slice(pair * PAIR, (pair + 1) * PAIR)
        query = qkv_ref[0, :, at]
        key = qkv_ref[0, :, width + at.start : width + at.stop]
        value = qkv_ref[0, :, 2 * width + at.start : 2 * width + at.stop]
        d_out = d_attended[:, at]
        parts = []
        for half in range(2):
            mine = low if half == 0 else jnp.logical_not(low)
            scores = jnp.where(allowed, mm(jnp.where(mine, query, BF16(0.0)), key, NT), -1e30)
            head = 2 * pair + half
            probs = jnp.exp(scores - logsum[:, head : head + 1])
            d_probs = mm(jnp.where(mine, d_out, BF16(0.0)), value, NT)
            d_scores = (probs * (d_probs - jnp.sum(probs * d_probs, axis=-1, keepdims=True))).astype(BF16)
            parts.append((mm(d_scores, key, NN), mm(d_scores, query, TN), mm(probs.astype(BF16), d_out, TN)))
        d_query, d_key, d_value = (jnp.where(low, a, b) for a, b in zip(*parts))
        d_qkv_ref[:, at] = turn(d_query * 0.125, cosine, sine).astype(BF16)
        d_qkv_ref[:, width + at.start : width + at.stop] = turn(d_key, cosine, sine).astype(BF16)
        d_qkv_ref[:, 2 * width + at.start : 2 * width + at.stop] = d_value.astype(BF16)

    x = tokens_ref[0].astype(F32)
    inverse_one = inverse_rms(x)
    unit_one = x * inverse_one
    normed = (unit_one * gain_one_ref[...]).astype(BF16)
    d_qkv = d_qkv_ref[...]
    sum_ref[:, : 3 * width] += mm(normed, d_qkv, TN)
    d_normed = mm(d_qkv, weight_ref[:, : 3 * width], NT)
    gains_ref[0:1, :] += jnp.sum(d_normed * unit_one, axis=0, keepdims=True)
    scaled = d_normed * gain_one_ref[...]
    grad_tokens_ref[0] = d_hidden + inverse_one * (
        scaled - unit_one * jnp.mean(scaled * unit_one, axis=-1, keepdims=True))

    @pl.when(step == pl.num_programs(0) - 1)
    def _():
        grad_weight_ref[:, : 4 * width] = sum_ref[:, : 4 * width].astype(BF16)
        gains = jnp.concatenate(
            [jnp.zeros((experts, width), F32), gains_ref[...], jnp.zeros((LANES - experts - 8, width), F32)], axis=0)
        grad_weight_ref[:, 4 * width :] = (sum_ref[:, 4 * width :] + gains.T).astype(BF16)


def feed_kernel(count, gated, *refs):
    rows_in, grads_in = refs[:count], refs[count : 2 * count]
    refs = refs[2 * count :]
    gates_in = refs[: count if gated else 0]
    refs = refs[len(gates_in) :]
    gate_ref, up_ref, down_ref = refs[:3]
    rows_out, grads_out = refs[3 : 3 + count], refs[3 + count : 3 + 2 * count]
    grad_in_ref, grad_down_ref, x_ref, d_ref, out_ref, dx_ref = refs[3 + 2 * count :]
    part = rows_in[0].shape[0]
    step = pl.program_id(1)

    @pl.when(step == 0)
    def _():
        out_ref[...] = jnp.zeros_like(out_ref)
        dx_ref[...] = jnp.zeros_like(dx_ref)
        for k in range(count):
            at = slice(k * part, (k + 1) * part)
            x_ref[at, :] = rows_in[k][...]
            grads = grads_in[k][...]
            if gated:
                square = (part, part)
                line = jnp.broadcast_to(gates_in[k][...], square)
                column = jnp.sum(jnp.where(iota(square, 0) == iota(square, 1), line, 0.0), axis=1, keepdims=True)
                grads = (grads.astype(F32) * column).astype(BF16)
            d_ref[at, :] = grads

    x, d = x_ref[...], d_ref[...]
    gate_weight, up_weight, down_weight = gate_ref[...], up_ref[...], down_ref[...]
    g = mm(x, gate_weight, NN)
    u = mm(x, up_weight, NN)
    sigma = 1.0 / (1.0 + jnp.exp(-g))
    active = g * sigma
    inner = (active * u).astype(BF16)
    out_ref[...] += mm(inner, down_weight, NN)
    d_inner = mm(d, down_weight, NT)
    d_g = (d_inner * u * (sigma * (1.0 + g * (1.0 - sigma)))).astype(BF16)
    d_u = (d_inner * active).astype(BF16)
    dx_ref[...] += mm(d_g, gate_weight, NT) + mm(d_u, up_weight, NT)
    grad_in_ref[0] = mm(x, d_g, TN).astype(BF16)
    grad_in_ref[1] = mm(x, d_u, TN).astype(BF16)
    grad_down_ref[...] = mm(inner, d, TN).astype(BF16)

    @pl.when(step == pl.num_programs(1) - 1)
    def _():
        for k in range(count):
            at = slice(k * part, (k + 1) * part)
            rows_out[k][...] = out_ref[at, :].astype(rows_out[k].dtype)
            grads_out[k][...] = dx_ref[at, :].astype(grads_out[k].dtype)


def feed(rows, grads, gates, both, down, block, out_dtype, name):
    count = len(rows)
    experts, part, width = rows[0].shape
    units = down.shape[1]
    squeezed = pl.Squeezed()
    piece = pl.BlockSpec((squeezed, part, width), lambda l, f: (l, 0, 0))
    gate = pl.BlockSpec((squeezed, 1, part), lambda l, f: (l, 0, 0))
    total = count * part
    outs = pl.pallas_call(
        functools.partial(feed_kernel, count, bool(gates)),
        grid=(experts, units // block),
        in_specs=[piece] * (2 * count)
        + [gate] * len(gates)
        + [
            pl.BlockSpec((squeezed, squeezed, width, block), lambda l, f: (l, 0, 0, f)),
            pl.BlockSpec((squeezed, squeezed, width, block), lambda l, f: (l, 1, 0, f)),
            pl.BlockSpec((squeezed, block, width), lambda l, f: (l, f, 0)),
        ],
        out_specs=[piece] * (2 * count)
        + [
            pl.BlockSpec((squeezed, 2, width, block), lambda l, f: (l, 0, 0, f)),
            pl.BlockSpec((squeezed, block, width), lambda l, f: (l, f, 0)),
        ],
        out_shape=[jax.ShapeDtypeStruct((experts, part, width), out_dtype)] * (2 * count)
        + [
            jax.ShapeDtypeStruct((experts, 2, width, units), BF16),
            jax.ShapeDtypeStruct((experts, units, width), BF16),
        ],
        scratch_shapes=[
            pltpu.VMEM((total, width), BF16),
            pltpu.VMEM((total, width), BF16),
            pltpu.VMEM((total, width), F32),
            pltpu.VMEM((total, width), F32),
        ],
        compiler_params=pltpu.CompilerParams(vmem_limit_bytes=VMEM_BYTES),
        cost_estimate=pl.CostEstimate(
            flops=18 * experts * total * width * units,
            bytes_accessed=experts * (12 * width * units + 8 * total * width),
            transcendentals=experts * total * units,
        ),
        name=name,
    )(*rows, *grads, *gates, both, both, down)
    return outs[:count], outs[count : 2 * count], outs[-2], outs[-1]


def on_device(
    tokens, cotangent, segments, routes, slots,
    norm1_gain, w_query, w_key, w_value, w_out, norm2_gain, w_router,
    shared_gate, shared_up, shared_down, expert_gate, expert_up, expert_down,
):
    length, width = tokens.shape[2], tokens.shape[3]
    batch = tokens.shape[0] * tokens.shape[1]
    devices = lax.axis_size("dp")
    owners = lax.axis_size("expert")
    local_experts = expert_gate.shape[0]
    experts = owners * local_experts
    hidden_units = shared_gate.shape[1]
    groups = 2
    group_size = local_experts // groups
    count = groups * owners
    own_owner = lax.axis_index("expert")

    pad = LANES - experts - 2
    first_part = jnp.concatenate(
        [w_query, w_key, w_value, w_out, w_router, norm1_gain[:, None], norm2_gain[:, None],
         jnp.zeros((w_query.shape[0], pad), BF16)], axis=1)
    first_all = gather_rows(first_part).reshape(width, -1)
    shared_both = jnp.stack(
        [gather_rows(shared_gate).reshape(width, -1), gather_rows(shared_up).reshape(width, -1)])[None]
    shared_dn = gather_rows(shared_down).reshape(1, hidden_units, width)
    pool_in, pool_dn = [], []
    for h in range(groups):
        part = slice(h * group_size, (h + 1) * group_size)
        both = jnp.stack([expert_gate[part], expert_up[part]], axis=1)
        pool_in.append(lax.all_gather(both, "dp", axis=2, tiled=True))
        pool_dn.append(lax.all_gather(expert_down[part], "dp", axis=1, tiled=True))
    gains = first_all[:, 4 * width + experts : 4 * width + experts + 2].astype(F32).T
    gain_one, gain_two = gains[0:1], gains[1:2]

    route_ids = routes.reshape(batch, length, 2)
    owner_of = (route_ids // local_experts) ^ own_owner
    local = route_ids % local_experts
    flat = ((local // group_size * owners + owner_of) * group_size + local % group_size) * CAP
    flat = (flat + slots.reshape(batch, length, 2)).transpose(0, 2, 1)

    def trade(field, k):
        if k == 0:
            return field
        return lax.ppermute(field, "expert", [(i, i ^ k) for i in range(owners)])

    def trade_all(pieces):
        return [trade(piece, n % owners) for n, piece in enumerate(pieces)]

    def lined(pieces):
        return [piece.reshape(group_size, batch * CAP, width) for piece in pieces]

    whole = lambda shape: pl.BlockSpec(shape, lambda b: (0,) * len(shape))
    each = lambda *shape: pl.BlockSpec((1,) + shape, lambda b: (b, 0, 0))
    piece_spec = pl.BlockSpec((group_size, 1, CAP, width), lambda b: (0, b, 0, 0))
    piece_shape = jax.ShapeDtypeStruct((group_size, batch, CAP, width), BF16)
    rows = experts * CAP
    params = pltpu.CompilerParams(vmem_limit_bytes=VMEM_BYTES)

    grad_low = cotangent.reshape(batch, length, width)
    grad_sent = pl.pallas_call(
        dispatch_kernel,
        grid=(batch,),
        in_specs=[each(2, length), each(length, width)],
        out_specs=[piece_spec] * count,
        out_shape=[piece_shape] * count,
        compiler_params=params,
        cost_estimate=pl.CostEstimate(
            flops=2 * batch * rows * length * width, bytes_accessed=4 * batch * rows * width, transcendentals=0),
        name="dispatch",
    )(flat, grad_low)
    grad_arrived = trade_all(grad_sent)

    token_rows = tokens.reshape(batch, length, width)
    segment_ids = segments.reshape(batch, length)
    half = HEAD_DIM // 2
    frequency = jnp.exp(-jnp.log(10000.0) * jnp.arange(half, dtype=F32) / half)
    angles = jnp.arange(length, dtype=F32)[:, None] * frequency[None, :]
    cosine = jnp.tile(jnp.cos(angles), (1, 4))
    sine = jnp.tile(jnp.concatenate([-jnp.sin(angles), jnp.sin(angles)], axis=1), (1, 2))
    columns = first_all.shape[1]
    position_args = (segment_ids[:, :, None], segment_ids[:, None, :], flat)
    position_specs = [each(length, 1), each(1, length), each(2, length)]
    weight_args = (first_all, gain_one, gain_two, cosine, sine)
    weight_specs = [
        whole((width, columns)), whole((1, width)), whole((1, width)), whole((length, LANES)), whole((length, LANES))]
    kept_shapes = [
        jax.ShapeDtypeStruct((batch, length, width), F32),
        jax.ShapeDtypeStruct((batch, length, width), BF16),
        jax.ShapeDtypeStruct((batch, length, width), BF16),
        jax.ShapeDtypeStruct((batch, length, 3 * width), BF16),
        jax.ShapeDtypeStruct((batch, length, LANES), F32),
        jax.ShapeDtypeStruct((batch, length, LANES), F32),
    ]
    kept_specs = [each(*shape.shape[1:]) for shape in kept_shapes]
    tokens_all = batch * length
    outs = pl.pallas_call(
        functools.partial(forward_kernel, experts),
        grid=(batch,),
        in_specs=[each(length, width)] + position_specs + weight_specs,
        out_specs=kept_specs + [piece_spec] * count,
        out_shape=kept_shapes + [piece_shape] * count,
        compiler_params=params,
        cost_estimate=pl.CostEstimate(
            flops=2 * tokens_all * width * (columns + 4 * length + rows),
            bytes_accessed=2 * width * columns + tokens_all * width * 20,
            transcendentals=tokens_all * length * width // HEAD_DIM,
        ),
        name="attention",
    )(token_rows, *position_args, *weight_args)
    kept, sent = outs[:6], outs[6:]
    mixed_in, router = kept[1], kept[5]
    arrived = trade_all(sent)
    chosen = route_ids[..., None] == jnp.arange(experts, dtype=jnp.int32)
    gates = jnp.sum(jnp.where(chosen, router[:, :, None, :experts], 0.0), axis=-1).transpose(0, 2, 1)
    held = flat[:, :, None, :] == jnp.arange(rows, dtype=jnp.int32)[:, None]
    slot_gates = jnp.sum(jnp.where(held, gates[:, :, None, :], 0.0), axis=(1, 3))
    slot_gates = slot_gates.reshape(batch, groups, owners, group_size, CAP).transpose(2, 1, 3, 0, 4)
    slot_gates = slot_gates.reshape(owners, groups, group_size, 1, batch * CAP)
    slot_gates = [trade(slot_gates[k], k) for k in range(owners)]

    shared_out, d_mixed, grad_shared_both, grad_shared_dn = feed(
        [mixed_in.reshape(1, tokens_all, width)], [grad_low.reshape(1, tokens_all, width)], [],
        shared_both, shared_dn, 512, F32, "shared")

    returned, d_back, pool_in_mine, pool_dn_mine = [], [], [], []
    for h in range(groups):
        part = slice(h * owners, (h + 1) * owners)
        results, d_send, grad_both, grad_dn = feed(
            lined(arrived[part]), lined(grad_arrived[part]), [gate[h] for gate in slot_gates],
            pool_in[h], pool_dn[h], 512, BF16, "experts")
        returned += trade_all(results)
        d_back += trade_all(d_send)
        pool_dn_mine.append(lax.psum_scatter(grad_dn, "dp", scatter_dimension=1, tiled=True))
        pool_in_mine.append(lax.psum_scatter(grad_both, "dp", scatter_dimension=2, tiled=True))
    unlined = lambda pieces: [piece.reshape(piece_shape.shape) for piece in pieces]
    pool_dn_mine = jnp.concatenate(pool_dn_mine, axis=0).astype(F32)
    pool_in_mine = jnp.concatenate(pool_in_mine, axis=0).astype(F32)

    layer_out, grad_tokens, first_grad = pl.pallas_call(
        functools.partial(backward_kernel, experts, count),
        grid=(batch,),
        in_specs=[each(length, width)] * 2 + position_specs + [each(length, 2)] + weight_specs + kept_specs
        + [each(length, width)] * 2 + [piece_spec] * (2 * count),
        out_specs=[each(length, width)] * 2 + [whole((width, columns))],
        out_shape=[
            jax.ShapeDtypeStruct((batch, length, width), BF16),
            jax.ShapeDtypeStruct((batch, length, width), F32),
            jax.ShapeDtypeStruct((width, columns), BF16),
        ],
        scratch_shapes=[
            pltpu.VMEM((rows, width), F32),
            pltpu.VMEM((width, columns), F32),
            pltpu.VMEM((8, width), F32),
            pltpu.VMEM((length, 3 * width), BF16),
        ],
        compiler_params=params,
        cost_estimate=pl.CostEstimate(
            flops=4 * tokens_all * width * (columns + 4 * length + rows),
            bytes_accessed=4 * width * columns + tokens_all * width * 32,
            transcendentals=tokens_all * length * width // HEAD_DIM,
        ),
        name="attention_back",
    )(
        token_rows, grad_low, *position_args, route_ids, *weight_args, *kept,
        shared_out[0].reshape(batch, length, width), d_mixed[0].reshape(batch, length, width),
        *unlined(returned), *unlined(d_back),
    )

    def finish(field):
        mine = scatter_rows(field.reshape((devices, field.shape[0] // devices) + field.shape[1:]))
        total = mine.astype(F32)
        for k in range(1, owners):
            total = total + trade(mine, k).astype(F32)
        return total

    shared_dn_mine = finish(grad_shared_dn[0])
    shared_gate_mine = finish(grad_shared_both[0, 0])
    shared_up_mine = finish(grad_shared_both[0, 1])
    first_mine = finish(first_grad)
    return (
        layer_out.reshape(tokens.shape),
        grad_tokens.reshape(tokens.shape),
        first_mine[:, 4 * width + experts],
        first_mine[:, :width],
        first_mine[:, width : 2 * width],
        first_mine[:, 2 * width : 3 * width],
        first_mine[:, 3 * width : 4 * width],
        first_mine[:, 4 * width + experts + 1],
        first_mine[:, 4 * width : 4 * width + experts],
        shared_gate_mine,
        shared_up_mine,
        shared_dn_mine,
        pool_in_mine[:, 0],
        pool_in_mine[:, 1],
        pool_dn_mine,
    )


def solution(mesh):
    token_spec = P(None, ("dp", "expert"), None, None)
    vector, matrix, pool = P("dp"), P("dp", None), P("expert", "dp", None)
    weights = (vector, matrix, matrix, matrix, matrix, vector, matrix, matrix, matrix, matrix, pool, pool, pool)
    return jax.shard_map(
        on_device,
        mesh=mesh,
        in_specs=(token_spec, token_spec, P(None, ("dp", "expert"), None), token_spec, token_spec) + weights,
        out_specs=(token_spec, token_spec) + weights,
        check_vma=False,
    )
```

time: 1600 us -> 953 us (0.60)
  matrix products: 631 us -> 0 us
  Pallas kernels: 0 us -> 242 us
  local copies, waits for them, and re-layouts: 209 us -> 41.6 us
  starting transfers between devices: 72 us -> 198 us
  waiting for transfers between devices: 487 us -> 401 us
  other arithmetic: 121 us -> 35.6 us
  blocking collectives: 51.5 us -> 0 us
    dot_general x156 -> x0, matrix products: 631 us -> none  [the longest x4 71.3 us: on_device(): jnp.einsum('slcf,slcd->lfd', pool_inner, d_result, preferred_element_type...]
    ppermute x0 -> x79, waiting for transfers between devices: none -> 399 us  [the longest x39 299 us: trade(): return lax.ppermute(field, 'expert', [(i, i ^ k) for i in range(owners)])]
    pallas_call x0 -> x10, Pallas kernels: none -> 242 us  [the longest x3 137 us: feed(): pl.pallas_call(functools.partial(feed_kernel, count, bool(gates)), grid=(...]
    reduce_scatter x10 -> x4, waiting for transfers between devices: 231 us -> 0.01 us  [the longest x2 0.01 us: on_device(): lax.psum_scatter(grad_dn, 'dp', scatter_dimension=1, tiled=True)]
    all_gather x10 -> x4, waiting for transfers between devices: 191 us -> 0.05 us  [the longest x2 0.03 us: on_device(): pool_in.append(lax.all_gather(both, 'dp', axis=2, tiled=True))]
    ppermute x0 -> x79, starting transfers between devices: none -> 188 us  [the longest x39 161 us: trade(): return lax.ppermute(field, 'expert', [(i, i ^ k) for i in range(owners)])]
    all_to_all x16 -> x0, starting transfers between devices: 70 us -> none  [the longest x4 19.4 us: on_device(): lax.all_to_all(send_rows, 'expert', split_axis=0, concat_axis=0, tiled=True)]
    gather x28 -> x0, local copies, waits for them, and re-layouts: 66.4 us -> none  [the longest x12 21 us: on_device(): gate_values = jnp.take_along_axis(router, route_ids, axis=1)]
  transfers between devices with their start and end apart: 38 -> 87, of which waited for: 23 -> 30; matrix products, arithmetic and copies ran while one was open for 53% -> 6% of each run, Pallas kernels for 0% -> 26%
where the time goes in v1:
time: 953 us; the launch traced here: 934 us
  waiting for transfers between devices  401 us (42%)
  Pallas kernels  242 us (25%)
  starting transfers between devices  198 us (21%)
  local copies, waits for them, and re-layouts  41.6 us (4%)
  other arithmetic  35.6 us (4%)
  between operations  15.8 us (2%)
    ppermute x39, waiting for transfers between devices, trade(): return lax.ppermute(field, 'expert', [(i, i ^ k) for i in range(owners)])  299 us
    ppermute x39, starting transfers between devices, trade(): return lax.ppermute(field, 'expert', [(i, i ^ k) for i in range(owners)])  161 us
    pallas_call x3, Pallas kernels, feed(): pl.pallas_call(functools.partial(feed_kernel, count, bool(gates)), grid=(...  137 us
    ppermute x40, waiting for transfers between devices, send(): return lax.ppermute(field, 'dp', [(i, step(i)) for i in range(8)])  100 us
    pallas_call x1, Pallas kernels, on_device(): pl.pallas_call(functools.partial(backward_kernel, experts, count), grid=(...  52.7 us
    pallas_call x1, Pallas kernels, on_device(): pl.pallas_call(functools.partial(forward_kernel, experts), grid=(batch,),...  31.6 us
    ppermute x40, starting transfers between devices, send(): return lax.ppermute(field, 'dp', [(i, step(i)) for i in range(8)])  26.8 us
  transfers between devices with their start and end apart: 87, of which 30 were waited for; matrix products, arithmetic and copies ran while one was open for 6% of the time, Pallas kernels for 26%

profile of v1, /device:TPU:0, one launch (start us, length us, event | category | flops | bytes accessed | tf_op | source)
XLA Modules:
  0.0 934.1 jit_solution(16287665202049888345)
XLA Ops:
  21.1 21.0 %collective-permute-done.refs_1_ = bf16[96,3200]{1,0:T(8,128)(2,1)S(1)} collective-permute-done((bf16[96,3200]{1,0:T(8,128)(2,1)S(1)}, bf16[96,3200]{1,0:T(8,128)(2,1)S(1)}, u32[]{:S(2)}, u32[]{:S(2)}) %collective-permute-start) | collective-permute-done | bytes 614432 | tf_op jit(solution)/shard_map/ppermute | solution.py:46
  77.2 31.6 %attention.1 = (f32[4,256,768]{2,1,0:T(8,128)}, bf16[4,256,768]{2,1,0:T(8,128)(2,1)}, bf16[4,256,768]{2,1,0:T(8,128)(2,1)}, bf16[4,256,2304]{2,1,0:T(8,128)(2,1)...) custom-call(bf16[4,256,768]{2,1,0:T(8,128)(2,1)} %bitcast.173, ...), custom_call_target="tpu_custom_call" | custom-call | flops 7650410496 | bytes 20643840 | tf_op jit(solution)/shard_map/attention/pallas_call | solution.py:487
  132.3 9.8 %collective-permute-done.40 = bf16[2,4,40,768]{3,2,1,0:T(8,128)(2,1)S(1)} collective-permute-done((bf16[2,4,40,768]{3,2,1,0:T(8,128)(2,1)}, bf16[2,4,40,768]{3,2,1,0:T(8,128)(2,1)S(1)}, u32[]{:S(2)}, u32[]{:S(2)}) %collective-permute-start.40) | collective-permute-done | bytes 491552 | tf_op jit(solution)/shard_map/ppermute | solution.py:435
  142.1 30.8 %collective-permute-done.41 = bf16[2,4,40,768]{3,2,1,0:T(8,128)(2,1)S(1)} collective-permute-done((bf16[2,4,40,768]{3,2,1,0:T(8,128)(2,1)}, bf16[2,4,40,768]{3,2,1,0:T(8,128)(2,1)S(1)}, u32[]{:S(2)}, u32[]{:S(2)}) %collective-permute-start.41) | collective-permute-done | bytes 491552 | tf_op jit(solution)/shard_map/ppermute | solution.py:435
  173.9 49.1 %experts.3 = (bf16[2,160,768]{2,1,0:T(8,128)(2,1)}, bf16[2,160,768]{2,1,0:T(8,128)(2,1)}, bf16[2,160,768]{2,1,0:T(8,128)(2,1)}, bf16[2,160,768]{2,1,0:T(8,128)(2...) custom-call(bf16[2,160,768]{2,1,0:T(8,128)(2,1)} %bitcast.209, ...), custom_call_target="tpu_custom_call" | custom-call | flops 36238786560 | bytes 45613056 | tf_op jit(solution)/shard_map/experts/pallas_call | solution.py:355
  224.0 9.3 collective-permute-start.31
  237.8 17.3 %collective-permute-done.31 = bf16[2,4,40,768]{3,2,1,0:T(8,128)(2,1)S(1)} collective-permute-done((bf16[2,4,40,768]{3,2,1,0:T(8,128)(2,1)S(1)}, bf16[2,4,40,768]{3,2,1,0:T(8,128)(2,1)S(1)}, u32[]{:S(2)}, u32[]{:S(2)}) %collective-permute-start.31) | collective-permute-done | bytes 491552 | tf_op jit(solution)/shard_map/ppermute | solution.py:435
  257.3 12.2 %collective-permute-done.32 = bf16[2,4,40,768]{3,2,1,0:T(8,128)(2,1)} collective-permute-done((bf16[2,4,40,768]{3,2,1,0:T(8,128)(2,1)S(1)}, bf16[2,4,40,768]{3,2,1,0:T(8,128)(2,1)}, u32[]{:S(2)}, u32[]{:S(2)}) %collective-permute-start.32) | collective-permute-done | bytes 491552 | tf_op jit(solution)/shard_map/ppermute | solution.py:435
  276.6 35.0 %collective-permute-done.29 = bf16[2,4,40,768]{3,2,1,0:T(8,128)(2,1)} collective-permute-done((bf16[2,4,40,768]{3,2,1,0:T(8,128)(2,1)S(1)}, bf16[2,4,40,768]{3,2,1,0:T(8,128)(2,1)}, u32[]{:S(2)}, u32[]{:S(2)}) %collective-permute-start.29) | collective-permute-done | bytes 491552 | tf_op jit(solution)/shard_map/ppermute | solution.py:435
  312.5 48.7 %experts.2 = (bf16[2,160,768]{2,1,0:T(8,128)(2,1)}, bf16[2,160,768]{2,1,0:T(8,128)(2,1)}, bf16[2,160,768]{2,1,0:T(8,128)(2,1)}, bf16[2,160,768]{2,1,0:T(8,128)(2...) custom-call(bf16[2,160,768]{2,1,0:T(8,128)(2,1)} %bitcast.208, ...), custom_call_target="tpu_custom_call" | custom-call | flops 36238786560 | bytes 45613056 | tf_op jit(solution)/shard_map/experts/pallas_call | solution.py:355
  362.0 9.8 %reduce-scatter.5.cloned.1.call-start = ((), (), s32[]{:S(2)}) async-start(), calls=%async_computation.8 | async-start | bytes 14155776 | tf_op jit(solution)/shard_map/reduce_scatter | solution.py:525
  394.5 10.7 %collective-permute-done.21.refs_1_ = bf16[256,768]{1,0:T(8,128)(2,1)S(1)} collective-permute-done((bf16[256,768]{1,0:T(8,128)(2,1)S(1)}, bf16[256,768]{1,0:T(8,128)(2,1)S(1)}, u32[]{:S(2)}, u32[]{:S(2)}) %collective-permute-start.21) | collective-permute-done | bytes 393248 | tf_op jit(solution)/shard_map/ppermute | solution.py:46
  407.1 12.1 %collective-permute-done.9.refs_3_ = bf16[96,2048]{1,0:T(8,128)(2,1)S(1)} collective-permute-done((bf16[96,2048]{1,0:T(8,128)(2,1)S(1)}, bf16[96,2048]{1,0:T(8,128)(2,1)S(1)}, u32[]{:S(2)}, u32[]{:S(2)}) %collective-permute-start.9) | collective-permute-done | bytes 393248 | tf_op jit(solution)/shard_map/ppermute | solution.py:46
  445.0 39.0 %shared.1 = (f32[1,1024,768]{2,1,0:T(8,128)}, f32[1,1024,768]{2,1,0:T(8,128)}, bf16[1,2,768,2048]{3,2,1,0:T(8,128)(2,1)}, bf16[1,2048,768]{2,1,0:T(8,128)(2,1)}) custom-call(bf16[1,1024,768]{2,1,0:T(8,128)(2,1)} %bitcast.200, bf16[1,1024,768]{2,1,0:T(8,128)(2,1)} %bitcast.176, bf16[1,2,768,2048]{3,2,1,0:T(8,128)(2,1)} %maximum_bitcast_fusion.refs_2_.refs_3_, ...), custom_call_target="tpu_custom_call" | custom-call | flops 28991029248 | bytes 25165824 | tf_op jit(solution)/shard_map/shared/pallas_call | solution.py:355
  486.8 12.9 %collective-permute-start.46 = (bf16[2,160,768]{2,1,0:T(8,128)(2,1)S(1)}, bf16[2,160,768]{2,1,0:T(8,128)(2,1)S(1)}, u32[]{:S(2)}, u32[]{:S(2)}) collective-permute-start(bf16[2,160,768]{2,1,0:T(8,128)(2,1)S(1)} %copy-done.51), channel_id=1, source_target_pairs={{0,1},{1,0},{2,3},{3,2},{4,5},{5,4},{6,7},{7,6},{8,9},{9,8},{10,11... | collective-permute-start | bytes 1474568 | tf_op jit(solution)/shard_map/ppermute | solution.py:435
  508.2 10.9 %collective-permute-done.46 = bf16[2,160,768]{2,1,0:T(8,128)(2,1)S(1)} collective-permute-done((bf16[2,160,768]{2,1,0:T(8,128)(2,1)S(1)}, bf16[2,160,768]{2,1,0:T(8,128)(2,1)S(1)}, u32[]{:S(2)}, u32[]{:S(2)}) %collective-permute-start.46) | collective-permute-done | bytes 491552 | tf_op jit(solution)/shard_map/ppermute | solution.py:435
  521.5 14.4 %collective-permute-done.47 = bf16[2,160,768]{2,1,0:T(8,128)(2,1)S(1)} collective-permute-done((bf16[2,160,768]{2,1,0:T(8,128)(2,1)S(1)}, bf16[2,160,768]{2,1,0:T(8,128)(2,1)S(1)}, u32[]{:S(2)}, u32[]{:S(2)}) %collective-permute-start.47) | collective-permute-done | bytes 491552 | tf_op jit(solution)/shard_map/ppermute | solution.py:435
  538.5 28.5 %collective-permute-start.38 = (bf16[2,160,768]{2,1,0:T(8,128)(2,1)S(1)}, bf16[2,160,768]{2,1,0:T(8,128)(2,1)S(1)}, u32[]{:S(2)}, u32[]{:S(2)}) collective-permute-start(bf16[2,160,768]{2,1,0:T(8,128)(2,1)S(1)} %copy-done.56), channel_id=1, source_target_pairs={{0,2},{1,3},{2,0},{3,1},{4,6},{5,7},{6,4},{7,5},{8,10},{9,11},{10,... | collective-permute-start | bytes 1474568 | tf_op jit(solution)/shard_map/ppermute | solution.py:435
  570.4 28.6 %collective-permute-done.53 = bf16[2,160,768]{2,1,0:T(8,128)(2,1)S(1)} collective-permute-done((bf16[2,160,768]{2,1,0:T(8,128)(2,1)S(1)}, bf16[2,160,768]{2,1,0:T(8,128)(2,1)S(1)}, u32[]{:S(2)}, u32[]{:S(2)}) %collective-permute-start.53) | collective-permute-done | bytes 491552 | tf_op jit(solution)/shard_map/ppermute | solution.py:435
  599.1 10.0 %collective-permute-start.50 = (bf16[2,160,768]{2,1,0:T(8,128)(2,1)S(1)}, bf16[2,160,768]{2,1,0:T(8,128)(2,1)S(1)}, u32[]{:S(2)}, u32[]{:S(2)}) collective-permute-start(bf16[2,160,768]{2,1,0:T(8,128)(2,1)S(1)} %copy-done.53), channel_id=1, source_target_pairs={{0,2},{1,3},{2,0},{3,1},{4,6},{5,7},{6,4},{7,5},{8,10},{9,11},{10,... | collective-permute-start | bytes 1474568 | tf_op jit(solution)/shard_map/ppermute | solution.py:435
  615.7 25.6 %collective-permute-done.38 = bf16[2,160,768]{2,1,0:T(8,128)(2,1)S(1)} collective-permute-done((bf16[2,160,768]{2,1,0:T(8,128)(2,1)S(1)}, bf16[2,160,768]{2,1,0:T(8,128)(2,1)S(1)}, u32[]{:S(2)}, u32[]{:S(2)}) %collective-permute-start.38) | collective-permute-done | bytes 491552 | tf_op jit(solution)/shard_map/ppermute | solution.py:435
  644.2 18.1 %collective-permute-done.50 = bf16[2,160,768]{2,1,0:T(8,128)(2,1)S(1)} collective-permute-done((bf16[2,160,768]{2,1,0:T(8,128)(2,1)S(1)}, bf16[2,160,768]{2,1,0:T(8,128)(2,1)S(1)}, u32[]{:S(2)}, u32[]{:S(2)}) %collective-permute-start.50) | collective-permute-done | bytes 491552 | tf_op jit(solution)/shard_map/ppermute | solution.py:435
  663.2 52.7 %attention_back.1 = (bf16[4,256,768]{2,1,0:T(8,128)(2,1)}, f32[4,256,768]{2,1,0:T(8,128)}, bf16[768,3200]{1,0:T(8,128)(2,1)}) custom-call(bf16[4,256,768]{2,1,0:T(8,128)(2,1)} %bitcast.174, bf16[4,256,768]{2,1,0:T(8,128)(2,1)} %bitcast.177, s32[4,256,1]{2,1,0:T(8,128)} %broadcast_in_dim_reshape.5.column_ref, s32[4,1,256]{2,1,0:T(1,128)} %row_ref.3, ...), custom_call_target="tpu_custom_call" | custom-call | flops 15300820992 | bytes 34996224 | tf_op jit(solution)/shard_map/attention_back/pallas_call | solution.py:530
  740.6 11.9 %collective-permute-done.62 = bf16[2,96,2048]{2,1,0:T(8,128)(2,1)} collective-permute-done((bf16[2,96,2048]{2,1,0:T(8,128)(2,1)S(1)}, bf16[2,96,2048]{2,1,0:T(8,128)(2,1)}, u32[]{:S(2)}, u32[]{:S(2)}) %collective-permute-start.62) | collective-permute-done | bytes 786464 | tf_op jit(solution)/shard_map/ppermute | solution.py:46
  760.1 10.2 %collective-permute-start.70 = (bf16[96,2048]{1,0:T(8,128)(2,1)S(1)}, bf16[96,2048]{1,0:T(8,128)(2,1)S(1)}, u32[]{:S(2)}, u32[]{:S(2)}) collective-permute-start(bf16[96,2048]{1,0:T(8,128)(2,1)S(1)} %fusion.14), channel_id=1, source_target_pairs={{0,1},{1,0},{2,3},{3,2},{4,5},{5,4},{6,7},{7,6},{8,9},{9,8},{10,11... | collective-permute-start | bytes 1179656 | tf_op jit(solution)/shard_map/ppermute | solution.py:435
  778.0 10.2 %collective-permute-start.76 = (bf16[256,768]{1,0:T(8,128)(2,1)S(1)}, bf16[256,768]{1,0:T(8,128)(2,1)S(1)}, u32[]{:S(2)}, u32[]{:S(2)}) collective-permute-start(bf16[256,768]{1,0:T(8,128)(2,1)S(1)} %fusion.13), channel_id=1, source_target_pairs={{0,1},{1,0},{2,3},{3,2},{4,5},{5,4},{6,7},{7,6},{8,9},{9,8},{10,11... | collective-permute-start | bytes 1179656 | tf_op jit(solution)/shard_map/ppermute | solution.py:435
  789.5 10.6 %collective-permute-done.71 = bf16[96,2048]{1,0:T(8,128)(2,1)S(1)} collective-permute-done((bf16[96,2048]{1,0:T(8,128)(2,1)S(1)}, bf16[96,2048]{1,0:T(8,128)(2,1)S(1)}, u32[]{:S(2)}, u32[]{:S(2)}) %collective-permute-start.71) | collective-permute-done | bytes 393248 | tf_op jit(solution)/shard_map/ppermute | solution.py:435
  800.1 25.8 %collective-permute-start.64 = (bf16[96,2048]{1,0:T(8,128)(2,1)S(1)}, bf16[96,2048]{1,0:T(8,128)(2,1)S(1)}, u32[]{:S(2)}, u32[]{:S(2)}) collective-permute-start(bf16[96,2048]{1,0:T(8,128)(2,1)S(1)} %fusion.15), channel_id=1, source_target_pairs={{0,1},{1,0},{2,3},{3,2},{4,5},{5,4},{6,7},{7,6},{8,9},{9,8},{10,11... | collective-permute-start | bytes 1179656 | tf_op jit(solution)/shard_map/ppermute | solution.py:435
  829.6 18.6 %collective-permute-done.77 = bf16[256,768]{1,0:T(8,128)(2,1)S(1)} collective-permute-done((bf16[256,768]{1,0:T(8,128)(2,1)S(1)}, bf16[256,768]{1,0:T(8,128)(2,1)S(1)}, u32[]{:S(2)}, u32[]{:S(2)}) %collective-permute-start.77) | collective-permute-done | bytes 393248 | tf_op jit(solution)/shard_map/ppermute | solution.py:435
  848.2 10.5 %collective-permute-start.59 = (bf16[96,3200]{1,0:T(8,128)(2,1)S(1)}, bf16[96,3200]{1,0:T(8,128)(2,1)S(1)}, u32[]{:S(2)}, u32[]{:S(2)}) collective-permute-start(bf16[96,3200]{1,0:T(8,128)(2,1)S(1)} %fusion.6), channel_id=1, source_target_pairs={{0,2},{1,3},{2,0},{3,1},{4,6},{5,7},{6,4},{7,5},{8,10},{9,11},{10,... | collective-permute-start | bytes 1843208 | tf_op jit(solution)/shard_map/ppermute | solution.py:435
  863.1 30.8 %collective-permute-done.65 = bf16[96,2048]{1,0:T(8,128)(2,1)S(1)} collective-permute-done((bf16[96,2048]{1,0:T(8,128)(2,1)S(1)}, bf16[96,2048]{1,0:T(8,128)(2,1)S(1)}, u32[]{:S(2)}, u32[]{:S(2)}) %collective-permute-start.65) | collective-permute-done | bytes 393248 | tf_op jit(solution)/shard_map/ppermute | solution.py:435
  895.0 20.5 %collective-permute-done.59 = bf16[96,3200]{1,0:T(8,128)(2,1)S(1)} collective-permute-done((bf16[96,3200]{1,0:T(8,128)(2,1)S(1)}, bf16[96,3200]{1,0:T(8,128)(2,1)S(1)}, u32[]{:S(2)}, u32[]{:S(2)}) %collective-permute-start.59) | collective-permute-done | bytes 614432 | tf_op jit(solution)/shard_map/ppermute | solution.py:435
  (416 shorter events, 231.0 us)
Async XLA Ops:
  7.2 165.7 %all-gather.11.cloned.1.call-start = ((), (), s32[]{:S(2)}) async-start(), calls=%async_computation.7 | async-start | bytes 7077888 | tf_op jit(solution)/shard_map/all_gather | solution.py:422
  10.0 163.0 %all-gather.9.cloned.1.call-start = ((), (), s32[]{:S(2)}) async-start(), calls=%async_computation.6 | async-start | bytes 14155776 | tf_op jit(solution)/shard_map/all_gather | solution.py:421
  13.0 298.7 %all-gather.7.cloned.1.call-start = ((), (), s32[]{:S(2)}) async-start(), calls=%async_computation.5 | async-start | bytes 7077888 | tf_op jit(solution)/shard_map/all_gather | solution.py:422
  13.8 297.9 %all-gather.5.cloned.1.call-start = ((), (), s32[]{:S(2)}) async-start(), calls=%async_computation.4 | async-start | bytes 14155776 | tf_op jit(solution)/shard_map/all_gather | solution.py:421
  15.2 903.0 %reduce-scatter.11.cloned.1.call-start = ((), (), s32[]{:S(2)}) async-start(), calls=%async_computation.11 | async-start | bytes 7077888 | tf_op jit(solution)/shard_map/reduce_scatter | solution.py:524
  51.1 65.3 %collective-permute-start.43 = (bf16[2,4,40,768]{3,2,1,0:T(8,128)(2,1)}, bf16[2,4,40,768]{3,2,1,0:T(8,128)(2,1)}, u32[]{:S(2)}, u32[]{:S(2)}) collective-permute-start(bf16[2,4,40,768]{3,2,1,0:T(8,128)(2,1)} %get-tuple-element.89), channel_id=1, source_target_pairs={{0,1},{1,0},{2,3},{3,2},{4,5},{5,4},{6,7},{7,6},{8,9},{9,8},{10,11... | collective-permute-start | bytes 1474568 | tf_op jit(solution)/shard_map/ppermute | solution.py:435
  65.1 58.5 %collective-permute-start.44 = (bf16[2,4,40,768]{3,2,1,0:T(8,128)(2,1)}, bf16[2,4,40,768]{3,2,1,0:T(8,128)(2,1)S(1)}, u32[]{:S(2)}, u32[]{:S(2)}) collective-permute-start(bf16[2,4,40,768]{3,2,1,0:T(8,128)(2,1)} %get-tuple-element.90), channel_id=1, source_target_pairs={{0,2},{1,3},{2,0},{3,1},{4,6},{5,7},{6,4},{7,5},{8,10},{9,11},{10,... | collective-permute-start | bytes 1474568 | tf_op jit(solution)/shard_map/ppermute | solution.py:435
  117.4 55.4 %collective-permute-start.41 = (bf16[2,4,40,768]{3,2,1,0:T(8,128)(2,1)}, bf16[2,4,40,768]{3,2,1,0:T(8,128)(2,1)S(1)}, u32[]{:S(2)}, u32[]{:S(2)}) collective-permute-start(bf16[2,4,40,768]{3,2,1,0:T(8,128)(2,1)} %get-tuple-element.86), channel_id=1, source_target_pairs={{0,2},{1,3},{2,0},{3,1},{4,6},{5,7},{6,4},{7,5},{8,10},{9,11},{10,... | collective-permute-start | bytes 1474568 | tf_op jit(solution)/shard_map/ppermute | solution.py:435
  120.8 52.1 %collective-permute-start.42 = (bf16[2,4,40,768]{3,2,1,0:T(8,128)(2,1)}, bf16[2,4,40,768]{3,2,1,0:T(8,128)(2,1)S(1)}, u32[]{:S(2)}, u32[]{:S(2)}) collective-permute-start(bf16[2,4,40,768]{3,2,1,0:T(8,128)(2,1)} %get-tuple-element.87), channel_id=1, source_target_pairs={{0,3},{1,2},{2,1},{3,0},{4,7},{5,6},{6,5},{7,4},{8,11},{9,10},{10,... | collective-permute-start | bytes 1474568 | tf_op jit(solution)/shard_map/ppermute | solution.py:435
  223.1 695.1 %reduce-scatter.9.cloned.1.call-start = ((), (), s32[]{:S(2)}) async-start(), calls=%async_computation.10 | async-start | bytes 7077888 | tf_op jit(solution)/shard_map/reduce_scatter | solution.py:524
  236.8 74.8 %collective-permute-start.29 = (bf16[2,4,40,768]{3,2,1,0:T(8,128)(2,1)S(1)}, bf16[2,4,40,768]{3,2,1,0:T(8,128)(2,1)}, u32[]{:S(2)}, u32[]{:S(2)}) collective-permute-start(bf16[2,4,40,768]{3,2,1,0:T(8,128)(2,1)S(1)} %copy-done.63), channel_id=1, source_target_pairs={{0,2},{1,3},{2,0},{3,1},{4,6},{5,7},{6,4},{7,5},{8,10},{9,11},{10,... | collective-permute-start | bytes 1474568 | tf_op jit(solution)/shard_map/ppermute | solution.py:435
  255.1 56.6 %collective-permute-start.30 = (bf16[2,4,40,768]{3,2,1,0:T(8,128)(2,1)S(1)}, bf16[2,4,40,768]{3,2,1,0:T(8,128)(2,1)S(1)}, u32[]{:S(2)}, u32[]{:S(2)}) collective-permute-start(bf16[2,4,40,768]{3,2,1,0:T(8,128)(2,1)S(1)} %copy-done.62), channel_id=1, source_target_pairs={{0,3},{1,2},{2,1},{3,0},{4,7},{5,6},{6,5},{7,4},{8,11},{9,10},{10,... | collective-permute-start | bytes 1474568 | tf_op jit(solution)/shard_map/ppermute | solution.py:435
  361.2 560.2 %reduce-scatter.7.cloned.1.call-start = ((), (), s32[]{:S(2)}) async-start(), calls=%async_computation.9 | async-start | bytes 14155776 | tf_op jit(solution)/shard_map/reduce_scatter | solution.py:525
  362.0 559.4 %reduce-scatter.5.cloned.1.call-start = ((), (), s32[]{:S(2)}) async-start(), calls=%async_computation.8 | async-start | bytes 14155776 | tf_op jit(solution)/shard_map/reduce_scatter | solution.py:525
  506.3 60.7 %collective-permute-start.52 = (bf16[2,160,768]{2,1,0:T(8,128)(2,1)S(1)}, bf16[2,160,768]{2,1,0:T(8,128)(2,1)S(1)}, u32[]{:S(2)}, u32[]{:S(2)}) collective-permute-start(bf16[2,160,768]{2,1,0:T(8,128)(2,1)S(1)} %copy-done.48), channel_id=1, source_target_pairs={{0,1},{1,0},{2,3},{3,2},{4,5},{5,4},{6,7},{7,6},{8,9},{9,8},{10,11... | collective-permute-start | bytes 1474568 | tf_op jit(solution)/shard_map/ppermute | solution.py:435
  507.2 91.8 %collective-permute-start.53 = (bf16[2,160,768]{2,1,0:T(8,128)(2,1)S(1)}, bf16[2,160,768]{2,1,0:T(8,128)(2,1)S(1)}, u32[]{:S(2)}, u32[]{:S(2)}) collective-permute-start(bf16[2,160,768]{2,1,0:T(8,128)(2,1)S(1)} %copy-done.47), channel_id=1, source_target_pairs={{0,2},{1,3},{2,0},{3,1},{4,6},{5,7},{6,4},{7,5},{8,10},{9,11},{10,... | collective-permute-start | bytes 1474568 | tf_op jit(solution)/shard_map/ppermute | solution.py:435
  519.1 79.9 %collective-permute-start.54 = (bf16[2,160,768]{2,1,0:T(8,128)(2,1)S(1)}, bf16[2,160,768]{2,1,0:T(8,128)(2,1)S(1)}, u32[]{:S(2)}, u32[]{:S(2)}) collective-permute-start(bf16[2,160,768]{2,1,0:T(8,128)(2,1)S(1)} %copy-done.46), channel_id=1, source_target_pairs={{0,3},{1,2},{2,1},{3,0},{4,7},{5,6},{6,5},{7,4},{8,11},{9,10},{10,... | collective-permute-start | bytes 1474568 | tf_op jit(solution)/shard_map/ppermute | solution.py:435
  535.8 73.3 %collective-permute-start.37 = (bf16[2,160,768]{2,1,0:T(8,128)(2,1)S(1)}, bf16[2,160,768]{2,1,0:T(8,128)(2,1)S(1)}, u32[]{:S(2)}, u32[]{:S(2)}) collective-permute-start(bf16[2,160,768]{2,1,0:T(8,128)(2,1)S(1)} %copy-done.57), channel_id=1, source_target_pairs={{0,1},{1,0},{2,3},{3,2},{4,5},{5,4},{6,7},{7,6},{8,9},{9,8},{10,11... | collective-permute-start | bytes 1474568 | tf_op jit(solution)/shard_map/ppermute | solution.py:435
  538.5 102.7 %collective-permute-start.38 = (bf16[2,160,768]{2,1,0:T(8,128)(2,1)S(1)}, bf16[2,160,768]{2,1,0:T(8,128)(2,1)S(1)}, u32[]{:S(2)}, u32[]{:S(2)}) collective-permute-start(bf16[2,160,768]{2,1,0:T(8,128)(2,1)S(1)} %copy-done.56), channel_id=1, source_target_pairs={{0,2},{1,3},{2,0},{3,1},{4,6},{5,7},{6,4},{7,5},{8,10},{9,11},{10,... | collective-permute-start | bytes 1474568 | tf_op jit(solution)/shard_map/ppermute | solution.py:435
  567.0 74.2 %collective-permute-start.39 = (bf16[2,160,768]{2,1,0:T(8,128)(2,1)S(1)}, bf16[2,160,768]{2,1,0:T(8,128)(2,1)S(1)}, u32[]{:S(2)}, u32[]{:S(2)}) collective-permute-start(bf16[2,160,768]{2,1,0:T(8,128)(2,1)S(1)} %copy-done.55), channel_id=1, source_target_pairs={{0,3},{1,2},{2,1},{3,0},{4,7},{5,6},{6,5},{7,4},{8,11},{9,10},{10,... | collective-permute-start | bytes 1474568 | tf_op jit(solution)/shard_map/ppermute | solution.py:435
  599.1 63.2 %collective-permute-start.50 = (bf16[2,160,768]{2,1,0:T(8,128)(2,1)S(1)}, bf16[2,160,768]{2,1,0:T(8,128)(2,1)S(1)}, u32[]{:S(2)}, u32[]{:S(2)}) collective-permute-start(bf16[2,160,768]{2,1,0:T(8,128)(2,1)S(1)} %copy-done.53), channel_id=1, source_target_pairs={{0,2},{1,3},{2,0},{3,1},{4,6},{5,7},{6,4},{7,5},{8,10},{9,11},{10,... | collective-permute-start | bytes 1474568 | tf_op jit(solution)/shard_map/ppermute | solution.py:435
  609.1 53.2 %collective-permute-start.51 = (bf16[2,160,768]{2,1,0:T(8,128)(2,1)S(1)}, bf16[2,160,768]{2,1,0:T(8,128)(2,1)S(1)}, u32[]{:S(2)}, u32[]{:S(2)}) collective-permute-start(bf16[2,160,768]{2,1,0:T(8,128)(2,1)S(1)} %copy-done.52), channel_id=1, source_target_pairs={{0,3},{1,2},{2,1},{3,0},{4,7},{5,6},{6,5},{7,4},{8,11},{9,10},{10,... | collective-permute-start | bytes 1474568 | tf_op jit(solution)/shard_map/ppermute | solution.py:435
  641.2 78.2 %collective-permute-start.67 = (bf16[4,96,2048]{2,1,0:T(8,128)(2,1)}, bf16[4,96,2048]{2,1,0:T(8,128)(2,1)}, u32[]{:S(2)}, u32[]{:S(2)}) collective-permute-start(bf16[4,96,2048]{2,1,0:T(8,128)(2,1)} %dynamic-slice_bitcast_fusion.2), channel_id=1, source_target_pairs={{0,4},{4,0},{8,12},{12,8},{16,20},{20,16},{24,28},{28,24},{1,5},{5... | collective-permute-start | bytes 4718600 | tf_op jit(solution)/shard_map/ppermute | solution.py:46
  641.2 84.0 %collective-permute-start.61 = (bf16[4,96,2048]{2,1,0:T(8,128)(2,1)}, bf16[4,96,2048]{2,1,0:T(8,128)(2,1)}, u32[]{:S(2)}, u32[]{:S(2)}) collective-permute-start(bf16[4,96,2048]{2,1,0:T(8,128)(2,1)} %dynamic-slice_bitcast_fusion.3), channel_id=1, source_target_pairs={{0,4},{4,0},{8,12},{12,8},{16,20},{20,16},{24,28},{28,24},{1,5},{5... | collective-permute-start | bytes 4718600 | tf_op jit(solution)/shard_map/ppermute | solution.py:46
  641.7 86.7 %collective-permute-start.74 = (bf16[2,256,768]{2,1,0:T(8,128)(2,1)S(1)}, bf16[2,256,768]{2,1,0:T(8,128)(2,1)}, u32[]{:S(2)}, u32[]{:S(2)}) collective-permute-start(bf16[2,256,768]{2,1,0:T(8,128)(2,1)S(1)} %pad_maximum_fusion.5), channel_id=1, source_target_pairs={{0,8},{4,20},{8,0},{12,28},{16,24},{20,4},{24,16},{28,12},{1,9},{5... | collective-permute-start | bytes 2359304 | tf_op jit(solution)/shard_map/ppermute | solution.py:46
  778.0 49.0 %collective-permute-start.76 = (bf16[256,768]{1,0:T(8,128)(2,1)S(1)}, bf16[256,768]{1,0:T(8,128)(2,1)S(1)}, u32[]{:S(2)}, u32[]{:S(2)}) collective-permute-start(bf16[256,768]{1,0:T(8,128)(2,1)S(1)} %fusion.13), channel_id=1, source_target_pairs={{0,1},{1,0},{2,3},{3,2},{4,5},{5,4},{6,7},{7,6},{8,9},{9,8},{10,11... | collective-permute-start | bytes 1179656 | tf_op jit(solution)/shard_map/ppermute | solution.py:435
  789.4 58.8 %collective-permute-start.77 = (bf16[256,768]{1,0:T(8,128)(2,1)S(1)}, bf16[256,768]{1,0:T(8,128)(2,1)S(1)}, u32[]{:S(2)}, u32[]{:S(2)}) collective-permute-start(bf16[256,768]{1,0:T(8,128)(2,1)S(1)} %fusion.13), channel_id=1, source_target_pairs={{0,2},{1,3},{2,0},{3,1},{4,6},{5,7},{6,4},{7,5},{8,10},{9,11},{10,... | collective-permute-start | bytes 1179656 | tf_op jit(solution)/shard_map/ppermute | solution.py:435
  800.1 58.6 %collective-permute-start.64 = (bf16[96,2048]{1,0:T(8,128)(2,1)S(1)}, bf16[96,2048]{1,0:T(8,128)(2,1)S(1)}, u32[]{:S(2)}, u32[]{:S(2)}) collective-permute-start(bf16[96,2048]{1,0:T(8,128)(2,1)S(1)} %fusion.15), channel_id=1, source_target_pairs={{0,1},{1,0},{2,3},{3,2},{4,5},{5,4},{6,7},{7,6},{8,9},{9,8},{10,11... | collective-permute-start | bytes 1179656 | tf_op jit(solution)/shard_map/ppermute | solution.py:435
  827.0 66.9 %collective-permute-start.65 = (bf16[96,2048]{1,0:T(8,128)(2,1)S(1)}, bf16[96,2048]{1,0:T(8,128)(2,1)S(1)}, u32[]{:S(2)}, u32[]{:S(2)}) collective-permute-start(bf16[96,2048]{1,0:T(8,128)(2,1)S(1)} %fusion.15), channel_id=1, source_target_pairs={{0,2},{1,3},{2,0},{3,1},{4,6},{5,7},{6,4},{7,5},{8,10},{9,11},{10,... | collective-permute-start | bytes 1179656 | tf_op jit(solution)/shard_map/ppermute | solution.py:435
  827.0 66.9 %collective-permute-start.66 = (bf16[96,2048]{1,0:T(8,128)(2,1)S(1)}, bf16[96,2048]{1,0:T(8,128)(2,1)S(1)}, u32[]{:S(2)}, u32[]{:S(2)}) collective-permute-start(bf16[96,2048]{1,0:T(8,128)(2,1)S(1)} %fusion.15), channel_id=1, source_target_pairs={{0,3},{1,2},{2,1},{3,0},{4,7},{5,6},{6,5},{7,4},{8,11},{9,10},{10,... | collective-permute-start | bytes 1179656 | tf_op jit(solution)/shard_map/ppermute | solution.py:435
  848.2 67.3 %collective-permute-start.59 = (bf16[96,3200]{1,0:T(8,128)(2,1)S(1)}, bf16[96,3200]{1,0:T(8,128)(2,1)S(1)}, u32[]{:S(2)}, u32[]{:S(2)}) collective-permute-start(bf16[96,3200]{1,0:T(8,128)(2,1)S(1)} %fusion.6), channel_id=1, source_target_pairs={{0,2},{1,3},{2,0},{3,1},{4,6},{5,7},{6,4},{7,5},{8,10},{9,11},{10,... | collective-permute-start | bytes 1843208 | tf_op jit(solution)/shard_map/ppermute | solution.py:435
  858.7 56.8 %collective-permute-start.60 = (bf16[96,3200]{1,0:T(8,128)(2,1)S(1)}, bf16[96,3200]{1,0:T(8,128)(2,1)S(1)}, u32[]{:S(2)}, u32[]{:S(2)}) collective-permute-start(bf16[96,3200]{1,0:T(8,128)(2,1)S(1)} %fusion.6), channel_id=1, source_target_pairs={{0,3},{1,2},{2,1},{3,0},{4,7},{5,6},{6,5},{7,4},{8,11},{9,10},{10,... | collective-permute-start | bytes 1843208 | tf_op jit(solution)/shard_map/ppermute | solution.py:435
  (139 other events, 2981.1 us)
Sparse Core Ops, SparseCore 0:
  10.5 60.4 all-gather.10
  73.5 73.4 all-gather.8
  149.4 45.3 all-gather.6
  197.2 71.9 all-gather.4
  272.4 61.6 reduce-scatter.10
  361.4 81.9 reduce-scatter.8
  446.9 92.2 reduce-scatter.6
  542.7 92.2 reduce-scatter.4

commit v2 on v1

v2 whole, which is shorter than its diff:
```python
import functools

import jax
import jax.numpy as jnp
from jax import lax
from jax.experimental import pallas as pl
from jax.experimental.pallas import tpu as pltpu
from jax.sharding import PartitionSpec as P

HEAD_DIM = 64
PAIR = 2 * HEAD_DIM
CAP = 40
LANES = 128
EPSILON = 1e-06
F32 = jnp.float32
BF16 = jnp.bfloat16
NN = (((1,), (0,)), ((), ()))
NT = (((1,), (1,)), ((), ()))
TN = (((0,), (0,)), ((), ()))
VMEM_BYTES = 60 * 1024 * 1024
ANY = pl.BlockSpec(memory_space=pl.ANY)


def mm(left, right, dims):
    return lax.dot_general(left, right, dims, preferred_element_type=F32)


def iota(shape, axis):
    return lax.broadcasted_iota(jnp.int32, shape, axis)


def skipping(body, inputs, unread):
    return lambda *refs: body(*refs[:inputs], *refs[inputs + unread :])


def tie(field, *after):
    return pl.pallas_call(
        lambda *refs: None,
        out_shape=jax.ShapeDtypeStruct(field.shape, field.dtype),
        in_specs=[ANY] * (1 + len(after)),
        out_specs=ANY,
        input_output_aliases={0: 0},
        name="tie",
    )(field, *after)


def place_of(flat, rows):
    at = iota((rows, flat.shape[1]), 0)
    held = jnp.logical_or(flat[0:1, :] == at, flat[1:2, :] == at)
    return jnp.where(held, 1.0, 0.0).astype(BF16)


def put_rows(sent, out):
    for expert in range(out.shape[0]):
        out[expert, 0] = sent[expert * CAP : (expert + 1) * CAP].astype(BF16)


def dispatch_kernel(flat_ref, field_ref, out_ref):
    put_rows(mm(place_of(flat_ref[0], out_ref.shape[0] * CAP), field_ref[0], NN), out_ref)


def swap_halves(field):
    low = iota(field.shape, 1) % HEAD_DIM < HEAD_DIM // 2
    ahead = pltpu.roll(field, PAIR - HEAD_DIM // 2, 1)
    behind = pltpu.roll(field, HEAD_DIM // 2, 1)
    return jnp.where(low, ahead, behind)


def turn(field, cosine, sine):
    return field * cosine + swap_halves(field) * sine


def allowed_of(column_ref, row_ref):
    length = row_ref.shape[2]
    square = (length, length)
    return jnp.logical_and(iota(square, 0) >= iota(square, 1), column_ref[0] == row_ref[0])


def inverse_rms(field):
    return lax.rsqrt(jnp.mean(field * field, axis=-1, keepdims=True) + EPSILON)


def forward_kernel(
    experts, tokens_ref, column_ref, row_ref, flat_ref, weight_ref, gain_one_ref, gain_two_ref, cosine_ref, sine_ref,
    hidden_ref, mixed_ref, attended_ref, qkv_ref, logsum_ref, router_ref, sent_ref,
):
    width = tokens_ref.shape[2]
    x = tokens_ref[0].astype(F32)
    normed = (x * inverse_rms(x) * gain_one_ref[...]).astype(BF16)
    allowed = allowed_of(column_ref, row_ref)
    cosine, sine = cosine_ref[...], sine_ref[...]
    low = iota((x.shape[0], PAIR), 1) < HEAD_DIM
    lane = iota((x.shape[0], LANES), 1)
    logsum = jnp.zeros((x.shape[0], LANES), F32)
    for pair in range(width // PAIR):
        at = slice(pair * PAIR, (pair + 1) * PAIR)
        query = turn(mm(normed, weight_ref[:, at], NN), cosine, sine).astype(BF16) * BF16(0.125)
        key = turn(mm(normed, weight_ref[:, width + at.start : width + at.stop], NN), cosine, sine).astype(BF16)
        value = mm(normed, weight_ref[:, 2 * width + at.start : 2 * width + at.stop], NN).astype(BF16)
        qkv_ref[0, :, at] = query
        qkv_ref[0, :, width + at.start : width + at.stop] = key
        qkv_ref[0, :, 2 * width + at.start : 2 * width + at.stop] = value
        both = []
        for half in range(2):
            mine = low if half == 0 else jnp.logical_not(low)
            scores = jnp.where(allowed, mm(jnp.where(mine, query, BF16(0.0)), key, NT), -1e30)
            peak = jnp.max(scores, axis=-1, keepdims=True)
            expo = jnp.exp(scores - peak)
            total = jnp.sum(expo, axis=-1, keepdims=True)
            logsum = jnp.where(lane == 2 * pair + half, peak + jnp.log(total), logsum)
            both.append(mm((expo * (1.0 / total)).astype(BF16), value, NN))
        attended_ref[0, :, at] = jnp.where(low, both[0], both[1]).astype(BF16)
    logsum_ref[0] = logsum
    hidden = x + mm(attended_ref[0], weight_ref[:, 3 * width : 4 * width], NN)
    hidden_ref[0] = hidden
    mixed = (hidden * inverse_rms(hidden) * gain_two_ref[...]).astype(BF16)
    mixed_ref[0] = mixed
    logits = jnp.where(lane < experts, mm(mixed, weight_ref[:, 4 * width :], NN), -1e30)
    expo = jnp.exp(logits - jnp.max(logits, axis=-1, keepdims=True))
    router_ref[0] = expo / jnp.sum(expo, axis=-1, keepdims=True)
    put_rows(mm(place_of(flat_ref[0], experts * CAP), mixed, NN), sent_ref)


def get_rows(backs, which, experts, held_ref):
    owners, _, size = backs[0].shape[:3]
    for expert in range(experts):
        owner, local = expert // (len(backs) * size), expert % (len(backs) * size)
        held_ref[expert * CAP : (expert + 1) * CAP, :] = backs[local // size][owner, which, local % size, 0].astype(F32)
    return held_ref[...].astype(BF16)


def backward_kernel(
    experts, groups, tokens_ref, grad_ref, column_ref, row_ref, flat_ref, routes_ref, weight_ref, gain_one_ref, gain_two_ref,
    cosine_ref, sine_ref, hidden_ref, mixed_ref, attended_ref, qkv_ref, logsum_ref, router_ref, shared_ref, d_mixed_ref, *refs,
):
    backs = refs[:groups]
    out_ref, grad_tokens_ref, grad_weight_ref, held_ref, sum_ref, gains_ref, d_qkv_ref = refs[groups:]
    width = tokens_ref.shape[2]
    step = pl.program_id(0)

    @pl.when(step == 0)
    def _():
        sum_ref[...] = jnp.zeros_like(sum_ref)
        gains_ref[...] = jnp.zeros_like(gains_ref)

    length = tokens_ref.shape[1]
    lane = iota((length, LANES), 1)
    grad = grad_ref[0].astype(F32)
    hidden = hidden_ref[0]
    mixed = mixed_ref[0]
    router = router_ref[0]
    flat = flat_ref[0]
    rows = experts * CAP
    at_row = iota((rows, length), 0)
    came = get_rows(backs, 0, experts, held_ref)
    layer = hidden + shared_ref[0]
    d_router = jnp.zeros((length, LANES), F32)
    for choice in range(2):
        place = jnp.where(flat[choice : choice + 1, :] == at_row, 1.0, 0.0).astype(BF16)
        picked = mm(place, came, TN)
        chosen = lane == routes_ref[0, :, choice : choice + 1]
        gate = jnp.sum(jnp.where(chosen, router, 0.0), axis=-1, keepdims=True)
        layer = layer + gate * picked
        d_gate = jnp.sum(grad * picked, axis=-1, keepdims=True)
        d_router = d_router + jnp.where(chosen, d_gate, 0.0)
    out_ref[0] = layer.astype(BF16)
    d_logits = (router * (d_router - jnp.sum(router * d_router, axis=-1, keepdims=True))).astype(BF16)
    sum_ref[:, 4 * width :] += mm(mixed, d_logits, TN)
    came = get_rows(backs, 1, experts, held_ref)
    d_mixed = d_mixed_ref[0] + mm(place_of(flat, rows), came, TN) + mm(d_logits, weight_ref[:, 4 * width :], NT)

    inverse_two = inverse_rms(hidden)
    unit_two = hidden * inverse_two
    gains_ref[1:2, :] += jnp.sum(d_mixed * unit_two, axis=0, keepdims=True)
    scaled = d_mixed * gain_two_ref[...]
    d_hidden = grad + inverse_two * (scaled - unit_two * jnp.mean(scaled * unit_two, axis=-1, keepdims=True))
    d_branch = d_hidden.astype(BF16)
    sum_ref[:, 3 * width : 4 * width] += mm(attended_ref[0], d_branch, TN)
    d_attended = mm(d_branch, weight_ref[:, 3 * width : 4 * width], NT).astype(BF16)

    allowed = allowed_of(column_ref, row_ref)
    cosine, sine = cosine_ref[...], -sine_ref[...]
    low = iota((length, PAIR), 1) < HEAD_DIM
    logsum = logsum_ref[0]
    for pair in range(width // PAIR):
        at = slice(pair * PAIR, (pair + 1) * PAIR)
        query = qkv_ref[0, :, at]
        key = qkv_ref[0, :, width + at.start : width + at.stop]
        value = qkv_ref[0, :, 2 * width + at.start : 2 * width + at.stop]
        d_out = d_attended[:, at]
        parts = []
        for half in range(2):
            mine = low if half == 0 else jnp.logical_not(low)
            scores = jnp.where(allowed, mm(jnp.where(mine, query, BF16(0.0)), key, NT), -1e30)
            head = 2 * pair + half
            probs = jnp.exp(scores - logsum[:, head : head + 1])
            d_probs = mm(jnp.where(mine, d_out, BF16(0.0)), value, NT)
            d_scores = (probs * (d_probs - jnp.sum(probs * d_probs, axis=-1, keepdims=True))).astype(BF16)
            parts.append((mm(d_scores, key, NN), mm(d_scores, query, TN), mm(probs.astype(BF16), d_out, TN)))
        d_query, d_key, d_value = (jnp.where(low, a, b) for a, b in zip(*parts))
        d_qkv_ref[:, at] = turn(d_query * 0.125, cosine, sine).astype(BF16)
        d_qkv_ref[:, width + at.start : width + at.stop] = turn(d_key, cosine, sine).astype(BF16)
        d_qkv_ref[:, 2 * width + at.start : 2 * width + at.stop] = d_value.astype(BF16)

    x = tokens_ref[0].astype(F32)
    inverse_one = inverse_rms(x)
    unit_one = x * inverse_one
    normed = (unit_one * gain_one_ref[...]).astype(BF16)
    d_qkv = d_qkv_ref[...]
    sum_ref[:, : 3 * width] += mm(normed, d_qkv, TN)
    d_normed = mm(d_qkv, weight_ref[:, : 3 * width], NT)
    gains_ref[0:1, :] += jnp.sum(d_normed * unit_one, axis=0, keepdims=True)
    scaled = d_normed * gain_one_ref[...]
    grad_tokens_ref[0] = d_hidden + inverse_one * (
        scaled - unit_one * jnp.mean(scaled * unit_one, axis=-1, keepdims=True))

    @pl.when(step == pl.num_programs(0) - 1)
    def _():
        grad_weight_ref[:, : 4 * width] = sum_ref[:, : 4 * width].astype(BF16)
        gains = jnp.concatenate(
            [jnp.zeros((experts, width), F32), gains_ref[...], jnp.zeros((LANES - experts - 8, width), F32)], axis=0)
        grad_weight_ref[:, 4 * width :] = (sum_ref[:, 4 * width :] + gains.T).astype(BF16)


def pack_pieces(packed, gate, up, down):
    steps, width = packed.shape[1], packed.shape[2]
    rows = gate.shape[0]
    for f in range(steps):
        for j in range(width // rows):
            at = slice((j * steps + f) * LANES, (j * steps + f + 1) * LANES)
            yield packed.at[0, f, j * rows : (j + 1) * rows], gate.at[:, at]
            yield packed.at[1, f, j * rows : (j + 1) * rows], up.at[:, at]
        for c in range(width // LANES):
            at = slice(c * LANES, (c + 1) * LANES)
            yield packed.at[2, f, at], down.at[f * LANES : (f + 1) * LANES, at]


def pack_kernel(count, *refs):
    out = refs[-1]
    step = pl.program_id(0)
    for n in range((len(refs) - 1) // 3):
        @pl.when((step < count) if n == 0 else (step >= count))
        def _():
            for to, source in pack_pieces(out, *refs[3 * n : 3 * n + 3]):
                to[...] = source[...]


def pack(first, count, pool, shared, devices):
    rows, units = pool[0].shape[1:]
    width = rows * devices
    steps = units // (devices * LANES)
    squeezed = pl.Squeezed()
    take = lambda l: (first + jnp.minimum(l, count - 1), 0, 0)
    total = count + (1 if shared else 0)
    return pl.pallas_call(
        functools.partial(pack_kernel, count),
        grid=(total,),
        in_specs=[pl.BlockSpec((squeezed,) + field.shape[1:], take) for field in pool]
        + [pl.BlockSpec(field.shape, lambda l: (0, 0)) for field in shared],
        out_specs=pl.BlockSpec((squeezed, 3, steps, width, LANES), lambda l: (l, 0, 0, 0, 0)),
        out_shape=jax.ShapeDtypeStruct((total, 3, steps, width, LANES), BF16),
        name="pack",
    )(*pool, *shared)


def unpack_kernel(sizes, *refs):
    packs, outs = refs[: len(sizes)], refs[len(sizes) :]
    step = pl.program_id(0)
    start = 0
    for n, size in enumerate(sizes):
        @pl.when(jnp.logical_and(step >= start, step < start + size))
        def _(source=packs[n]):
            for piece, to in pack_pieces(source, *outs):
                to[...] = piece[...].astype(F32)
        start += size


def unpack(packs, sizes, rows, units, name):
    squeezed = pl.Squeezed()
    specs, start = [], 0
    for field, size in zip(packs, sizes):
        specs.append(pl.BlockSpec(
            (squeezed,) + field.shape[1:],
            lambda l, start=start, size=size: (jnp.clip(l - start, 0, size - 1), 0, 0, 0, 0)))
        start += size
    width = packs[0].shape[3]
    shapes = [(rows, units), (rows, units), (rows * units // width, width)]
    return pl.pallas_call(
        functools.partial(unpack_kernel, tuple(sizes)),
        grid=(start,),
        in_specs=specs,
        out_specs=[pl.BlockSpec((squeezed,) + shape, lambda l: (l, 0, 0)) for shape in shapes],
        out_shape=[jax.ShapeDtypeStruct((start,) + shape, F32) for shape in shapes],
        name=name,
    )(*packs)


def feed_step(x, d, gate_weight, up_weight, down_weight, out, dx):
    g = mm(x, gate_weight, NN)
    u = mm(x, up_weight, NN)
    sigma = 1.0 / (1.0 + jnp.exp(-g))
    active = g * sigma
    inner = (active * u).astype(BF16)
    out[...] += mm(inner, down_weight, NN)
    d_inner = mm(d, down_weight, NT)
    d_g = (d_inner * u * (sigma * (1.0 + g * (1.0 - sigma)))).astype(BF16)
    d_u = (d_inner * active).astype(BF16)
    dx[...] += mm(d_g, gate_weight, NT) + mm(d_u, up_weight, NT)
    return mm(x, d_g, TN).astype(BF16), mm(x, d_u, TN).astype(BF16), mm(inner, d, TN).astype(BF16)


def feed_kernel(gated, packed, rows_ref, grads_ref, *refs):
    if gated:
        gates_ref, refs = refs[0], refs[1:]
    count, part, width = rows_ref.shape
    weights = refs[: 1 if packed else 3]
    refs = refs[len(weights) :]
    if gated:
        back_ref, refs = refs[0], refs[1:]
        sums, (x_ref, d_ref, out_ref, dx_ref) = refs[:-4], refs[-4:]
    else:
        out_ref, dx_ref, sums = refs[0].at[0], refs[1].at[0], refs[2:]
    step = pl.program_id(1)

    @pl.when(step == 0)
    def _():
        out_ref[...] = jnp.zeros_like(out_ref)
        dx_ref[...] = jnp.zeros_like(dx_ref)
        if gated:
            square = (part, part)
            for k in range(count):
                at = slice(k * part, (k + 1) * part)
                x_ref[at, :] = rows_ref[k]
                line = jnp.broadcast_to(gates_ref[k], square)
                column = jnp.sum(jnp.where(iota(square, 0) == iota(square, 1), line, 0.0), axis=1, keepdims=True)
                d_ref[at, :] = (grads_ref[k].astype(F32) * column).astype(BF16)

    x, d = (x_ref[...], d_ref[...]) if gated else (rows_ref[0], grads_ref[0])
    if packed:
        field, total = weights[0], sums[0]
        devices = field.shape[0]
        rows = width // devices
        size = min(devices, 4)
        for start in range(0, devices, size):
            columns = range(start, start + size)
            side = lambda n: jnp.concatenate(
                [field[:, n, j * rows : (j + 1) * rows, :].reshape(width, LANES) for j in columns], axis=1)
            down = jnp.concatenate(
                [field[start : start + size, 2, c * LANES : (c + 1) * LANES, :].reshape(size * LANES, LANES)
                 for c in range(width // LANES)], axis=1)
            gate_sum, up_sum, down_sum = feed_step(x, d, side(0), side(1), down, out_ref, dx_ref)
            for n, value in enumerate((gate_sum, up_sum)):
                for j in columns:
                    total[:, n, j * rows : (j + 1) * rows, :] = value[
                        :, (j - start) * LANES : (j - start + 1) * LANES].reshape(devices, rows, LANES)
            for c in range(width // LANES):
                at = slice(c * LANES, (c + 1) * LANES)
                total[start : start + size, 2, at, :] = down_sum[:, at].reshape(size, LANES, LANES)
    else:
        sums[0][0], sums[0][1], sums[1][...] = feed_step(x, d, *(ref[...] for ref in weights), out_ref, dx_ref)

    if gated:
        @pl.when(step == pl.num_programs(1) - 1)
        def _():
            for k in range(count):
                at = slice(k * part, (k + 1) * part)
                back_ref[k, 0] = out_ref[at, :].astype(BF16)
                back_ref[k, 1] = dx_ref[at, :].astype(BF16)


def feed(rows, grads, gates, weights, first_row, first_weight, experts, name, carried=None, after=()):
    count, _, part, width = rows.shape
    squeezed = pl.Squeezed()
    gated, packed = gates is not None, len(weights) == 1
    total = count * part
    row = lambda l, f: (0, first_row + l, 0, 0)
    operands = [rows, grads] + ([gates] if gated else [])
    in_specs = [pl.BlockSpec((count, squeezed, part, width), row)] * 2
    in_specs += [pl.BlockSpec((count, squeezed, 1, part), row)] * gated
    if packed:
        devices, _, _, steps = weights[0].shape[:4]
        units = steps * devices * LANES
        pack_spec = pl.BlockSpec(
            (devices, squeezed, 3, squeezed, width, LANES), lambda l, f: (0, first_weight + l, 0, f, 0, 0))
        operands += weights
        in_specs += [pack_spec]
        sum_specs, sum_shapes = [pack_spec], [jax.ShapeDtypeStruct(weights[0].shape, BF16)]
    else:
        units, block = weights[1].shape[1], 512
        steps = units // block
        side = lambda n: pl.BlockSpec((squeezed, squeezed, width, block), lambda l, f: (l, n, 0, f))
        down_spec = pl.BlockSpec((squeezed, block, width), lambda l, f: (l, f, 0))
        operands += [weights[0], weights[0], weights[1]]
        in_specs += [side(0), side(1), down_spec]
        sum_specs = [pl.BlockSpec((squeezed, 2, width, block), lambda l, f: (l, 0, 0, f)), down_spec]
        sum_shapes = [jax.ShapeDtypeStruct(field.shape, BF16) for field in weights]
    if gated:
        out_specs = [pl.BlockSpec((count, 2, squeezed, part, width), lambda l, f: (0, 0, l, 0, 0))]
        out_shapes = [jax.ShapeDtypeStruct((count, 2, experts, part, width), BF16)]
        scratch = [pltpu.VMEM((total, width), BF16)] * 2 + [pltpu.VMEM((total, width), F32)] * 2
    else:
        out_specs = [pl.BlockSpec((count, squeezed, part, width), lambda l, f: (0, l, 0, 0))] * 2
        out_shapes = [jax.ShapeDtypeStruct((count, experts, part, width), F32)] * 2
        scratch = []
    inputs = len(operands)
    unread = ([carried] if carried is not None else []) + list(after)
    return pl.pallas_call(
        skipping(functools.partial(feed_kernel, gated, packed), inputs, len(unread)),
        grid=(experts, steps),
        in_specs=in_specs + [ANY] * len(unread),
        out_specs=out_specs + sum_specs,
        out_shape=out_shapes + sum_shapes,
        scratch_shapes=scratch,
        input_output_aliases={inputs: len(out_shapes)} if carried is not None else {},
        compiler_params=pltpu.CompilerParams(vmem_limit_bytes=VMEM_BYTES),
        cost_estimate=pl.CostEstimate(
            flops=18 * experts * total * width * units,
            bytes_accessed=experts * (12 * width * units + 8 * total * width),
            transcendentals=experts * total * units,
        ),
        name=name,
    )(*operands, *unread)


def on_device(
    tokens, cotangent, segments, routes, slots,
    norm1_gain, w_query, w_key, w_value, w_out, norm2_gain, w_router,
    shared_gate, shared_up, shared_down, expert_gate, expert_up, expert_down,
):
    length, width = tokens.shape[2], tokens.shape[3]
    batch = tokens.shape[0] * tokens.shape[1]
    devices = lax.axis_size("dp")
    owners = lax.axis_size("expert")
    local_experts = expert_gate.shape[0]
    experts = owners * local_experts
    hidden_units = shared_gate.shape[1]
    groups = 2
    size = local_experts // groups
    packed = (hidden_units == expert_gate.shape[2] and hidden_units % (devices * LANES) == 0
              and width % LANES == 0 and expert_gate.shape[1] % 16 == 0)
    pool = (expert_gate, expert_up, expert_down)

    pad = LANES - experts - 2
    first_part = jnp.concatenate(
        [w_query, w_key, w_value, w_out, w_router, norm1_gain[:, None], norm2_gain[:, None],
         jnp.zeros((w_query.shape[0], pad), BF16)], axis=1)
    first_all = lax.all_gather(first_part, "dp", axis=0, tiled=True)
    if packed:
        weights = [
            [lax.all_gather(
                pack(h * size, size, pool, (shared_gate, shared_up, shared_down) if h == 0 else (), devices), "dp", axis=0)]
            for h in range(groups)]
        shared_weights = weights[0]
    else:
        gather = lambda both, down: [
            lax.all_gather(both, "dp", axis=2, tiled=True), lax.all_gather(down, "dp", axis=1, tiled=True)]
        shared_weights = gather(jnp.stack([shared_gate, shared_up])[None], shared_down[None])
        weights = []
        for h in range(groups):
            part = slice(h * size, (h + 1) * size)
            weights.append(gather(jnp.stack([expert_gate[part], expert_up[part]], axis=1), expert_down[part]))
    gains = first_all[:, 4 * width + experts : 4 * width + experts + 2].astype(F32).T
    gain_one, gain_two = gains[0:1], gains[1:2]

    route_ids = routes.reshape(batch, length, 2)
    flat = (route_ids * CAP + slots.reshape(batch, length, 2)).transpose(0, 2, 1)

    def trade(field):
        return lax.all_to_all(field.reshape(owners, local_experts, batch * CAP, width), "expert", 0, 0)

    whole = lambda shape: pl.BlockSpec(shape, lambda b: (0,) * len(shape))
    each = lambda *shape: pl.BlockSpec((1,) + shape, lambda b: (b, 0, 0))
    piece_spec = pl.BlockSpec((experts, 1, CAP, width), lambda b: (0, b, 0, 0))
    piece_shape = jax.ShapeDtypeStruct((experts, batch, CAP, width), BF16)
    rows = experts * CAP
    params = pltpu.CompilerParams(vmem_limit_bytes=VMEM_BYTES)

    grad_low = cotangent.reshape(batch, length, width)
    grad_sent = pl.pallas_call(
        dispatch_kernel,
        grid=(batch,),
        in_specs=[each(2, length), each(length, width)],
        out_specs=piece_spec,
        out_shape=piece_shape,
        compiler_params=params,
        cost_estimate=pl.CostEstimate(
            flops=2 * batch * rows * length * width, bytes_accessed=4 * batch * rows * width, transcendentals=0),
        name="dispatch",
    )(flat, grad_low)
    grad_arrived = trade(grad_sent)

    token_rows = tokens.reshape(batch, length, width)
    segment_ids = segments.reshape(batch, length)
    half = HEAD_DIM // 2
    frequency = jnp.exp(-jnp.log(10000.0) * jnp.arange(half, dtype=F32) / half)
    angles = jnp.arange(length, dtype=F32)[:, None] * frequency[None, :]
    cosine = jnp.tile(jnp.cos(angles), (1, 4))
    sine = jnp.tile(jnp.concatenate([-jnp.sin(angles), jnp.sin(angles)], axis=1), (1, 2))
    columns = first_all.shape[1]
    position_args = (segment_ids[:, :, None], segment_ids[:, None, :], flat)
    position_specs = [each(length, 1), each(1, length), each(2, length)]
    weight_args = (first_all, gain_one, gain_two, cosine, sine)
    weight_specs = [
        whole((width, columns)), whole((1, width)), whole((1, width)), whole((length, LANES)), whole((length, LANES))]
    kept_shapes = [
        jax.ShapeDtypeStruct((batch, length, width), F32),
        jax.ShapeDtypeStruct((batch, length, width), BF16),
        jax.ShapeDtypeStruct((batch, length, width), BF16),
        jax.ShapeDtypeStruct((batch, length, 3 * width), BF16),
        jax.ShapeDtypeStruct((batch, length, LANES), F32),
        jax.ShapeDtypeStruct((batch, length, LANES), F32),
    ]
    kept_specs = [each(*shape.shape[1:]) for shape in kept_shapes]
    tokens_all = batch * length
    outs = pl.pallas_call(
        functools.partial(forward_kernel, experts),
        grid=(batch,),
        in_specs=[each(length, width)] + position_specs + weight_specs,
        out_specs=kept_specs + [piece_spec],
        out_shape=kept_shapes + [piece_shape],
        compiler_params=params,
        cost_estimate=pl.CostEstimate(
            flops=2 * tokens_all * width * (columns + 4 * length + rows),
            bytes_accessed=2 * width * columns + tokens_all * width * 20,
            transcendentals=tokens_all * length * width // HEAD_DIM,
        ),
        name="attention",
    )(token_rows, *position_args, *weight_args)
    kept, sent = outs[:6], outs[6]
    mixed_in, router = kept[1], kept[5]
    arrived = trade(sent)
    chosen = route_ids[..., None] == jnp.arange(experts, dtype=jnp.int32)
    gates = jnp.sum(jnp.where(chosen, router[:, :, None, :experts], 0.0), axis=-1).transpose(0, 2, 1)
    held = flat[:, :, None, :] == jnp.arange(rows, dtype=jnp.int32)[:, None]
    slot_gates = jnp.sum(jnp.where(held, gates[:, :, None, :], 0.0), axis=(1, 3))
    slot_gates = slot_gates.reshape(batch, owners, local_experts, CAP).transpose(1, 2, 0, 3)
    slot_gates = lax.all_to_all(slot_gates.reshape(owners, local_experts, 1, batch * CAP), "expert", 0, 0)

    shared_out, d_mixed, *shared_sums = feed(
        mixed_in.reshape(1, 1, tokens_all, width), grad_low.reshape(1, 1, tokens_all, width), None,
        shared_weights, 0, size if packed else 0, 1, "shared")

    backs, sums = [], []
    for h in range(groups):
        results, *grads = feed(
            arrived, grad_arrived, slot_gates, weights[h], h * size, 0, size, "experts",
            shared_sums[0] if packed and h == 0 else None, [shared_out if h == 0 else results])
        backs.append(lax.all_to_all(results, "expert", 0, 0).reshape(owners, 2, size, batch, CAP, width))
        sums.append(grads)

    layer_out, grad_tokens, first_grad = pl.pallas_call(
        functools.partial(backward_kernel, experts, groups),
        grid=(batch,),
        in_specs=[each(length, width)] * 2 + position_specs + [each(length, 2)] + weight_specs + kept_specs
        + [each(length, width)] * 2
        + [pl.BlockSpec((owners, 2, size, 1, CAP, width), lambda b: (0, 0, 0, b, 0, 0))] * groups,
        out_specs=[each(length, width)] * 2 + [whole((width, columns))],
        out_shape=[
            jax.ShapeDtypeStruct((batch, length, width), BF16),
            jax.ShapeDtypeStruct((batch, length, width), F32),
            jax.ShapeDtypeStruct((width, columns), BF16),
        ],
        scratch_shapes=[
            pltpu.VMEM((rows, width), F32),
            pltpu.VMEM((width, columns), F32),
            pltpu.VMEM((8, width), F32),
            pltpu.VMEM((length, 3 * width), BF16),
        ],
        compiler_params=params,
        cost_estimate=pl.CostEstimate(
            flops=4 * tokens_all * width * (columns + 4 * length + rows),
            bytes_accessed=4 * width * columns + tokens_all * width * 32,
            transcendentals=tokens_all * length * width // HEAD_DIM,
        ),
        name="attention_back",
    )(
        token_rows, grad_low, *position_args, route_ids, *weight_args, *kept,
        shared_out.reshape(batch, length, width), d_mixed.reshape(batch, length, width), *backs,
    )

    def over_owners(field):
        k = 1
        while k < owners:
            came = lax.ppermute(field, "expert", [(i, i ^ k) for i in range(owners)])
            field = field.astype(F32) + came.astype(F32)
            k *= 2
            field = field.astype(BF16) if k < owners else field
        return field

    units = hidden_units
    if packed:
        mine = []
        for field in sums:
            mine.append(lax.psum_scatter(tie(field[0], *mine[-1:]), "dp", scatter_dimension=0))
        first_grad = tie(first_grad, mine[-1])
        pool_mine = unpack(mine, [size] * groups, width // devices, units, "unpack_experts")
        shared_mine = unpack(
            [over_owners(mine[0][size:])], [1], width // devices, units, "unpack_shared")
        shared_mine = [field[0] for field in shared_mine]
    else:
        def scatter(both, down):
            return (lax.psum_scatter(both, "dp", scatter_dimension=2, tiled=True),
                    lax.psum_scatter(down, "dp", scatter_dimension=1, tiled=True))

        both, down = (jnp.concatenate(fields, axis=0).astype(F32) for fields in zip(*(scatter(*field) for field in sums)))
        pool_mine = [both[:, 0], both[:, 1], down]
        both, down = (over_owners(field[0]) for field in scatter(*shared_sums))
        shared_mine = [both[0], both[1], down]
    first_mine = over_owners(lax.psum_scatter(first_grad, "dp", scatter_dimension=0, tiled=True))
    return (
        layer_out.reshape(tokens.shape),
        grad_tokens.reshape(tokens.shape),
        first_mine[:, 4 * width + experts],
        first_mine[:, :width],
        first_mine[:, width : 2 * width],
        first_mine[:, 2 * width : 3 * width],
        first_mine[:, 3 * width : 4 * width],
        first_mine[:, 4 * width + experts + 1],
        first_mine[:, 4 * width : 4 * width + experts],
        *shared_mine,
        *pool_mine,
    )


def solution(mesh):
    token_spec = P(None, ("dp", "expert"), None, None)
    vector, matrix, pool = P("dp"), P("dp", None), P("expert", "dp", None)
    weights = (vector, matrix, matrix, matrix, matrix, vector, matrix, matrix, matrix, matrix, pool, pool, pool)
    return jax.shard_map(
        on_device,
        mesh=mesh,
        in_specs=(token_spec, token_spec, P(None, ("dp", "expert"), None), token_spec, token_spec) + weights,
        out_specs=(token_spec, token_spec) + weights,
        check_vma=False,
    )
```

time: 953 us -> 864 us (0.907); the launches traced: 934 us -> 856 us
  blocking collectives: 0 us -> 193 us
  starting transfers between devices: 198 us -> 16.3 us
  waiting for transfers between devices: 401 us -> 359 us
  other arithmetic: 35.6 us -> 5.56 us
  local copies, waits for them, and re-layouts: 41.6 us -> 16.6 us
    ppermute x79 -> x4, waiting for transfers between devices: 399 us -> 65 us  [over_owners(): came = lax.ppermute(field, 'expert', [(i, i ^ k) for i in range(owners)])]
    all_to_all x0 -> x3, blocking collectives: none -> 193 us  [the longest x2 184 us: on_device(): lax.all_to_all(results, 'expert', 0, 0)]
    ppermute x79 -> x4, starting transfers between devices: 188 us -> 4.81 us  [over_owners(): came = lax.ppermute(field, 'expert', [(i, i ^ k) for i in range(owners)])]
    reduce_scatter x4 -> x3, waiting for transfers between devices: 0.01 us -> 180 us  [the longest x2 130 us: on_device(): lax.psum_scatter(tie(field[0], *mine[-1:]), 'dp', scatter_dimension=0)]
    all_gather x4 -> x3, waiting for transfers between devices: 0.05 us -> 83.1 us  [the longest x2 64.2 us: on_device(): lax.all_gather(pack(h * size, size, pool, (shared_gate, shared_up, shared...]
    all_to_all x0 -> x2, waiting for transfers between devices: none -> 30.5 us  [trade(): lax.all_to_all(field.reshape(owners, local_experts, batch * CAP, width),...]
    convert_element_type x18 -> x2, other arithmetic: 19.4 us -> 1.72 us  [over_owners(): field = field.astype(BF16) if k < owners else field]
    squeeze x13 -> x0, local copies, waits for them, and re-layouts: 15.3 us -> none  [the longest x4 8.79 us: scatter_rows(): came = send(take(blocks, 1 - core, 1), core_step)]
  transfers between devices with their start and end apart: 87 -> 12, of which waited for: 30 -> 8; matrix products, arithmetic and copies ran while one was open for 6% -> 1% of each run, Pallas kernels for 26% -> 29%
where the time goes in v2:
time: 864 us; the launch traced here: 856 us
  waiting for transfers between devices  359 us (42%)
  Pallas kernels  251 us (29%)
  blocking collectives  193 us (22%)
  local copies, waits for them, and re-layouts  16.6 us (2%)
  starting transfers between devices  16.3 us (2%)
  between operations  14.5 us (2%)
    all_to_all x2, blocking collectives, on_device(): lax.all_to_all(results, 'expert', 0, 0)  184 us
    pallas_call x3, Pallas kernels, feed(): pl.pallas_call(skipping(functools.partial(feed_kernel, gated, packed), in...  147 us
    reduce_scatter x2, waiting for transfers between devices, on_device(): lax.psum_scatter(tie(field[0], *mine[-1:]), 'dp', scatter_dimension=0)  130 us
    ppermute x4, waiting for transfers between devices, over_owners(): came = lax.ppermute(field, 'expert', [(i, i ^ k) for i in range(owners)])  65 us
    all_gather x2, waiting for transfers between devices, on_device(): lax.all_gather(pack(h * size, size, pool, (shared_gate, shared_up, shared...  64.2 us
    pallas_call x1, Pallas kernels, on_device(): pl.pallas_call(functools.partial(backward_kernel, experts, groups), grid=...  51.4 us
    reduce_scatter x1, waiting for transfers between devices, on_device(): lax.psum_scatter(first_grad, 'dp', scatter_dimension=0, tiled=True)  49.7 us
    pallas_call x1, Pallas kernels, on_device(): pl.pallas_call(functools.partial(forward_kernel, experts), grid=(batch,),...  31.3 us
  transfers between devices with their start and end apart: 12, of which 8 were waited for; matrix products, arithmetic and copies ran while one was open for 1% of the time, Pallas kernels for 29%

profile of v2, /device:TPU:0, one launch (start us, length us, event | category | flops | bytes accessed | tf_op | source)
XLA Modules:
  0.0 855.9 jit_solution(13447358518738607245)
XLA Ops:
  9.6 2.0 concatenate.6
  11.6 4.2 pack.2
  15.9 2.9 pack.3
  20.7 4.9 dispatch.1
  25.7 6.5 all-to-all-start.1
  35.1 18.9 %all-gather.6.cloned.1.call-done.weight_ref = bf16[768,3200]{1,0:T(8,128)(2,1)} async-done(((bf16[96,3200]{1,0:T(8,128)(2,1)}), bf16[768,3200]{1,0:T(8,128)(2,1)}) %all-gather.6.cloned.1.call-update) | async-done | bytes 4915216 | tf_op jit(solution)/shard_map/all_gather | solution.py:447
  54.1 1.0 slice_convert_fusion
  55.9 31.3 %attention.1 = (f32[4,256,768]{2,1,0:T(8,128)}, bf16[4,256,768]{2,1,0:T(8,128)(2,1)}, bf16[4,256,768]{2,1,0:T(8,128)(2,1)}, bf16[4,256,2304]{2,1,0:T(8,128)(2,1)...) custom-call(bf16[4,256,768]{2,1,0:T(8,128)(2,1)} %bitcast.67, ...), custom_call_target="tpu_custom_call" | custom-call | flops 7650410496 | bytes 20643840 | tf_op jit(solution)/shard_map/attention/pallas_call | solution.py:515
  87.2 1.2 copy.107
  89.4 30.5 %all-to-all-done.1.refs_1_ = bf16[4,4,160,768]{3,2,1,0:T(8,128)(2,1)} async-done(((bf16[4,4,160,768]{3,2,1,0:T(8,128)(2,1)}), bf16[4,4,160,768]{3,2,1,0:T(8,128)(2,1)}, u32[]{:S(2)}, u32[]{:S(2)}) %all-to-all-start.1) | async-done | bytes 3932192 | tf_op jit(solution)/shard_map/all_to_all | solution.py:469
  119.9 8.6 %all_to_all.25.refs_2_ = f32[4,4,1,160]{3,2,1,0:T(1,128)} all-to-all(f32[4,4,1,160]{3,2,1,0:T(1,128)S(1)} %reshape.135), channel_id=1, replica_groups=mesh['dp'=8,'expert'=4] {'expert'}, dimensions={0} | all-to-all | bytes 20480 | tf_op jit(solution)/shard_map/all_to_all | solution.py:537
  128.5 4.8 all-to-all-start
  133.4 61.1 %all-gather.8.cloned.1.call-done = bf16[24,3,2,768,128]{4,3,2,1,0:T(8,128)(2,1)} async-done(((bf16[3,3,2,768,128]{4,3,2,1,0:T(8,128)(2,1)}), bf16[24,3,2,768,128]{4,3,2,1,0:T(8,128)(2,1)}) %all-gather.8.cloned.1.call-update) | async-done | bytes 28311568 | tf_op jit(solution)/shard_map/all_gather | solution.py:450
  194.5 48.5 %shared.1 = (f32[1,1,1024,768]{3,2,1,0:T(8,128)}, f32[1,1,1024,768]{3,2,1,0:T(8,128)}, bf16[8,3,3,2,768,128]{5,4,3,2,1,0:T(8,128)(2,1)}) custom-call(bf16[1,1,1024,768]{3,2,1,0:T(8,128)(2,1)} %bitcast.76, bf16[1,1,1024,768]{3,2,1,0:T(8,128)(2,1)} %bitcast.54, bf16[8,3,3,2,768,128]{5,4,3,2,1,0:T(8,128)(2,1)} %bitcast.64), custom_call_target="tpu_custom_call" | custom-call | flops 28991029248 | bytes 25165824 | tf_op jit(solution)/shard_map/shared/pallas_call | solution.py:407
  243.0 49.3 %experts.2 = (bf16[4,2,2,160,768]{4,3,2,1,0:T(8,128)(2,1)}, bf16[8,3,3,2,768,128]{5,4,3,2,1,0:T(8,128)(2,1)}) custom-call(bf16[4,4,160,768]{3,2,1,0:T(8,128)(2,1)} %all-to-all-done.refs_0_, bf16[4,4,160,768]{3,2,1,0:T(8,128)(2,1)} %all-to-all-done.1.refs_1_, f32[4,4,1,160]{3,2,1,0:T(1,128)} %all_to_all.25.refs_2_, ...), custom_call_target="tpu_custom_call", output_to_operand_aliasing={{1}: (4, {})} | custom-call | flops 36238786560 | bytes 45613056 | tf_op jit(solution)/shard_map/experts/pallas_call | solution.py:407
  292.4 3.1 all-gather.10.cloned.1.call-done
  295.6 48.7 %experts.3 = (bf16[4,2,2,160,768]{4,3,2,1,0:T(8,128)(2,1)}, bf16[8,2,3,2,768,128]{5,4,3,2,1,0:T(8,128)(2,1)}) custom-call(bf16[4,4,160,768]{3,2,1,0:T(8,128)(2,1)} %all-to-all-done.refs_0_, bf16[4,4,160,768]{3,2,1,0:T(8,128)(2,1)} %all-to-all-done.1.refs_1_, f32[4,4,1,160]{3,2,1,0:T(1,128)} %all_to_all.25.refs_2_, bf16[8,2,3,2,768,128]{5,4,3,2,1,0:T(8,128)(2,1)} %bitcast.66, ...), custom_call_target="tpu_custom_call" | custom-call | flops 36238786560 | bytes 45613056 | tf_op jit(solution)/shard_map/experts/pallas_call | solution.py:407
  344.3 130.3 %reduce-scatter.4.cloned.1.call-done = bf16[1,3,3,2,768,128]{5,4,3,2,1,0:T(8,128)(2,1)} async-done(((bf16[8,3,3,2,768,128]{5,4,3,2,1,0:T(8,128)(2,1)}), bf16[1,3,3,2,768,128]{5,4,3,2,1,0:T(8,128)(2,1)}) %reduce-scatter.4.cloned.1.call-update) | async-done | bytes 3538960 | tf_op jit(solution)/shard_map/reduce_scatter | solution.py:594
  474.6 93.5 %all_to_all.26 = bf16[4,2,2,160,768]{4,3,2,1,0:T(8,128)(2,1)} all-to-all(bf16[4,2,2,160,768]{4,3,2,1,0:T(8,128)(2,1)} %get-tuple-element.48.refs_4_), channel_id=1, replica_groups=mesh['dp'=8,'expert'=4] {'expert'}, dimensions={0} | all-to-all | bytes 7864320 | tf_op jit(solution)/shard_map/all_to_all | solution.py:548
  568.1 90.6 %all_to_all.27 = bf16[4,2,2,160,768]{4,3,2,1,0:T(8,128)(2,1)} all-to-all(bf16[4,2,2,160,768]{4,3,2,1,0:T(8,128)(2,1)S(1)} %copy-done.2), channel_id=1, replica_groups=mesh['dp'=8,'expert'=4] {'expert'}, dimensions={0} | all-to-all | bytes 7864320 | tf_op jit(solution)/shard_map/all_to_all | solution.py:548
  658.7 51.4 %attention_back.1 = (bf16[4,256,768]{2,1,0:T(8,128)(2,1)}, f32[4,256,768]{2,1,0:T(8,128)}, bf16[768,3200]{1,0:T(8,128)(2,1)}) custom-call(bf16[4,256,768]{2,1,0:T(8,128)(2,1)} %bitcast.68, bf16[4,256,768]{2,1,0:T(8,128)(2,1)} %bitcast.55, s32[4,256,1]{2,1,0:T(8,128)} %broadcast_in_dim_reshape.5.column_ref, s32[4,1,256]{2,1,0:T(1,128)} %row_ref.3, ...), custom_call_target="tpu_custom_call" | custom-call | flops 15300820992 | bytes 34996224 | tf_op jit(solution)/shard_map/attention_back/pallas_call | solution.py:551
  710.2 2.0 copy-done
  712.2 1.1 slice_bitcast_fusion
  713.5 49.7 %reduce-scatter.8.cloned.1.call-done = bf16[96,3200]{1,0:T(8,128)(2,1)} async-done(((bf16[768,3200]{1,0:T(8,128)(2,1)}), bf16[96,3200]{1,0:T(8,128)(2,1)}) %reduce-scatter.8.cloned.1.call-update) | async-done | bytes 614416 | tf_op jit(solution)/shard_map/reduce_scatter | solution.py:609
  763.3 1.5 collective-permute-start
  764.8 1.6 add_convert_fusion
  766.3 2.5 collective-permute-start.3
  768.8 21.6 %collective-permute-done = bf16[96,3200]{1,0:T(8,128)(2,1)S(1)} collective-permute-done((bf16[96,3200]{1,0:T(8,128)(2,1)}, bf16[96,3200]{1,0:T(8,128)(2,1)S(1)}, u32[]{:S(2)}, u32[]{:S(2)}) %collective-permute-start) | collective-permute-done | bytes 614432 | tf_op jit(solution)/shard_map/ppermute | solution.py:584
  791.2 43.4 %collective-permute-done.3 = bf16[1,3,2,768,128]{4,3,2,1,0:T(8,128)(2,1)S(1)} collective-permute-done((bf16[1,3,2,768,128]{4,3,2,1,0:T(8,128)(2,1)S(1)}, bf16[1,3,2,768,128]{4,3,2,1,0:T(8,128)(2,1)S(1)}, u32[]{:S(2)}, u32[]{:S(2)}) %collective-permute-start.3) | collective-permute-done | bytes 1179680 | tf_op jit(solution)/shard_map/ppermute | solution.py:584
  834.6 1.6 convert_add_fusion.refs_0_
  836.2 3.1 unpack_shared.1
  839.4 7.0 unpack_experts.1
  (67 shorter events, 12.9 us)
Async XLA Ops:
  7.2 46.9 %all-gather.6.cloned.1.call-start = ((), (), s32[]{:S(2)}) async-start(), calls=%async_computation.8 | async-start | bytes 5529600 | tf_op jit(solution)/shard_map/all_gather | solution.py:447
  11.6 182.9 %all-gather.8.cloned.1.call-start = ((), (), s32[]{:S(2)}) async-start(), calls=%async_computation.12 | async-start | bytes 31850496 | tf_op jit(solution)/shard_map/all_gather | solution.py:450
  15.8 279.7 %all-gather.10.cloned.1.call-start = ((), (), s32[]{:S(2)}) async-start(), calls=%async_computation.13 | async-start | bytes 21233664 | tf_op jit(solution)/shard_map/all_gather | solution.py:450
  18.7 0.7 copy-start.5
  18.7 0.9 copy-start.6
  19.9 15.0 %copy-start.1 = (s32[4,1,256,2]{3,2,0,1:T(8,128)}, s32[4,1,256,2]{3,2,0,1:T(8,128)S(1)}, u32[]{:S(2)}) copy-start(s32[4,1,256,2]{3,2,0,1:T(8,128)S(1)} %copy.94) | copy-start | bytes 24580
  25.7 6.5 copy-start.7
  25.7 94.2 %all-to-all-start.1 = ((bf16[4,4,160,768]{3,2,1,0:T(8,128)(2,1)}), bf16[4,4,160,768]{3,2,1,0:T(8,128)(2,1)}, u32[]{:S(2)}, u32[]{:S(2)}) async-start(bf16[4,4,160,768]{3,2,1,0:T(8,128)(2,1)} %bitcast.45), calls=%async_computation.1 | async-start | bytes 7864320 | tf_op jit(solution)/shard_map/all_to_all | solution.py:469
  55.8 32.6 %copy-start.4 = (s32[4,2,256]{2,1,0:T(2,128)S(1)}, s32[4,2,256]{2,1,0:T(2,128)}, u32[]{:S(2)}) copy-start(s32[4,2,256]{2,1,0:T(2,128)} %copy.110.flat_ref) | copy-start | bytes 24580
  128.5 114.5 %all-to-all-start = ((bf16[4,4,160,768]{3,2,1,0:T(8,128)(2,1)}), bf16[4,4,160,768]{3,2,1,0:T(8,128)(2,1)}, u32[]{:S(2)}, u32[]{:S(2)}) async-start(bf16[4,4,160,768]{3,2,1,0:T(8,128)(2,1)} %bitcast.50), calls=%async_computation | async-start | bytes 7864320 | tf_op jit(solution)/shard_map/all_to_all | solution.py:469
  133.3 341.2 %reduce-scatter.4.cloned.1.call-start = ((), (), s32[]{:S(2)}) async-start(), calls=%async_computation.9 | async-start | bytes 31850496 | tf_op jit(solution)/shard_map/reduce_scatter | solution.py:594
  292.4 417.8 %reduce-scatter.6.cloned.1.call-start = ((), (), s32[]{:S(2)}) async-start(), calls=%async_computation.10 | async-start | bytes 21233664 | tf_op jit(solution)/shard_map/reduce_scatter | solution.py:594
  474.6 288.7 %reduce-scatter.8.cloned.1.call-start = ((), (), s32[]{:S(2)}) async-start(), calls=%async_computation.11 | async-start | bytes 5529600 | tf_op jit(solution)/shard_map/reduce_scatter | solution.py:609
  474.6 93.5 %copy-start.2 = (bf16[4,2,2,160,768]{4,3,2,1,0:T(8,128)(2,1)S(1)}, bf16[4,2,2,160,768]{4,3,2,1,0:T(8,128)(2,1)}, u32[]{:S(2)}) copy-start(bf16[4,2,2,160,768]{4,3,2,1,0:T(8,128)(2,1)} %get-tuple-element.49) | copy-start | bytes 11796484
  710.2 2.0 copy-start
  713.3 51.5 %collective-permute-start.2 = (bf16[1,3,2,768,128]{4,3,2,1,0:T(8,128)(2,1)}, bf16[1,3,2,768,128]{4,3,2,1,0:T(8,128)(2,1)}, u32[]{:S(2)}, u32[]{:S(2)}) collective-permute-start(bf16[1,3,2,768,128]{4,3,2,1,0:T(8,128)(2,1)} %slice_bitcast_fusion), channel_id=1, source_target_pairs={{0,1},{1,0},{2,3},{3,2},{4,5},{5,4},{6,7},{7,6},{8,9},{9,8},{10,11... | collective-permute-start | bytes 3538952 | tf_op jit(solution)/shard_map/ppermute | solution.py:584
  763.3 27.2 %copy-start.3 = (bf16[96,3200]{1,0:T(8,128)(2,1)S(1)}, bf16[96,3200]{1,0:T(8,128)(2,1)}, u32[]{:S(2)}) copy-start(bf16[96,3200]{1,0:T(8,128)(2,1)} %reduce-scatter.8.cloned.1.call-done) | copy-start | bytes 1843204
  763.3 27.2 %collective-permute-start = (bf16[96,3200]{1,0:T(8,128)(2,1)}, bf16[96,3200]{1,0:T(8,128)(2,1)S(1)}, u32[]{:S(2)}, u32[]{:S(2)}) collective-permute-start(bf16[96,3200]{1,0:T(8,128)(2,1)} %reduce-scatter.8.cloned.1.call-done), channel_id=1, source_target_pairs={{0,1},{1,0},{2,3},{3,2},{4,5},{5,4},{6,7},{7,6},{8,9},{9,8},{10,11... | collective-permute-start | bytes 1843208 | tf_op jit(solution)/shard_map/ppermute | solution.py:584
  766.3 68.3 %collective-permute-start.3 = (bf16[1,3,2,768,128]{4,3,2,1,0:T(8,128)(2,1)S(1)}, bf16[1,3,2,768,128]{4,3,2,1,0:T(8,128)(2,1)S(1)}, u32[]{:S(2)}, u32[]{:S(2)}) collective-permute-start(bf16[1,3,2,768,128]{4,3,2,1,0:T(8,128)(2,1)S(1)} %add_convert_fusion), channel_id=1, source_target_pairs={{0,2},{1,3},{2,0},{3,1},{4,6},{5,7},{6,4},{7,5},{8,10},{9,11},{10,... | collective-permute-start | bytes 3538952 | tf_op jit(solution)/shard_map/ppermute | solution.py:584
  790.6 55.8 %collective-permute-start.1 = (bf16[96,3200]{1,0:T(8,128)(2,1)S(1)}, bf16[96,3200]{1,0:T(8,128)(2,1)S(1)}, u32[]{:S(2)}, u32[]{:S(2)}) collective-permute-start(bf16[96,3200]{1,0:T(8,128)(2,1)S(1)} %add_convert_fusion.1), channel_id=1, source_target_pairs={{0,2},{1,3},{2,0},{3,1},{4,6},{5,7},{6,4},{7,5},{8,10},{9,11},{10,... | collective-permute-start | bytes 1843208 | tf_op jit(solution)/shard_map/ppermute | solution.py:584
Sparse Core Ops, SparseCore 0:
  11.7 42.3 all-gather.5
  55.9 138.4 all-gather.7
  196.9 98.5 all-gather.9
  299.1 175.3 reduce-scatter.3
  478.0 126.4 reduce-scatter.5
  710.4 52.8 reduce-scatter.7

commit v3 on v2

--- a/solution.py
+++ b/solution.py
@@ -42,6 +42,43 @@
         input_output_aliases={0: 0},
         name="tie",
     )(field, *after)
+
+
+def first_step(i):
+    return i ^ (2 if i % 2 == 0 else 4)
+
+
+def second_step(i):
+    return i ^ (4 if i % 2 == 0 else 2)
+
+
+def core_step(i):
+    return i ^ 1
+
+
+def send(field, step):
+    return lax.ppermute(field, "dp", [(i, step(i)) for i in range(8)])
+
+
+def scatter_rows(field):
+    count = lax.axis_size("dp")
+    if count != 8:
+        return lax.psum_scatter(field, "dp", scatter_dimension=0, tiled=False)
+    index = lax.axis_index("dp")
+    core, x, y = index % 2, (index // 2) % 2, index // 4
+    take = functools.partial(lax.dynamic_index_in_dim, keepdims=False)
+    blocks = field.reshape((4, 2) + field.shape[1:])
+    came = send(take(blocks, 1 - core, 1), core_step)
+    total = (take(blocks, core, 1).astype(F32) + came.astype(F32)).astype(BF16)
+    one, two = jnp.where(core == 0, x, y), jnp.where(core == 0, y, x)
+
+    def at(first, second):
+        return take(total, jnp.where(core == 0, second * 2 + first, first * 2 + second), 0)
+
+    came = send(jnp.stack([at(1 - one, two), at(1 - one, 1 - two)]), first_step).astype(F32)
+    keep = (at(one, two).astype(F32) + came[0]).astype(BF16)
+    pass_on = (at(one, 1 - two).astype(F32) + came[1]).astype(BF16)
+    return (keep.astype(F32) + send(pass_on, second_step).astype(F32)).astype(BF16)
 
 
 def place_of(flat, rows):
@@ -591,11 +628,12 @@
     if packed:
         mine = []
         for field in sums:
-            mine.append(lax.psum_scatter(tie(field[0], *mine[-1:]), "dp", scatter_dimension=0))
-        first_grad = tie(first_grad, mine[-1])
+            field = tie(field[0], *mine, *backs) if mine else field[0]
+            mine.append(lax.psum_scatter(field, "dp", scatter_dimension=0))
         pool_mine = unpack(mine, [size] * groups, width // devices, units, "unpack_experts")
         shared_mine = unpack(
             [over_owners(mine[0][size:])], [1], width // devices, units, "unpack_shared")
+        first_grad = tie(first_grad, shared_mine[0])
         shared_mine = [field[0] for field in shared_mine]
     else:
         def scatter(both, down):
@@ -606,7 +644,7 @@
         pool_mine = [both[:, 0], both[:, 1], down]
         both, down = (over_owners(field[0]) for field in scatter(*shared_sums))
         shared_mine = [both[0], both[1], down]
-    first_mine = over_owners(lax.psum_scatter(first_grad, "dp", scatter_dimension=0, tiled=True))
+    first_mine = over_owners(scatter_rows(first_grad.reshape(devices, width // devices, columns)))
     return (
         layer_out.reshape(tokens.shape),
         grad_tokens.reshape(tokens.shape),

time: 864 us -> 700 us (0.81)
  blocking collectives: 193 us -> 102 us
  waiting for transfers between devices: 359 us -> 272 us
  Pallas kernels: 251 us -> 239 us
  starting transfers between devices: 16.3 us -> 27.5 us
  other arithmetic: 5.56 us -> 16.3 us
    reduce_scatter x3 -> x2, waiting for transfers between devices: 180 us -> 8.22 us  [on_device(): mine.append(lax.psum_scatter(field, 'dp', scatter_dimension=0))]
    all_to_all x2 -> x1, blocking collectives: 184 us -> 93.2 us  [on_device(): lax.all_to_all(results, 'expert', 0, 0)]
    ppermute x0 -> x3, waiting for transfers between devices: none -> 48 us  [send(): return lax.ppermute(field, 'dp', [(i, step(i)) for i in range(8)])]
    all_to_all x0 -> x1, waiting for transfers between devices: none -> 28.9 us  [on_device(): lax.all_to_all(results, 'expert', 0, 0)]
    pallas_call x3, Pallas kernels: 147 us -> 134 us  [feed(): pl.pallas_call(skipping(functools.partial(feed_kernel, gated, packed), in...]
  transfers between devices with their start and end apart: 12 -> 15, of which waited for: 8 -> 12; matrix products, arithmetic and copies ran while one was open for 1% -> 4% of each run, Pallas kernels for 29% -> 34%
where the time goes in v3:
time: 700 us; the launch traced here: 691 us
  waiting for transfers between devices  272 us (39%)
  Pallas kernels  239 us (34%)
  blocking collectives  102 us (15%)
  starting transfers between devices  27.5 us (4%)
  local copies, waits for them, and re-layouts  19.5 us (3%)
  other arithmetic  16.3 us (2%)
  between operations  14.3 us (2%)
    pallas_call x3, Pallas kernels, feed(): pl.pallas_call(skipping(functools.partial(feed_kernel, gated, packed), in...  134 us
    all_to_all x1, blocking collectives, on_device(): lax.all_to_all(results, 'expert', 0, 0)  93.2 us
    all_gather x2, waiting for transfers between devices, on_device(): lax.all_gather(pack(h * size, size, pool, (shared_gate, shared_up, shared...  71.8 us
    ppermute x4, waiting for transfers between devices, over_owners(): came = lax.ppermute(field, 'expert', [(i, i ^ k) for i in range(owners)])  65.7 us
    pallas_call x1, Pallas kernels, on_device(): pl.pallas_call(functools.partial(backward_kernel, experts, groups), grid=...  51.6 us
    ppermute x3, waiting for transfers between devices, send(): return lax.ppermute(field, 'dp', [(i, step(i)) for i in range(8)])  48 us
    pallas_call x1, Pallas kernels, on_device(): pl.pallas_call(functools.partial(forward_kernel, experts), grid=(batch,),...  31.3 us
    all_to_all x2, waiting for transfers between devices, trade(): lax.all_to_all(field.reshape(owners, local_experts, batch * CAP, width),...  30.4 us
  transfers between devices with their start and end apart: 15, of which 12 were waited for; matrix products, arithmetic and copies ran while one was open for 4% of the time, Pallas kernels for 34%

profile of v3, /device:TPU:0, one launch (start us, length us, event | category | flops | bytes accessed | tf_op | source)
XLA Modules:
  0.0 691.0 jit_solution(6927828064894798117)
XLA Ops:
  11.6 4.2 pack.2
  15.9 2.9 pack.3
  20.6 4.9 dispatch.1
  25.5 6.5 all-to-all-start.1
  35.0 19.1 %all-gather.6.cloned.1.call-done.weight_ref = bf16[768,3200]{1,0:T(8,128)(2,1)} async-done(((bf16[96,3200]{1,0:T(8,128)(2,1)}), bf16[768,3200]{1,0:T(8,128)(2,1)}) %all-gather.6.cloned.1.call-update) | async-done | bytes 4915216 | tf_op jit(solution)/shard_map/all_gather | solution.py:484
  55.8 31.3 %attention.1 = (f32[4,256,768]{2,1,0:T(8,128)}, bf16[4,256,768]{2,1,0:T(8,128)(2,1)}, bf16[4,256,768]{2,1,0:T(8,128)(2,1)}, bf16[4,256,2304]{2,1,0:T(8,128)(2,1)...) custom-call(bf16[4,256,768]{2,1,0:T(8,128)(2,1)} %bitcast.84, ...), custom_call_target="tpu_custom_call" | custom-call | flops 7650410496 | bytes 20643840 | tf_op jit(solution)/shard_map/attention/pallas_call | solution.py:552
  89.4 30.4 %all-to-all-done.1.refs_1_ = bf16[4,4,160,768]{3,2,1,0:T(8,128)(2,1)} async-done(((bf16[4,4,160,768]{3,2,1,0:T(8,128)(2,1)}), bf16[4,4,160,768]{3,2,1,0:T(8,128)(2,1)}, u32[]{:S(2)}, u32[]{:S(2)}) %all-to-all-start.1) | async-done | bytes 3932192 | tf_op jit(solution)/shard_map/all_to_all | solution.py:506
  119.8 8.6 %all_to_all.25.refs_2_ = f32[4,4,1,160]{3,2,1,0:T(1,128)} all-to-all(f32[4,4,1,160]{3,2,1,0:T(1,128)S(1)} %reshape.145), channel_id=1, replica_groups=mesh['dp'=8,'expert'=4] {'expert'}, dimensions={0} | all-to-all | bytes 20480 | tf_op jit(solution)/shard_map/all_to_all | solution.py:574
  128.4 4.8 all-to-all-start
  133.3 61.2 %all-gather.8.cloned.1.call-done = bf16[24,3,2,768,128]{4,3,2,1,0:T(8,128)(2,1)} async-done(((bf16[3,3,2,768,128]{4,3,2,1,0:T(8,128)(2,1)}), bf16[24,3,2,768,128]{4,3,2,1,0:T(8,128)(2,1)}) %all-gather.8.cloned.1.call-update) | async-done | bytes 28311568 | tf_op jit(solution)/shard_map/all_gather | solution.py:487
  194.5 37.2 %shared.1 = (f32[1,1,1024,768]{3,2,1,0:T(8,128)}, f32[1,1,1024,768]{3,2,1,0:T(8,128)}, bf16[8,3,3,2,768,128]{5,4,3,2,1,0:T(8,128)(2,1)}) custom-call(bf16[1,1,1024,768]{3,2,1,0:T(8,128)(2,1)} %bitcast.92, bf16[1,1,1024,768]{3,2,1,0:T(8,128)(2,1)} %bitcast.70, bf16[8,3,3,2,768,128]{5,4,3,2,1,0:T(8,128)(2,1)} %bitcast.81), custom_call_target="tpu_custom_call" | custom-call | flops 28991029248 | bytes 25165824 | tf_op jit(solution)/shard_map/shared/pallas_call | solution.py:444
  231.7 48.3 %experts.2 = (bf16[4,2,2,160,768]{4,3,2,1,0:T(8,128)(2,1)}, bf16[8,3,3,2,768,128]{5,4,3,2,1,0:T(8,128)(2,1)}) custom-call(bf16[4,4,160,768]{3,2,1,0:T(8,128)(2,1)} %all-to-all-done.refs_0_, bf16[4,4,160,768]{3,2,1,0:T(8,128)(2,1)} %all-to-all-done.1.refs_1_, f32[4,4,1,160]{3,2,1,0:T(1,128)} %all_to_all.25.refs_2_, ...), custom_call_target="tpu_custom_call", output_to_operand_aliasing={{1}: (4, {})} | custom-call | flops 36238786560 | bytes 45613056 | tf_op jit(solution)/shard_map/experts/pallas_call | solution.py:444
  280.0 4.8 all-to-all-start.3
  284.9 10.6 %all-gather.10.cloned.1.call-done = bf16[16,3,2,768,128]{4,3,2,1,0:T(8,128)(2,1)} async-done(((bf16[2,3,2,768,128]{4,3,2,1,0:T(8,128)(2,1)}), bf16[16,3,2,768,128]{4,3,2,1,0:T(8,128)(2,1)}) %all-gather.10.cloned.1.call-update) | async-done | bytes 18874384 | tf_op jit(solution)/shard_map/all_gather | solution.py:487
  295.6 48.7 %experts.3 = (bf16[4,2,2,160,768]{4,3,2,1,0:T(8,128)(2,1)}, bf16[8,2,3,2,768,128]{5,4,3,2,1,0:T(8,128)(2,1)}) custom-call(bf16[4,4,160,768]{3,2,1,0:T(8,128)(2,1)} %all-to-all-done.refs_0_, bf16[4,4,160,768]{3,2,1,0:T(8,128)(2,1)} %all-to-all-done.1.refs_1_, f32[4,4,1,160]{3,2,1,0:T(1,128)} %all_to_all.25.refs_2_, bf16[8,2,3,2,768,128]{5,4,3,2,1,0:T(8,128)(2,1)} %bitcast.83, ...), custom_call_target="tpu_custom_call" | custom-call | flops 36238786560 | bytes 45613056 | tf_op jit(solution)/shard_map/experts/pallas_call | solution.py:444
  344.3 28.9 %all-to-all-done.3 = bf16[4,2,2,160,768]{4,3,2,1,0:T(8,128)(2,1)} async-done(((bf16[4,2,2,160,768]{4,3,2,1,0:T(8,128)(2,1)}), bf16[4,2,2,160,768]{4,3,2,1,0:T(8,128)(2,1)}, u32[]{:S(2)}, u32[]{:S(2)}) %all-to-all-start.3) | async-done | bytes 3932192 | tf_op jit(solution)/shard_map/all_to_all | solution.py:585
  373.1 93.2 %all_to_all.26 = bf16[4,2,2,160,768]{4,3,2,1,0:T(8,128)(2,1)} all-to-all(bf16[4,2,2,160,768]{4,3,2,1,0:T(8,128)(2,1)} %get-tuple-element.49), channel_id=1, replica_groups=mesh['dp'=8,'expert'=4] {'expert'}, dimensions={0} | all-to-all | bytes 7864320 | tf_op jit(solution)/shard_map/all_to_all | solution.py:585
  466.3 8.2 %reduce-scatter.3.cloned.1.call-done = bf16[1,3,3,2,768,128]{5,4,3,2,1,0:T(8,128)(2,1)} async-done(((bf16[8,3,3,2,768,128]{5,4,3,2,1,0:T(8,128)(2,1)}), bf16[1,3,3,2,768,128]{5,4,3,2,1,0:T(8,128)(2,1)}) %reduce-scatter.3.cloned.1.call-update) | async-done | bytes 3538960 | tf_op jit(solution)/shard_map/reduce_scatter | solution.py:632
  479.1 26.4 %collective-permute-done = bf16[1,3,2,768,128]{4,3,2,1,0:T(8,128)(2,1)} collective-permute-done((bf16[1,3,2,768,128]{4,3,2,1,0:T(8,128)(2,1)}, bf16[1,3,2,768,128]{4,3,2,1,0:T(8,128)(2,1)}, u32[]{:S(2)}, u32[]{:S(2)}) %collective-permute-start) | collective-permute-done | bytes 1179680 | tf_op jit(solution)/shard_map/ppermute | solution.py:621
  505.5 2.7 add_convert_fusion
  508.2 2.5 collective-permute-start.1
  510.7 51.6 %attention_back.1 = (bf16[4,256,768]{2,1,0:T(8,128)(2,1)}, f32[4,256,768]{2,1,0:T(8,128)}, bf16[768,3200]{1,0:T(8,128)(2,1)}) custom-call(bf16[4,256,768]{2,1,0:T(8,128)(2,1)} %bitcast.85, bf16[4,256,768]{2,1,0:T(8,128)(2,1)} %bitcast.71, s32[4,256,1]{2,1,0:T(8,128)} %broadcast_in_dim_reshape.5.column_ref, s32[4,1,256]{2,1,0:T(1,128)} %row_ref.3, ...), custom_call_target="tpu_custom_call" | custom-call | flops 15300820992 | bytes 34996224 | tf_op jit(solution)/shard_map/attention_back/pallas_call | solution.py:588
  562.3 2.9 convert_add_fusion.1.refs_0_
  565.2 3.1 unpack_shared.1
  570.4 4.7 collective-permute-done.2
  575.1 3.5 fusion
  581.7 34.4 %collective-permute-done.3 = bf16[2,96,3200]{2,1,0:T(8,128)(2,1)} collective-permute-done((bf16[2,96,3200]{2,1,0:T(8,128)(2,1)S(1)}, bf16[2,96,3200]{2,1,0:T(8,128)(2,1)}, u32[]{:S(2)}, u32[]{:S(2)}) %collective-permute-start.3) | collective-permute-done | bytes 1228832 | tf_op jit(solution)/shard_map/ppermute | solution.py:60
  621.1 8.9 %collective-permute-done.4 = bf16[96,3200]{1,0:T(8,128)(2,1)S(1)} collective-permute-done((bf16[96,3200]{1,0:T(8,128)(2,1)}, bf16[96,3200]{1,0:T(8,128)(2,1)S(1)}, u32[]{:S(2)}, u32[]{:S(2)}) %collective-permute-start.4) | collective-permute-done | bytes 614432 | tf_op jit(solution)/shard_map/ppermute | solution.py:60
  632.7 13.5 %collective-permute-done.5 = bf16[96,3200]{1,0:T(8,128)(2,1)S(1)} collective-permute-done((bf16[96,3200]{1,0:T(8,128)(2,1)S(1)}, bf16[96,3200]{1,0:T(8,128)(2,1)S(1)}, u32[]{:S(2)}, u32[]{:S(2)}) %collective-permute-start.5) | collective-permute-done | bytes 614432 | tf_op jit(solution)/shard_map/ppermute | solution.py:621
  646.4 2.5 collective-permute-start.6
  648.9 25.8 %collective-permute-done.6 = bf16[96,3200]{1,0:T(8,128)(2,1)S(1)} collective-permute-done((bf16[96,3200]{1,0:T(8,128)(2,1)S(1)}, bf16[96,3200]{1,0:T(8,128)(2,1)S(1)}, u32[]{:S(2)}, u32[]{:S(2)}) %collective-permute-start.6) | collective-permute-done | bytes 614432 | tf_op jit(solution)/shard_map/ppermute | solution.py:621
  677.2 7.0 %unpack_experts.1 = (f32[4,96,2048]{2,1,0:T(8,128)}, f32[4,96,2048]{2,1,0:T(8,128)}, f32[4,256,768]{2,1,0:T(8,128)}) custom-call(bf16[3,3,2,768,128]{4,3,2,1,0:T(8,128)(2,1)} %bitcast.59, bf16[2,3,2,768,128]{4,3,2,1,0:T(8,128)(2,1)} %bitcast.68), custom_call_target="tpu_custom_call" | custom-call | tf_op jit(solution)/shard_map/unpack_experts/pallas_call | solution.py:325
  (75 shorter events, 33.3 us)
Async XLA Ops:
  7.2 46.9 %all-gather.6.cloned.1.call-start = ((), (), s32[]{:S(2)}) async-start(), calls=%async_computation.7 | async-start | bytes 5529600 | tf_op jit(solution)/shard_map/all_gather | solution.py:484
  11.6 182.9 %all-gather.8.cloned.1.call-start = ((), (), s32[]{:S(2)}) async-start(), calls=%async_computation.10 | async-start | bytes 31850496 | tf_op jit(solution)/shard_map/all_gather | solution.py:487
  15.9 3.0 copy-start.4
  15.9 279.7 %all-gather.10.cloned.1.call-start = ((), (), s32[]{:S(2)}) async-start(), calls=%async_computation.11 | async-start | bytes 21233664 | tf_op jit(solution)/shard_map/all_gather | solution.py:487
  18.8 0.7 copy-start.5
  19.7 15.1 %copy-start.2 = (s32[4,1,256,2]{3,2,0,1:T(8,128)}, s32[4,1,256,2]{3,2,0,1:T(8,128)S(1)}, u32[]{:S(2)}) copy-start(s32[4,1,256,2]{3,2,0,1:T(8,128)S(1)} %copy.125) | copy-start | bytes 24580
  25.5 6.5 copy-start.6
  25.5 94.3 %all-to-all-start.1 = ((bf16[4,4,160,768]{3,2,1,0:T(8,128)(2,1)}), bf16[4,4,160,768]{3,2,1,0:T(8,128)(2,1)}, u32[]{:S(2)}, u32[]{:S(2)}) async-start(bf16[4,4,160,768]{3,2,1,0:T(8,128)(2,1)} %bitcast.64), calls=%async_computation.1 | async-start | bytes 7864320 | tf_op jit(solution)/shard_map/all_to_all | solution.py:506
  55.8 32.6 %copy-start.3 = (s32[4,2,256]{2,1,0:T(2,128)S(1)}, s32[4,2,256]{2,1,0:T(2,128)}, u32[]{:S(2)}) copy-start(s32[4,2,256]{2,1,0:T(2,128)} %copy.141.flat_ref) | copy-start | bytes 24580
  128.4 103.3 %all-to-all-start = ((bf16[4,4,160,768]{3,2,1,0:T(8,128)(2,1)}), bf16[4,4,160,768]{3,2,1,0:T(8,128)(2,1)}, u32[]{:S(2)}, u32[]{:S(2)}) async-start(bf16[4,4,160,768]{3,2,1,0:T(8,128)(2,1)} %bitcast.67), calls=%async_computation | async-start | bytes 7864320 | tf_op jit(solution)/shard_map/all_to_all | solution.py:506
  133.2 341.3 %reduce-scatter.3.cloned.1.call-start = ((), (), s32[]{:S(2)}) async-start(), calls=%async_computation.8 | async-start | bytes 31850496 | tf_op jit(solution)/shard_map/reduce_scatter | solution.py:632
  280.0 93.1 %all-to-all-start.3 = ((bf16[4,2,2,160,768]{4,3,2,1,0:T(8,128)(2,1)}), bf16[4,2,2,160,768]{4,3,2,1,0:T(8,128)(2,1)}, u32[]{:S(2)}, u32[]{:S(2)}) async-start(bf16[4,2,2,160,768]{4,3,2,1,0:T(8,128)(2,1)} %get-tuple-element.48.refs_4_), calls=%async_computation.3 | async-start | bytes 7864320 | tf_op jit(solution)/shard_map/all_to_all | solution.py:585
  284.9 392.4 %reduce-scatter.5.cloned.1.call-start = ((), (), s32[]{:S(2)}) async-start(), calls=%async_computation.9 | async-start | bytes 21233664 | tf_op jit(solution)/shard_map/reduce_scatter | solution.py:632
  474.5 2.0 copy-start
  477.6 27.9 %collective-permute-start = (bf16[1,3,2,768,128]{4,3,2,1,0:T(8,128)(2,1)}, bf16[1,3,2,768,128]{4,3,2,1,0:T(8,128)(2,1)}, u32[]{:S(2)}, u32[]{:S(2)}) collective-permute-start(bf16[1,3,2,768,128]{4,3,2,1,0:T(8,128)(2,1)} %slice_bitcast_fusion), channel_id=1, source_target_pairs={{0,1},{1,0},{2,3},{3,2},{4,5},{5,4},{6,7},{7,6},{8,9},{9,8},{10,11... | collective-permute-start | bytes 3538952 | tf_op jit(solution)/shard_map/ppermute | solution.py:621
  508.2 54.1 %collective-permute-start.1 = (bf16[1,3,2,768,128]{4,3,2,1,0:T(8,128)(2,1)}, bf16[1,3,2,768,128]{4,3,2,1,0:T(8,128)(2,1)S(1)}, u32[]{:S(2)}, u32[]{:S(2)}) collective-permute-start(bf16[1,3,2,768,128]{4,3,2,1,0:T(8,128)(2,1)} %add_convert_fusion), channel_id=1, source_target_pairs={{0,2},{1,3},{2,0},{3,1},{4,6},{5,7},{6,4},{7,5},{8,10},{9,11},{10,... | collective-permute-start | bytes 3538952 | tf_op jit(solution)/shard_map/ppermute | solution.py:621
  570.2 4.9 collective-permute-start.2
  578.6 1.4 copy-start.1
  580.0 36.1 %collective-permute-start.3 = (bf16[2,96,3200]{2,1,0:T(8,128)(2,1)S(1)}, bf16[2,96,3200]{2,1,0:T(8,128)(2,1)}, u32[]{:S(2)}, u32[]{:S(2)}) collective-permute-start(bf16[2,96,3200]{2,1,0:T(8,128)(2,1)S(1)} %pad_maximum_fusion), channel_id=1, source_target_pairs={{0,8},{4,20},{8,0},{12,28},{16,24},{20,4},{24,16},{28,12},{1,9},{5... | collective-permute-start | bytes 3686408 | tf_op jit(solution)/shard_map/ppermute | solution.py:60
  619.6 10.4 %collective-permute-start.4 = (bf16[96,3200]{1,0:T(8,128)(2,1)}, bf16[96,3200]{1,0:T(8,128)(2,1)S(1)}, u32[]{:S(2)}, u32[]{:S(2)}) collective-permute-start(bf16[96,3200]{1,0:T(8,128)(2,1)} %fusion.5), channel_id=1, source_target_pairs={{0,16},{4,12},{8,24},{12,4},{16,0},{20,28},{24,8},{28,20},{1,17},{... | collective-permute-start | bytes 1843208 | tf_op jit(solution)/shard_map/ppermute | solution.py:60
  631.2 15.1 %collective-permute-start.5 = (bf16[96,3200]{1,0:T(8,128)(2,1)S(1)}, bf16[96,3200]{1,0:T(8,128)(2,1)S(1)}, u32[]{:S(2)}, u32[]{:S(2)}) collective-permute-start(bf16[96,3200]{1,0:T(8,128)(2,1)S(1)} %fusion.3), channel_id=1, source_target_pairs={{0,1},{1,0},{2,3},{3,2},{4,5},{5,4},{6,7},{7,6},{8,9},{9,8},{10,11... | collective-permute-start | bytes 1843208 | tf_op jit(solution)/shard_map/ppermute | solution.py:621
  646.4 28.3 %collective-permute-start.6 = (bf16[96,3200]{1,0:T(8,128)(2,1)S(1)}, bf16[96,3200]{1,0:T(8,128)(2,1)S(1)}, u32[]{:S(2)}, u32[]{:S(2)}) collective-permute-start(bf16[96,3200]{1,0:T(8,128)(2,1)S(1)} %add_convert_fusion.1), channel_id=1, source_target_pairs={{0,2},{1,3},{2,0},{3,1},{4,6},{5,7},{6,4},{7,5},{8,10},{9,11},{10,... | collective-permute-start | bytes 1843208 | tf_op jit(solution)/shard_map/ppermute | solution.py:621
Sparse Core Ops, SparseCore 0:
  11.7 42.3 all-gather.5
  55.9 138.4 all-gather.7
  196.9 98.5 all-gather.9
  299.1 175.3 reduce-scatter.2
  478.0 136.5 reduce-scatter.4

commit v4 on v3

--- a/solution.py
+++ b/solution.py
@@ -87,13 +87,16 @@
     return jnp.where(held, 1.0, 0.0).astype(BF16)
 
 
-def put_rows(sent, out):
-    for expert in range(out.shape[0]):
-        out[expert, 0] = sent[expert * CAP : (expert + 1) * CAP].astype(BF16)
-
-
-def dispatch_kernel(flat_ref, field_ref, out_ref):
-    put_rows(mm(place_of(flat_ref[0], out_ref.shape[0] * CAP), field_ref[0], NN), out_ref)
+def put_rows(sent, outs):
+    owners, size = outs[0].shape[:2]
+    local = len(outs) * size
+    for expert in range(owners * local):
+        rows = sent[expert * CAP : (expert + 1) * CAP].astype(BF16)
+        outs[expert % local // size][expert // local, expert % size, 0] = rows
+
+
+def dispatch_kernel(experts, flat_ref, field_ref, *outs):
+    put_rows(mm(place_of(flat_ref[0], experts * CAP), field_ref[0], NN), outs)
 
 
 def swap_halves(field):
@@ -119,7 +122,7 @@
 
 def forward_kernel(
     experts, tokens_ref, column_ref, row_ref, flat_ref, weight_ref, gain_one_ref, gain_two_ref, cosine_ref, sine_ref,
-    hidden_ref, mixed_ref, attended_ref, qkv_ref, logsum_ref, router_ref, sent_ref,
+    hidden_ref, mixed_ref, attended_ref, qkv_ref, logsum_ref, router_ref, *outs,
 ):
     width = tokens_ref.shape[2]
     x = tokens_ref[0].astype(F32)
@@ -155,7 +158,7 @@
     logits = jnp.where(lane < experts, mm(mixed, weight_ref[:, 4 * width :], NN), -1e30)
     expo = jnp.exp(logits - jnp.max(logits, axis=-1, keepdims=True))
     router_ref[0] = expo / jnp.sum(expo, axis=-1, keepdims=True)
-    put_rows(mm(place_of(flat_ref[0], experts * CAP), mixed, NN), sent_ref)
+    put_rows(mm(place_of(flat_ref[0], experts * CAP), mixed, NN), outs)
 
 
 def get_rows(backs, which, experts, held_ref):
@@ -405,15 +408,16 @@
                 back_ref[k, 1] = dx_ref[at, :].astype(BF16)
 
 
-def feed(rows, grads, gates, weights, first_row, first_weight, experts, name, carried=None, after=()):
+def feed(rows, grads, gates, weights, first_grad, first_weight, experts, name, carried=None, after=()):
     count, _, part, width = rows.shape
     squeezed = pl.Squeezed()
     gated, packed = gates is not None, len(weights) == 1
     total = count * part
-    row = lambda l, f: (0, first_row + l, 0, 0)
+    row = lambda l, f: (0, l, 0, 0)
+    grad = lambda l, f: (0, first_grad + l, 0, 0)
     operands = [rows, grads] + ([gates] if gated else [])
-    in_specs = [pl.BlockSpec((count, squeezed, part, width), row)] * 2
-    in_specs += [pl.BlockSpec((count, squeezed, 1, part), row)] * gated
+    in_specs = [pl.BlockSpec((count, squeezed, part, width), index) for index in (row, grad)]
+    in_specs += [pl.BlockSpec((count, squeezed, 1, part), grad)] * gated
     if packed:
         devices, _, _, steps = weights[0].shape[:4]
         units = steps * devices * LANES
@@ -451,9 +455,9 @@
         input_output_aliases={inputs: len(out_shapes)} if carried is not None else {},
         compiler_params=pltpu.CompilerParams(vmem_limit_bytes=VMEM_BYTES),
         cost_estimate=pl.CostEstimate(
-            flops=18 * experts * total * width * units,
+            flops=360 * experts * total * width * units,
             bytes_accessed=experts * (12 * width * units + 8 * total * width),
-            transcendentals=experts * total * units,
+            transcendentals=0,
         ),
         name=name,
     )(*operands, *unread)
@@ -503,28 +507,28 @@
     flat = (route_ids * CAP + slots.reshape(batch, length, 2)).transpose(0, 2, 1)
 
     def trade(field):
-        return lax.all_to_all(field.reshape(owners, local_experts, batch * CAP, width), "expert", 0, 0)
+        return lax.all_to_all(field.reshape(owners, field.shape[1], batch * CAP, width), "expert", 0, 0)
 
     whole = lambda shape: pl.BlockSpec(shape, lambda b: (0,) * len(shape))
     each = lambda *shape: pl.BlockSpec((1,) + shape, lambda b: (b, 0, 0))
-    piece_spec = pl.BlockSpec((experts, 1, CAP, width), lambda b: (0, b, 0, 0))
-    piece_shape = jax.ShapeDtypeStruct((experts, batch, CAP, width), BF16)
+    piece_spec = lambda count: pl.BlockSpec((owners, count, 1, CAP, width), lambda b: (0, 0, b, 0, 0))
+    piece_shape = lambda count: jax.ShapeDtypeStruct((owners, count, batch, CAP, width), BF16)
     rows = experts * CAP
     params = pltpu.CompilerParams(vmem_limit_bytes=VMEM_BYTES)
 
     grad_low = cotangent.reshape(batch, length, width)
     grad_sent = pl.pallas_call(
-        dispatch_kernel,
+        functools.partial(dispatch_kernel, experts),
         grid=(batch,),
         in_specs=[each(2, length), each(length, width)],
-        out_specs=piece_spec,
-        out_shape=piece_shape,
+        out_specs=[piece_spec(local_experts)],
+        out_shape=[piece_shape(local_experts)],
         compiler_params=params,
         cost_estimate=pl.CostEstimate(
             flops=2 * batch * rows * length * width, bytes_accessed=4 * batch * rows * width, transcendentals=0),
         name="dispatch",
     )(flat, grad_low)
-    grad_arrived = trade(grad_sent)
+    grad_arrived = trade(grad_sent[0])
 
     token_rows = tokens.reshape(batch, length, width)
     segment_ids = segments.reshape(batch, length)
@@ -553,8 +557,8 @@
         functools.partial(forward_kernel, experts),
         grid=(batch,),
         in_specs=[each(length, width)] + position_specs + weight_specs,
-        out_specs=kept_specs + [piece_spec],
-        out_shape=kept_shapes + [piece_shape],
+        out_specs=kept_specs + [piece_spec(size)] * groups,
+        out_shape=kept_shapes + [piece_shape(size)] * groups,
         compiler_params=params,
         cost_estimate=pl.CostEstimate(
             flops=2 * tokens_all * width * (columns + 4 * length + rows),
@@ -563,9 +567,9 @@
         ),
         name="attention",
     )(token_rows, *position_args, *weight_args)
-    kept, sent = outs[:6], outs[6]
+    kept, sent = outs[:6], outs[6:]
     mixed_in, router = kept[1], kept[5]
-    arrived = trade(sent)
+    arrived = [trade(field) for field in sent]
     chosen = route_ids[..., None] == jnp.arange(experts, dtype=jnp.int32)
     gates = jnp.sum(jnp.where(chosen, router[:, :, None, :experts], 0.0), axis=-1).transpose(0, 2, 1)
     held = flat[:, :, None, :] == jnp.arange(rows, dtype=jnp.int32)[:, None]
@@ -573,17 +577,21 @@
     slot_gates = slot_gates.reshape(batch, owners, local_experts, CAP).transpose(1, 2, 0, 3)
     slot_gates = lax.all_to_all(slot_gates.reshape(owners, local_experts, 1, batch * CAP), "expert", 0, 0)
 
-    shared_out, d_mixed, *shared_sums = feed(
-        mixed_in.reshape(1, 1, tokens_all, width), grad_low.reshape(1, 1, tokens_all, width), None,
-        shared_weights, 0, size if packed else 0, 1, "shared")
-
     backs, sums = [], []
+    after = []
     for h in range(groups):
         results, *grads = feed(
-            arrived, grad_arrived, slot_gates, weights[h], h * size, 0, size, "experts",
-            shared_sums[0] if packed and h == 0 else None, [shared_out if h == 0 else results])
-        backs.append(lax.all_to_all(results, "expert", 0, 0).reshape(owners, 2, size, batch, CAP, width))
+            arrived[h], grad_arrived, slot_gates, weights[h], h * size, 0, size, "experts", None, after)
+        back = lax.all_to_all(tie(results, *(backs[-1:] if h else arrived[1:])), "expert", 0, 0)
+        backs.append(back.reshape(owners, 2, size, batch, CAP, width))
         sums.append(grads)
+        if h == 0:
+            shared_out, d_mixed, *shared_sums = feed(
+                mixed_in.reshape(1, 1, tokens_all, width), grad_low.reshape(1, 1, tokens_all, width), None,
+                shared_weights, 0, size if packed else 0, 1, "shared", grads[0] if packed else None, arrived[1:])
+            after = [shared_out]
+            if packed:
+                sums[0] = shared_sums
 
     layer_out, grad_tokens, first_grad = pl.pallas_call(
         functools.partial(backward_kernel, experts, groups),
@@ -626,14 +634,12 @@
 
     units = hidden_units
     if packed:
-        mine = []
-        for field in sums:
-            field = tie(field[0], *mine, *backs) if mine else field[0]
-            mine.append(lax.psum_scatter(field, "dp", scatter_dimension=0))
+        mine = [
+            lax.psum_scatter(tie(field[0], *(backs[h - 1 : h] if h else arrived[1:])), "dp", scatter_dimension=0)
+            for h, field in enumerate(sums)]
         pool_mine = unpack(mine, [size] * groups, width // devices, units, "unpack_experts")
         shared_mine = unpack(
             [over_owners(mine[0][size:])], [1], width // devices, units, "unpack_shared")
-        first_grad = tie(first_grad, shared_mine[0])
         shared_mine = [field[0] for field in shared_mine]
     else:
         def scatter(both, down):
@@ -644,7 +650,8 @@
         pool_mine = [both[:, 0], both[:, 1], down]
         both, down = (over_owners(field[0]) for field in scatter(*shared_sums))
         shared_mine = [both[0], both[1], down]
-    first_mine = over_owners(scatter_rows(first_grad.reshape(devices, width // devices, columns)))
+    first_mine = scatter_rows(first_grad.reshape(devices, width // devices, columns))
+    first_mine = over_owners(tie(first_mine, shared_mine[0]) if packed else first_mine)
     return (
         layer_out.reshape(tokens.shape),
         grad_tokens.reshape(tokens.shape),

time: 700 us -> 664 us (0.949)
  blocking collectives: 102 us -> 8.63 us
  waiting for transfers between devices: 272 us -> 323 us
    all_to_all x3 -> x5, waiting for transfers between devices: 59.3 us -> 157 us  [the longest x2 88.3 us: on_device(): lax.all_to_all(tie(results, *(backs[-1:] if h else arrived[1:])), 'expert...]
    all_to_all x1 -> x0, blocking collectives: 93.2 us -> none  [on_device(): lax.all_to_all(results, 'expert', 0, 0)]
    all_gather x2, waiting for transfers between devices: 71.8 us -> 25.3 us  [on_device(): lax.all_gather(pack(h * size, size, pool, (shared_gate, shared_up, shared...]
    all_to_all x3 -> x5, starting transfers between devices: 16.1 us -> 25.1 us  [the longest x3 15 us: trade(): lax.all_to_all(field.reshape(owners, field.shape[1], batch * CAP, width),...]
    reduce_scatter x2, waiting for transfers between devices: 8.22 us -> 0.01 us  [on_device(): lax.psum_scatter(tie(field[0], *(backs[h - 1:h] if h else arrived[1:])),...]
    ppermute x4, starting transfers between devices: 7.96 us -> 0.39 us  [over_owners(): came = lax.ppermute(field, 'expert', [(i, i ^ k) for i in range(owners)])]
  transfers between devices with their start and end apart: 15 -> 17, of which waited for: 12 -> 12; matrix products, arithmetic and copies ran while one was open for 4% -> 5% of each run, Pallas kernels for 34% -> 37%
where the time goes in v4:
time: 664 us; the launch traced here: 654 us
  waiting for transfers between devices  323 us (49%)
  Pallas kernels  242 us (36%)
  starting transfers between devices  27.2 us (4%)
  other arithmetic  19.6 us (3%)
  local copies, waits for them, and re-layouts  19.5 us (3%)
  between operations  14.3 us (2%)
  blocking collectives  8.63 us (1%)
    pallas_call x3, Pallas kernels, feed(): pl.pallas_call(skipping(functools.partial(feed_kernel, gated, packed), in...  136 us
    all_to_all x2, waiting for transfers between devices, on_device(): lax.all_to_all(tie(results, *(backs[-1:] if h else arrived[1:])), 'expert...  88.3 us
    all_to_all x3, waiting for transfers between devices, trade(): lax.all_to_all(field.reshape(owners, field.shape[1], batch * CAP, width),...  68.5 us
    ppermute x4, waiting for transfers between devices, over_owners(): came = lax.ppermute(field, 'expert', [(i, i ^ k) for i in range(owners)])  67.1 us
    pallas_call x1, Pallas kernels, on_device(): pl.pallas_call(functools.partial(backward_kernel, experts, groups), grid=...  52.9 us
    ppermute x3, waiting for transfers between devices, send(): return lax.ppermute(field, 'dp', [(i, step(i)) for i in range(8)])  51.9 us
    pallas_call x1, Pallas kernels, on_device(): pl.pallas_call(functools.partial(forward_kernel, experts), grid=(batch,),...  31.3 us
    all_gather x2, waiting for transfers between devices, on_device(): lax.all_gather(pack(h * size, size, pool, (shared_gate, shared_up, shared...  25.3 us
  transfers between devices with their start and end apart: 17, of which 12 were waited for; matrix products, arithmetic and copies ran while one was open for 5% of the time, Pallas kernels for 37%

profile of v4, /device:TPU:0, one launch (start us, length us, event | category | flops | bytes accessed | tf_op | source)
XLA Modules:
  0.0 654.3 jit_solution(18428453213301930348)
XLA Ops:
  11.6 4.2 pack.2
  17.8 5.0 dispatch.1
  22.8 6.5 all-to-all-start.1
  32.3 21.8 %all-gather.6.cloned.1.call-done.weight_ref = bf16[768,3200]{1,0:T(8,128)(2,1)} async-done(((bf16[96,3200]{1,0:T(8,128)(2,1)}), bf16[768,3200]{1,0:T(8,128)(2,1)}) %all-gather.6.cloned.1.call-update) | async-done | bytes 4915216 | tf_op jit(solution)/shard_map/all_gather | solution.py:488
  55.9 31.3 %attention.1 = (f32[4,256,768]{2,1,0:T(8,128)}, bf16[4,256,768]{2,1,0:T(8,128)(2,1)}, bf16[4,256,768]{2,1,0:T(8,128)(2,1)}, bf16[4,256,2304]{2,1,0:T(8,128)(2,1)...) custom-call(bf16[4,256,768]{2,1,0:T(8,128)(2,1)} %bitcast.83, ...), custom_call_target="tpu_custom_call" | custom-call | flops 7650410496 | bytes 20643840 | tf_op jit(solution)/shard_map/attention/pallas_call | solution.py:556
  89.4 27.8 %all-to-all-done.1.refs_1_ = bf16[4,4,160,768]{3,2,1,0:T(8,128)(2,1)} async-done(((bf16[4,4,160,768]{3,2,1,0:T(8,128)(2,1)}), bf16[4,4,160,768]{3,2,1,0:T(8,128)(2,1)}, u32[]{:S(2)}, u32[]{:S(2)}) %all-to-all-start.1) | async-done | bytes 3932192 | tf_op jit(solution)/shard_map/all_to_all | solution.py:510
  117.2 8.6 %all_to_all.30.refs_2_ = f32[4,4,1,160]{3,2,1,0:T(1,128)} all-to-all(f32[4,4,1,160]{3,2,1,0:T(1,128)S(1)} %reshape.146), channel_id=1, replica_groups=mesh['dp'=8,'expert'=4] {'expert'}, dimensions={0} | all-to-all | bytes 20480 | tf_op jit(solution)/shard_map/all_to_all | solution.py:578
  125.8 3.6 all-to-all-start
  129.4 2.9 pack.3
  132.3 40.7 %all-to-all-done.refs_0_ = bf16[4,2,160,768]{3,2,1,0:T(8,128)(2,1)S(1)} async-done(((bf16[4,2,160,768]{3,2,1,0:T(8,128)(2,1)}), bf16[4,2,160,768]{3,2,1,0:T(8,128)(2,1)S(1)}, u32[]{:S(2)}, u32[]{:S(2)}) %all-to-all-start) | async-done | bytes 1966112 | tf_op jit(solution)/shard_map/all_to_all | solution.py:510
  173.0 5.0 all-to-all-start.3
  178.0 16.5 %all-gather.8.cloned.1.call-done = bf16[24,3,2,768,128]{4,3,2,1,0:T(8,128)(2,1)} async-done(((bf16[3,3,2,768,128]{4,3,2,1,0:T(8,128)(2,1)}), bf16[24,3,2,768,128]{4,3,2,1,0:T(8,128)(2,1)}) %all-gather.8.cloned.1.call-update) | async-done | bytes 28311568 | tf_op jit(solution)/shard_map/all_gather | solution.py:491
  194.5 49.9 %experts.2 = (bf16[4,2,2,160,768]{4,3,2,1,0:T(8,128)(2,1)}, bf16[8,3,3,2,768,128]{5,4,3,2,1,0:T(8,128)(2,1)}) custom-call(bf16[4,2,160,768]{3,2,1,0:T(8,128)(2,1)} %copy-done.2, bf16[4,4,160,768]{3,2,1,0:T(8,128)(2,1)} %all-to-all-done.1.refs_1_, f32[4,4,1,160]{3,2,1,0:T(1,128)} %all_to_all.30.refs_2_, bf16[8,3,3,2,768,128]{5,4,3,2,1,0:T(8,128)(2,1)} %bitcast.80), custom_call_target="tpu_custom_call" | custom-call | flops 724775731200 | bytes 45613056 | tf_op jit(solution)/shard_map/experts/pallas_call | solution.py:448
  244.4 4.8 all-to-all-start.4
  249.3 37.4 %shared.1 = (f32[1,1,1024,768]{3,2,1,0:T(8,128)}, f32[1,1,1024,768]{3,2,1,0:T(8,128)}, bf16[8,3,3,2,768,128]{5,4,3,2,1,0:T(8,128)(2,1)}) custom-call(bf16[1,1,1024,768]{3,2,1,0:T(8,128)(2,1)} %bitcast.91, bf16[1,1,1024,768]{3,2,1,0:T(8,128)(2,1)} %bitcast.68, bf16[8,3,3,2,768,128]{5,4,3,2,1,0:T(8,128)(2,1)} %bitcast.81, ...), custom_call_target="tpu_custom_call", output_to_operand_aliasing={{2}: (3, {})} | custom-call | flops 579820584960 | bytes 25165824 | tf_op jit(solution)/shard_map/shared/pallas_call | solution.py:448
  286.8 8.8 %all-gather.10.cloned.1.call-done = bf16[16,3,2,768,128]{4,3,2,1,0:T(8,128)(2,1)} async-done(((bf16[2,3,2,768,128]{4,3,2,1,0:T(8,128)(2,1)}), bf16[16,3,2,768,128]{4,3,2,1,0:T(8,128)(2,1)}) %all-gather.10.cloned.1.call-update) | async-done | bytes 18874384 | tf_op jit(solution)/shard_map/all_gather | solution.py:491
  295.6 48.4 %experts.3 = (bf16[4,2,2,160,768]{4,3,2,1,0:T(8,128)(2,1)}, bf16[8,2,3,2,768,128]{5,4,3,2,1,0:T(8,128)(2,1)}) custom-call(bf16[4,2,160,768]{3,2,1,0:T(8,128)(2,1)} %all-to-all-done.3.refs_4_.refs_1_.refs_0_, bf16[4,4,160,768]{3,2,1,0:T(8,128)(2,1)} %all-to-all-done.1.refs_1_, f32[4,4,1,160]{3,2,1,0:T(1,128)} %all_to_all.30.refs_2_, ...), custom_call_target="tpu_custom_call" | custom-call | flops 724775731200 | bytes 45613056 | tf_op jit(solution)/shard_map/experts/pallas_call | solution.py:448
  344.0 5.2 all-to-all-start.5
  349.3 88.2 %all-to-all-done.5 = bf16[4,2,2,160,768]{4,3,2,1,0:T(8,128)(2,1)} async-done(((bf16[4,2,2,160,768]{4,3,2,1,0:T(8,128)(2,1)}), bf16[4,2,2,160,768]{4,3,2,1,0:T(8,128)(2,1)}, u32[]{:S(2)}, u32[]{:S(2)}) %all-to-all-start.5) | async-done | bytes 3932192 | tf_op jit(solution)/shard_map/all_to_all | solution.py:585
  437.5 52.9 %attention_back.1 = (bf16[4,256,768]{2,1,0:T(8,128)(2,1)}, f32[4,256,768]{2,1,0:T(8,128)}, bf16[768,3200]{1,0:T(8,128)(2,1)}) custom-call(bf16[4,256,768]{2,1,0:T(8,128)(2,1)} %bitcast.84, bf16[4,256,768]{2,1,0:T(8,128)(2,1)} %bitcast.69, s32[4,256,1]{2,1,0:T(8,128)} %broadcast_in_dim_reshape.5.column_ref, s32[4,1,256]{2,1,0:T(1,128)} %row_ref.3, ...), custom_call_target="tpu_custom_call" | custom-call | flops 15300820992 | bytes 34996224 | tf_op jit(solution)/shard_map/attention_back/pallas_call | solution.py:596
  492.9 8.0 %collective-permute-done = bf16[4,96,3200]{2,1,0:T(8,128)(2,1)} collective-permute-done((bf16[4,96,3200]{2,1,0:T(8,128)(2,1)S(1)}, bf16[4,96,3200]{2,1,0:T(8,128)(2,1)}, u32[]{:S(2)}, u32[]{:S(2)}) %collective-permute-start) | collective-permute-done | bytes 2457632 | tf_op jit(solution)/shard_map/ppermute | solution.py:60
  500.8 4.1 fusion
  507.8 2.4 slice_bitcast_fusion
  510.3 23.3 %collective-permute-done.1 = bf16[2,96,3200]{2,1,0:T(8,128)(2,1)} collective-permute-done((bf16[2,96,3200]{2,1,0:T(8,128)(2,1)S(1)}, bf16[2,96,3200]{2,1,0:T(8,128)(2,1)}, u32[]{:S(2)}, u32[]{:S(2)}) %collective-permute-start.1) | collective-permute-done | bytes 1228832 | tf_op jit(solution)/shard_map/ppermute | solution.py:60
  537.2 3.0 add_convert_fusion
  540.3 20.6 %collective-permute-done.2 = bf16[96,3200]{1,0:T(8,128)(2,1)S(1)} collective-permute-done((bf16[96,3200]{1,0:T(8,128)(2,1)}, bf16[96,3200]{1,0:T(8,128)(2,1)S(1)}, u32[]{:S(2)}, u32[]{:S(2)}) %collective-permute-start.2) | collective-permute-done | bytes 614432 | tf_op jit(solution)/shard_map/ppermute | solution.py:60
  563.0 29.4 %collective-permute-done.4 = bf16[1,3,2,768,128]{4,3,2,1,0:T(8,128)(2,1)} collective-permute-done((bf16[1,3,2,768,128]{4,3,2,1,0:T(8,128)(2,1)}, bf16[1,3,2,768,128]{4,3,2,1,0:T(8,128)(2,1)}, u32[]{:S(2)}, u32[]{:S(2)}) %collective-permute-start.4) | collective-permute-done | bytes 1179680 | tf_op jit(solution)/shard_map/ppermute | solution.py:629
  592.4 3.3 convert_add_fusion.1.refs_0_
  595.6 3.1 unpack_shared.1
  598.8 16.0 %collective-permute-done.5 = bf16[96,3200]{1,0:T(8,128)(2,1)S(1)} collective-permute-done((bf16[96,3200]{1,0:T(8,128)(2,1)}, bf16[96,3200]{1,0:T(8,128)(2,1)S(1)}, u32[]{:S(2)}, u32[]{:S(2)}) %collective-permute-start.5) | collective-permute-done | bytes 614432 | tf_op jit(solution)/shard_map/ppermute | solution.py:629
  616.4 7.0 %unpack_experts.1 = (f32[4,96,2048]{2,1,0:T(8,128)}, f32[4,96,2048]{2,1,0:T(8,128)}, f32[4,256,768]{2,1,0:T(8,128)}) custom-call(bf16[3,3,2,768,128]{4,3,2,1,0:T(8,128)(2,1)} %bitcast.60, bf16[2,3,2,768,128]{4,3,2,1,0:T(8,128)(2,1)} %bitcast.65), custom_call_target="tpu_custom_call" | custom-call | tf_op jit(solution)/shard_map/unpack_experts/pallas_call | solution.py:328
  623.4 21.7 %collective-permute-done.6 = bf16[96,3200]{1,0:T(8,128)(2,1)S(1)} collective-permute-done((bf16[96,3200]{1,0:T(8,128)(2,1)S(1)}, bf16[96,3200]{1,0:T(8,128)(2,1)S(1)}, u32[]{:S(2)}, u32[]{:S(2)}) %collective-permute-start.6) | collective-permute-done | bytes 614432 | tf_op jit(solution)/shard_map/ppermute | solution.py:629
  (81 shorter events, 28.6 us)
Async XLA Ops:
  7.2 46.9 %all-gather.6.cloned.1.call-start = ((), (), s32[]{:S(2)}) async-start(), calls=%async_computation.8 | async-start | bytes 5529600 | tf_op jit(solution)/shard_map/all_gather | solution.py:488
  11.6 182.9 %all-gather.8.cloned.1.call-start = ((), (), s32[]{:S(2)}) async-start(), calls=%async_computation.11 | async-start | bytes 31850496 | tf_op jit(solution)/shard_map/all_gather | solution.py:491
  15.8 0.7 copy-start.4
  15.8 0.9 copy-start.5
  17.0 15.1 %copy-start.1 = (s32[4,1,256,2]{3,2,0,1:T(8,128)}, s32[4,1,256,2]{3,2,0,1:T(8,128)S(1)}, u32[]{:S(2)}) copy-start(s32[4,1,256,2]{3,2,0,1:T(8,128)S(1)} %copy.98) | copy-start | bytes 24580
  22.8 6.5 copy-start.6
  22.8 94.3 %all-to-all-start.1 = ((bf16[4,4,160,768]{3,2,1,0:T(8,128)(2,1)}), bf16[4,4,160,768]{3,2,1,0:T(8,128)(2,1)}, u32[]{:S(2)}, u32[]{:S(2)}) async-start(bf16[4,4,160,768]{3,2,1,0:T(8,128)(2,1)} %bitcast.59), calls=%async_computation.1 | async-start | bytes 7864320 | tf_op jit(solution)/shard_map/all_to_all | solution.py:510
  55.9 32.5 %copy-start.3 = (s32[4,2,256]{2,1,0:T(2,128)S(1)}, s32[4,2,256]{2,1,0:T(2,128)}, u32[]{:S(2)}) copy-start(s32[4,2,256]{2,1,0:T(2,128)} %copy.114.flat_ref) | copy-start | bytes 24580
  125.8 47.2 %all-to-all-start = ((bf16[4,2,160,768]{3,2,1,0:T(8,128)(2,1)}), bf16[4,2,160,768]{3,2,1,0:T(8,128)(2,1)S(1)}, u32[]{:S(2)}, u32[]{:S(2)}) async-start(bf16[4,2,160,768]{3,2,1,0:T(8,128)(2,1)} %bitcast.66), calls=%async_computation | async-start | bytes 3932160 | tf_op jit(solution)/shard_map/all_to_all | solution.py:510
  129.4 166.2 %all-gather.10.cloned.1.call-start = ((), (), s32[]{:S(2)}) async-start(), calls=%async_computation.12 | async-start | bytes 21233664 | tf_op jit(solution)/shard_map/all_gather | solution.py:491
  173.0 21.5 %copy-start.2 = (bf16[4,2,160,768]{3,2,1,0:T(8,128)(2,1)}, bf16[4,2,160,768]{3,2,1,0:T(8,128)(2,1)S(1)}, u32[]{:S(2)}) copy-start(bf16[4,2,160,768]{3,2,1,0:T(8,128)(2,1)S(1)} %all-to-all-done.refs_0_) | copy-start | bytes 5898244
  173.0 71.4 %all-to-all-start.3 = ((bf16[4,2,160,768]{3,2,1,0:T(8,128)(2,1)}), bf16[4,2,160,768]{3,2,1,0:T(8,128)(2,1)}, u32[]{:S(2)}, u32[]{:S(2)}) async-start(bf16[4,2,160,768]{3,2,1,0:T(8,128)(2,1)} %bitcast.17), calls=%async_computation.3 | async-start | bytes 3932160 | tf_op jit(solution)/shard_map/all_to_all | solution.py:510
  244.4 99.5 %all-to-all-start.4 = ((bf16[4,2,2,160,768]{4,3,2,1,0:T(8,128)(2,1)}), bf16[4,2,2,160,768]{4,3,2,1,0:T(8,128)(2,1)}, u32[]{:S(2)}, u32[]{:S(2)}) async-start(bf16[4,2,2,160,768]{4,3,2,1,0:T(8,128)(2,1)} %tie.5), calls=%async_computation.4 | async-start | bytes 7864320 | tf_op jit(solution)/shard_map/all_to_all | solution.py:585
  249.3 258.6 %reduce-scatter.3.cloned.1.call-start = ((), (), s32[]{:S(2)}) async-start(), calls=%async_computation.9 | async-start | bytes 31850496 | tf_op jit(solution)/shard_map/reduce_scatter | solution.py:638
  286.7 329.7 %reduce-scatter.5.cloned.1.call-start = ((), (), s32[]{:S(2)}) async-start(), calls=%async_computation.10 | async-start | bytes 21233664 | tf_op jit(solution)/shard_map/reduce_scatter | solution.py:638
  344.0 93.5 %all-to-all-start.5 = ((bf16[4,2,2,160,768]{4,3,2,1,0:T(8,128)(2,1)}), bf16[4,2,2,160,768]{4,3,2,1,0:T(8,128)(2,1)}, u32[]{:S(2)}, u32[]{:S(2)}) async-start(bf16[4,2,2,160,768]{4,3,2,1,0:T(8,128)(2,1)} %tie.6), calls=%async_computation.5 | async-start | bytes 7864320 | tf_op jit(solution)/shard_map/all_to_all | solution.py:585
  492.7 8.1 %collective-permute-start = (bf16[4,96,3200]{2,1,0:T(8,128)(2,1)S(1)}, bf16[4,96,3200]{2,1,0:T(8,128)(2,1)}, u32[]{:S(2)}, u32[]{:S(2)}) collective-permute-start(bf16[4,96,3200]{2,1,0:T(8,128)(2,1)S(1)} %dynamic-slice_bitcast_fusion), channel_id=1, source_target_pairs={{0,4},{4,0},{8,12},{12,8},{16,20},{20,16},{24,28},{28,24},{1,5},{5... | collective-permute-start | bytes 7372808 | tf_op jit(solution)/shard_map/ppermute | solution.py:60
  504.9 1.4 copy-start
  506.4 27.2 %collective-permute-start.1 = (bf16[2,96,3200]{2,1,0:T(8,128)(2,1)S(1)}, bf16[2,96,3200]{2,1,0:T(8,128)(2,1)}, u32[]{:S(2)}, u32[]{:S(2)}) collective-permute-start(bf16[2,96,3200]{2,1,0:T(8,128)(2,1)S(1)} %pad_maximum_fusion), channel_id=1, source_target_pairs={{0,8},{4,20},{8,0},{12,28},{16,24},{20,4},{24,16},{28,12},{1,9},{5... | collective-permute-start | bytes 3686408 | tf_op jit(solution)/shard_map/ppermute | solution.py:60
  510.3 27.0 %collective-permute-start.3 = (bf16[1,3,2,768,128]{4,3,2,1,0:T(8,128)(2,1)}, bf16[1,3,2,768,128]{4,3,2,1,0:T(8,128)(2,1)}, u32[]{:S(2)}, u32[]{:S(2)}) collective-permute-start(bf16[1,3,2,768,128]{4,3,2,1,0:T(8,128)(2,1)} %slice_bitcast_fusion), channel_id=1, source_target_pairs={{0,1},{1,0},{2,3},{3,2},{4,5},{5,4},{6,7},{7,6},{8,9},{9,8},{10,11... | collective-permute-start | bytes 3538952 | tf_op jit(solution)/shard_map/ppermute | solution.py:629
  537.2 23.6 %collective-permute-start.2 = (bf16[96,3200]{1,0:T(8,128)(2,1)}, bf16[96,3200]{1,0:T(8,128)(2,1)S(1)}, u32[]{:S(2)}, u32[]{:S(2)}) collective-permute-start(bf16[96,3200]{1,0:T(8,128)(2,1)} %fusion.5), channel_id=1, source_target_pairs={{0,16},{4,12},{8,24},{12,4},{16,0},{20,28},{24,8},{28,20},{1,17},{... | collective-permute-start | bytes 1843208 | tf_op jit(solution)/shard_map/ppermute | solution.py:60
  540.3 52.1 %collective-permute-start.4 = (bf16[1,3,2,768,128]{4,3,2,1,0:T(8,128)(2,1)}, bf16[1,3,2,768,128]{4,3,2,1,0:T(8,128)(2,1)}, u32[]{:S(2)}, u32[]{:S(2)}) collective-permute-start(bf16[1,3,2,768,128]{4,3,2,1,0:T(8,128)(2,1)} %add_convert_fusion), channel_id=1, source_target_pairs={{0,2},{1,3},{2,0},{3,1},{4,6},{5,7},{6,4},{7,5},{8,10},{9,11},{10,... | collective-permute-start | bytes 3538952 | tf_op jit(solution)/shard_map/ppermute | solution.py:629
  598.8 16.0 %collective-permute-start.5 = (bf16[96,3200]{1,0:T(8,128)(2,1)}, bf16[96,3200]{1,0:T(8,128)(2,1)S(1)}, u32[]{:S(2)}, u32[]{:S(2)}) collective-permute-start(bf16[96,3200]{1,0:T(8,128)(2,1)} %tie.8), channel_id=1, source_target_pairs={{0,1},{1,0},{2,3},{3,2},{4,5},{5,4},{6,7},{7,6},{8,9},{9,8},{10,11... | collective-permute-start | bytes 1843208 | tf_op jit(solution)/shard_map/ppermute | solution.py:629
  616.0 29.1 %collective-permute-start.6 = (bf16[96,3200]{1,0:T(8,128)(2,1)S(1)}, bf16[96,3200]{1,0:T(8,128)(2,1)S(1)}, u32[]{:S(2)}, u32[]{:S(2)}) collective-permute-start(bf16[96,3200]{1,0:T(8,128)(2,1)S(1)} %add_convert_fusion.1), channel_id=1, source_target_pairs={{0,2},{1,3},{2,0},{3,1},{4,6},{5,7},{6,4},{7,5},{8,10},{9,11},{10,... | collective-permute-start | bytes 1843208 | tf_op jit(solution)/shard_map/ppermute | solution.py:629
Sparse Core Ops, SparseCore 0:
  11.7 42.3 all-gather.5
  56.0 138.4 all-gather.7
  196.9 98.5 all-gather.9
  299.1 175.3 reduce-scatter.2
  478.0 135.4 reduce-scatter.4

commit v5 on v4

--- a/solution.py
+++ b/solution.py
@@ -315,7 +315,7 @@
         start += size
 
 
-def unpack(packs, sizes, rows, units, name):
+def unpack(packs, sizes, rows, units, name, after=()):
     squeezed = pl.Squeezed()
     specs, start = [], 0
     for field, size in zip(packs, sizes):
@@ -326,13 +326,13 @@
     width = packs[0].shape[3]
     shapes = [(rows, units), (rows, units), (rows * units // width, width)]
     return pl.pallas_call(
-        functools.partial(unpack_kernel, tuple(sizes)),
+        skipping(functools.partial(unpack_kernel, tuple(sizes)), len(packs), len(after)),
         grid=(start,),
-        in_specs=specs,
+        in_specs=specs + [ANY] * len(after),
         out_specs=[pl.BlockSpec((squeezed,) + shape, lambda l: (l, 0, 0)) for shape in shapes],
         out_shape=[jax.ShapeDtypeStruct((start,) + shape, F32) for shape in shapes],
         name=name,
-    )(*packs)
+    )(*packs, *after)
 
 
 def feed_step(x, d, gate_weight, up_weight, down_weight, out, dx):
@@ -375,29 +375,31 @@
                 column = jnp.sum(jnp.where(iota(square, 0) == iota(square, 1), line, 0.0), axis=1, keepdims=True)
                 d_ref[at, :] = (grads_ref[k].astype(F32) * column).astype(BF16)
 
-    x, d = (x_ref[...], d_ref[...]) if gated else (rows_ref[0], grads_ref[0])
+    read = lambda: (x_ref[...], d_ref[...]) if gated else (rows_ref[0], grads_ref[0])
     if packed:
         field, total = weights[0], sums[0]
         devices = field.shape[0]
         rows = width // devices
         size = min(devices, 4)
-        for start in range(0, devices, size):
-            columns = range(start, start + size)
-            side = lambda n: jnp.concatenate(
-                [field[:, n, j * rows : (j + 1) * rows, :].reshape(width, LANES) for j in columns], axis=1)
+        def half(n, carry):
+            start = n * size
+            chunks = [pl.ds(pl.multiple_of((start + j) * rows, rows), rows) for j in range(size)]
+            side = lambda k: jnp.concatenate([field[:, k, at, :].reshape(width, LANES) for at in chunks], axis=1)
             down = jnp.concatenate(
-                [field[start : start + size, 2, c * LANES : (c + 1) * LANES, :].reshape(size * LANES, LANES)
+                [field[pl.ds(start, size), 2, c * LANES : (c + 1) * LANES, :].reshape(size * LANES, LANES)
                  for c in range(width // LANES)], axis=1)
-            gate_sum, up_sum, down_sum = feed_step(x, d, side(0), side(1), down, out_ref, dx_ref)
-            for n, value in enumerate((gate_sum, up_sum)):
-                for j in columns:
-                    total[:, n, j * rows : (j + 1) * rows, :] = value[
-                        :, (j - start) * LANES : (j - start + 1) * LANES].reshape(devices, rows, LANES)
+            gate_sum, up_sum, down_sum = feed_step(*read(), side(0), side(1), down, out_ref, dx_ref)
+            for k, value in enumerate((gate_sum, up_sum)):
+                for j, at in enumerate(chunks):
+                    total[:, k, at, :] = value[:, j * LANES : (j + 1) * LANES].reshape(devices, rows, LANES)
             for c in range(width // LANES):
                 at = slice(c * LANES, (c + 1) * LANES)
-                total[start : start + size, 2, at, :] = down_sum[:, at].reshape(size, LANES, LANES)
+                total[pl.ds(start, size), 2, at, :] = down_sum[:, at].reshape(size, LANES, LANES)
+            return carry
+
+        lax.fori_loop(0, devices // size, half, 0)
     else:
-        sums[0][0], sums[0][1], sums[1][...] = feed_step(x, d, *(ref[...] for ref in weights), out_ref, dx_ref)
+        sums[0][0], sums[0][1], sums[1][...] = feed_step(*read(), *(ref[...] for ref in weights), out_ref, dx_ref)
 
     if gated:
         @pl.when(step == pl.num_programs(1) - 1)
@@ -624,12 +626,28 @@
     )
 
     def over_owners(field):
-        k = 1
+        k, before = 1, field
         while k < owners:
-            came = lax.ppermute(field, "expert", [(i, i ^ k) for i in range(owners)])
-            field = field.astype(F32) + came.astype(F32)
+            before = field.astype(BF16)
+            came = lax.ppermute(before, "expert", [(i, i ^ k) for i in range(owners)])
+            field = before.astype(F32) + came.astype(F32)
             k *= 2
-            field = field.astype(BF16) if k < owners else field
+        return field, before
+
+    def over_owners_by_halves(field):
+        place = lax.axis_index("expert")
+        steps = [1 << n for n in range(owners.bit_length() - 1)]
+        swap = lambda part, k: lax.ppermute(part, "expert", [(i, i ^ k) for i in range(owners)])
+        for k in steps:
+            second = place // k % 2
+            half = field.shape[0] // 2
+            keep = lax.dynamic_slice_in_dim(field, second * half, half)
+            came = swap(lax.dynamic_slice_in_dim(field, (1 - second) * half, half), k)
+            field = (keep.astype(F32) + came.astype(F32)).astype(BF16)
+        for k in reversed(steps):
+            came = swap(field, k)
+            second = place // k % 2 == 1
+            field = jnp.concatenate([jnp.where(second, came, field), jnp.where(second, field, came)])
         return field
 
     units = hidden_units
@@ -637,9 +655,10 @@
         mine = [
             lax.psum_scatter(tie(field[0], *(backs[h - 1 : h] if h else arrived[1:])), "dp", scatter_dimension=0)
             for h, field in enumerate(sums)]
-        pool_mine = unpack(mine, [size] * groups, width // devices, units, "unpack_experts")
         shared_mine = unpack(
-            [over_owners(mine[0][size:])], [1], width // devices, units, "unpack_shared")
+            [over_owners_by_halves(mine[0][size].reshape(-1, LANES)).reshape(mine[0][size:].shape)], [1],
+            width // devices, units, "unpack_shared")
+        first_grad = tie(first_grad, mine[0])
         shared_mine = [field[0] for field in shared_mine]
     else:
         def scatter(both, down):
@@ -648,10 +667,12 @@
 
         both, down = (jnp.concatenate(fields, axis=0).astype(F32) for fields in zip(*(scatter(*field) for field in sums)))
         pool_mine = [both[:, 0], both[:, 1], down]
-        both, down = (over_owners(field[0]) for field in scatter(*shared_sums))
+        both, down = (over_owners(field[0])[0] for field in scatter(*shared_sums))
         shared_mine = [both[0], both[1], down]
     first_mine = scatter_rows(first_grad.reshape(devices, width // devices, columns))
-    first_mine = over_owners(tie(first_mine, shared_mine[0]) if packed else first_mine)
+    first_mine, before = over_owners(first_mine)
+    if packed:
+        pool_mine = unpack(mine, [size] * groups, width // devices, units, "unpack_experts", [before] + shared_mine)
     return (
         layer_out.reshape(tokens.shape),
         grad_tokens.reshape(tokens.shape),

time: 664 us -> 645 us (0.971)
  waiting for transfers between devices: 323 us -> 301 us
    ppermute x4 -> x6, waiting for transfers between devices: 67.1 us -> 31 us  [the longest x2 21.1 us: over_owners(): came = lax.ppermute(before, 'expert', [(i, i ^ k) for i in range(owners)])]
    reduce_scatter x2, waiting for transfers between devices: 0.01 us -> 10.3 us  [on_device(): lax.psum_scatter(tie(field[0], *(backs[h - 1:h] if h else arrived[1:])),...]
  transfers between devices with their start and end apart: 17 -> 19, of which waited for: 12 -> 13; matrix products, arithmetic and copies ran while one was open for 5% -> 4% of each run, Pallas kernels for 37% -> 39%
where the time goes in v5:
time: 645 us; the launch traced here: 636 us
  waiting for transfers between devices  301 us (47%)
  Pallas kernels  247 us (38%)
  starting transfers between devices  29.3 us (5%)
  local copies, waits for them, and re-layouts  20.9 us (3%)
  other arithmetic  14.7 us (2%)
  between operations  14.3 us (2%)
  blocking collectives  8.63 us (1%)
    pallas_call x3, Pallas kernels, feed(): pl.pallas_call(skipping(functools.partial(feed_kernel, gated, packed), in...  141 us
    all_to_all x2, waiting for transfers between devices, on_device(): lax.all_to_all(tie(results, *(backs[-1:] if h else arrived[1:])), 'expert...  88.3 us
    all_to_all x3, waiting for transfers between devices, trade(): lax.all_to_all(field.reshape(owners, field.shape[1], batch * CAP, width),...  68.5 us
    ppermute x3, waiting for transfers between devices, send(): return lax.ppermute(field, 'dp', [(i, step(i)) for i in range(8)])  58.3 us
    pallas_call x1, Pallas kernels, on_device(): pl.pallas_call(functools.partial(backward_kernel, experts, groups), grid=...  52.9 us
    pallas_call x1, Pallas kernels, on_device(): pl.pallas_call(functools.partial(forward_kernel, experts), grid=(batch,),...  31.3 us
    all_gather x2, waiting for transfers between devices, on_device(): lax.all_gather(pack(h * size, size, pool, (shared_gate, shared_up, shared...  22.3 us
    all_gather x1, waiting for transfers between devices, on_device(): first_all = lax.all_gather(first_part, 'dp', axis=0, tiled=True)  21.8 us
  transfers between devices with their start and end apart: 19, of which 13 were waited for; matrix products, arithmetic and copies ran while one was open for 4% of the time, Pallas kernels for 39%

profile of v5, /device:TPU:0, one launch (start us, length us, event | category | flops | bytes accessed | tf_op | source)
XLA Modules:
  0.0 635.7 jit_solution(9861474500295325350)
XLA Ops:
  11.6 4.2 pack.2
  17.8 5.0 dispatch.1
  22.8 6.5 %all-to-all-start.1 = ((bf16[4,4,160,768]{3,2,1,0:T(8,128)(2,1)}), bf16[4,4,160,768]{3,2,1,0:T(8,128)(2,1)}, u32[]{:S(2)}, u32[]{:S(2)}) async-start(bf16[4,4,160,768]{3,2,1,0:T(8,128)(2,1)} %bitcast.61), calls=%async_computation.1 | async-start | bytes 7864320 | tf_op jit(solution)/shard_map/all_to_all | solution.py:512
  32.2 21.8 %all-gather.6.cloned.1.call-done.weight_ref = bf16[768,3200]{1,0:T(8,128)(2,1)} async-done(((bf16[96,3200]{1,0:T(8,128)(2,1)}), bf16[768,3200]{1,0:T(8,128)(2,1)}) %all-gather.6.cloned.1.call-update) | async-done | bytes 4915216 | tf_op jit(solution)/shard_map/all_gather | solution.py:490
  55.8 31.3 %attention.1 = (f32[4,256,768]{2,1,0:T(8,128)}, bf16[4,256,768]{2,1,0:T(8,128)(2,1)}, bf16[4,256,768]{2,1,0:T(8,128)(2,1)}, bf16[4,256,2304]{2,1,0:T(8,128)(2,1)...) custom-call(bf16[4,256,768]{2,1,0:T(8,128)(2,1)} %bitcast.89, ...), custom_call_target="tpu_custom_call" | custom-call | flops 7650410496 | bytes 20643840 | tf_op jit(solution)/shard_map/attention/pallas_call | solution.py:558
  89.3 27.8 %all-to-all-done.1.refs_1_ = bf16[4,4,160,768]{3,2,1,0:T(8,128)(2,1)} async-done(((bf16[4,4,160,768]{3,2,1,0:T(8,128)(2,1)}), bf16[4,4,160,768]{3,2,1,0:T(8,128)(2,1)}, u32[]{:S(2)}, u32[]{:S(2)}) %all-to-all-start.1) | async-done | bytes 3932192 | tf_op jit(solution)/shard_map/all_to_all | solution.py:512
  117.1 8.6 %all_to_all.30.refs_2_ = f32[4,4,1,160]{3,2,1,0:T(1,128)} all-to-all(f32[4,4,1,160]{3,2,1,0:T(1,128)S(1)} %reshape.138), channel_id=1, replica_groups=mesh['dp'=8,'expert'=4] {'expert'}, dimensions={0} | all-to-all | bytes 20480 | tf_op jit(solution)/shard_map/all_to_all | solution.py:580
  125.7 3.6 all-to-all-start
  129.4 2.9 pack.3
  132.3 40.7 %all-to-all-done.refs_0_ = bf16[4,2,160,768]{3,2,1,0:T(8,128)(2,1)S(1)} async-done(((bf16[4,2,160,768]{3,2,1,0:T(8,128)(2,1)}), bf16[4,2,160,768]{3,2,1,0:T(8,128)(2,1)S(1)}, u32[]{:S(2)}, u32[]{:S(2)}) %all-to-all-start) | async-done | bytes 1966112 | tf_op jit(solution)/shard_map/all_to_all | solution.py:512
  173.0 4.8 all-to-all-start.3
  177.7 16.7 %all-gather.8.cloned.1.call-done = bf16[24,3,2,768,128]{4,3,2,1,0:T(8,128)(2,1)} async-done(((bf16[3,3,2,768,128]{4,3,2,1,0:T(8,128)(2,1)}), bf16[24,3,2,768,128]{4,3,2,1,0:T(8,128)(2,1)}) %all-gather.8.cloned.1.call-update) | async-done | bytes 28311568 | tf_op jit(solution)/shard_map/all_gather | solution.py:493
  194.5 50.6 %experts.2 = (bf16[4,2,2,160,768]{4,3,2,1,0:T(8,128)(2,1)}, bf16[8,3,3,2,768,128]{5,4,3,2,1,0:T(8,128)(2,1)}) custom-call(bf16[4,2,160,768]{3,2,1,0:T(8,128)(2,1)} %copy-done.3, bf16[4,4,160,768]{3,2,1,0:T(8,128)(2,1)} %all-to-all-done.1.refs_1_, f32[4,4,1,160]{3,2,1,0:T(1,128)} %all_to_all.30.refs_2_, bf16[8,3,3,2,768,128]{5,4,3,2,1,0:T(8,128)(2,1)} %bitcast.86), custom_call_target="tpu_custom_call" | custom-call | flops 724775731200 | bytes 45613056 | tf_op jit(solution)/shard_map/experts/pallas_call | solution.py:450
  245.0 4.8 all-to-all-start.4
  249.9 40.0 %shared.1 = (f32[1,1,1024,768]{3,2,1,0:T(8,128)}, f32[1,1,1024,768]{3,2,1,0:T(8,128)}, bf16[8,3,3,2,768,128]{5,4,3,2,1,0:T(8,128)(2,1)}) custom-call(bf16[1,1,1024,768]{3,2,1,0:T(8,128)(2,1)} %bitcast.95, bf16[1,1,1024,768]{3,2,1,0:T(8,128)(2,1)} %bitcast.70, bf16[8,3,3,2,768,128]{5,4,3,2,1,0:T(8,128)(2,1)} %bitcast.87, ...), custom_call_target="tpu_custom_call", output_to_operand_aliasing={{2}: (3, {})} | custom-call | flops 579820584960 | bytes 25165824 | tf_op jit(solution)/shard_map/shared/pallas_call | solution.py:450
  290.0 5.6 all-gather.10.cloned.1.call-done
  295.6 50.6 %experts.3 = (bf16[4,2,2,160,768]{4,3,2,1,0:T(8,128)(2,1)}, bf16[8,2,3,2,768,128]{5,4,3,2,1,0:T(8,128)(2,1)}) custom-call(bf16[4,2,160,768]{3,2,1,0:T(8,128)(2,1)} %all-to-all-done.3.refs_4_.refs_1_.refs_0_, bf16[4,4,160,768]{3,2,1,0:T(8,128)(2,1)} %all-to-all-done.1.refs_1_, f32[4,4,1,160]{3,2,1,0:T(1,128)} %all_to_all.30.refs_2_, ...), custom_call_target="tpu_custom_call" | custom-call | flops 724775731200 | bytes 45613056 | tf_op jit(solution)/shard_map/experts/pallas_call | solution.py:450
  346.2 5.1 all-to-all-start.5
  351.3 88.3 %all-to-all-done.5 = bf16[4,2,2,160,768]{4,3,2,1,0:T(8,128)(2,1)} async-done(((bf16[4,2,2,160,768]{4,3,2,1,0:T(8,128)(2,1)}), bf16[4,2,2,160,768]{4,3,2,1,0:T(8,128)(2,1)}, u32[]{:S(2)}, u32[]{:S(2)}) %all-to-all-start.5) | async-done | bytes 3932192 | tf_op jit(solution)/shard_map/all_to_all | solution.py:587
  439.6 52.9 %attention_back.1 = (bf16[4,256,768]{2,1,0:T(8,128)(2,1)}, f32[4,256,768]{2,1,0:T(8,128)}, bf16[768,3200]{1,0:T(8,128)(2,1)}) custom-call(bf16[4,256,768]{2,1,0:T(8,128)(2,1)} %bitcast.90, bf16[4,256,768]{2,1,0:T(8,128)(2,1)} %bitcast.71, s32[4,256,1]{2,1,0:T(8,128)} %broadcast_in_dim_reshape.5.column_ref, s32[4,1,256]{2,1,0:T(1,128)} %row_ref.3, ...), custom_call_target="tpu_custom_call" | custom-call | flops 15300820992 | bytes 34996224 | tf_op jit(solution)/shard_map/attention_back/pallas_call | solution.py:598
  492.5 3.8 dynamic-slice_bitcast_fusion
  498.0 6.8 %collective-permute-done = bf16[4,96,3200]{2,1,0:T(8,128)(2,1)} collective-permute-done((bf16[4,96,3200]{2,1,0:T(8,128)(2,1)}, bf16[4,96,3200]{2,1,0:T(8,128)(2,1)}, u32[]{:S(2)}, u32[]{:S(2)}) %collective-permute-start) | collective-permute-done | bytes 2457632 | tf_op jit(solution)/shard_map/ppermute | solution.py:60
  504.7 3.5 fusion
  511.3 2.6 collective-permute-done.5
  516.2 28.0 %collective-permute-done.1 = bf16[2,96,3200]{2,1,0:T(8,128)(2,1)} collective-permute-done((bf16[2,96,3200]{2,1,0:T(8,128)(2,1)S(1)}, bf16[2,96,3200]{2,1,0:T(8,128)(2,1)}, u32[]{:S(2)}, u32[]{:S(2)}) %collective-permute-start.1) | collective-permute-done | bytes 1228832 | tf_op jit(solution)/shard_map/ppermute | solution.py:60
  547.8 23.6 %collective-permute-done.2 = bf16[96,3200]{1,0:T(8,128)(2,1)} collective-permute-done((bf16[96,3200]{1,0:T(8,128)(2,1)}, bf16[96,3200]{1,0:T(8,128)(2,1)}, u32[]{:S(2)}, u32[]{:S(2)}) %collective-permute-start.2) | collective-permute-done | bytes 614432 | tf_op jit(solution)/shard_map/ppermute | solution.py:60
  573.1 2.1 collective-permute-start.8
  575.1 21.1 %collective-permute-done.3 = bf16[96,3200]{1,0:T(8,128)(2,1)S(1)} collective-permute-done((bf16[96,3200]{1,0:T(8,128)(2,1)S(1)}, bf16[96,3200]{1,0:T(8,128)(2,1)S(1)}, u32[]{:S(2)}, u32[]{:S(2)}) %collective-permute-start.3) | collective-permute-done | bytes 614432 | tf_op jit(solution)/shard_map/ppermute | solution.py:632
  596.5 7.3 %collective-permute-done.8 = bf16[2304,128]{1,0:T(8,128)(2,1)S(1)} collective-permute-done((bf16[2304,128]{1,0:T(8,128)(2,1)S(1)}, bf16[2304,128]{1,0:T(8,128)(2,1)S(1)}, u32[]{:S(2)}, u32[]{:S(2)}) %collective-permute-start.8) | collective-permute-done | bytes 589856 | tf_op jit(solution)/shard_map/ppermute | solution.py:640
  605.1 2.9 unpack_shared.1
  608.0 10.3 %reduce-scatter.5.cloned.1.call-done = bf16[1,2,3,2,768,128]{5,4,3,2,1,0:T(8,128)(2,1)} async-done(((bf16[8,2,3,2,768,128]{5,4,3,2,1,0:T(8,128)(2,1)}), bf16[1,2,3,2,768,128]{5,4,3,2,1,0:T(8,128)(2,1)}) %reduce-scatter.5.cloned.1.call-update) | async-done | bytes 2359312 | tf_op jit(solution)/shard_map/reduce_scatter | solution.py:656
  618.3 7.0 %unpack_experts.1 = (f32[4,96,2048]{2,1,0:T(8,128)}, f32[4,96,2048]{2,1,0:T(8,128)}, f32[4,256,768]{2,1,0:T(8,128)}) custom-call(bf16[3,3,2,768,128]{4,3,2,1,0:T(8,128)(2,1)} %bitcast.60, bf16[2,3,2,768,128]{4,3,2,1,0:T(8,128)(2,1)} %bitcast.67, bf16[96,3200]{1,0:T(8,128)(2,1)} %copy-done.1, f32[96,2048]{1,0:T(8,128)} %bitcast.72, f32[96,2048]{1,0:T(8,128)} %bitcast.74, ...), custom_call_target="tpu_custom_call" | custom-call | tf_op jit(solution)/shard_map/unpack_experts/pallas_call | solution.py:328
  (93 shorter events, 30.9 us)
Async XLA Ops:
  7.2 46.9 %all-gather.6.cloned.1.call-start = ((), (), s32[]{:S(2)}) async-start(), calls=%async_computation.8 | async-start | bytes 5529600 | tf_op jit(solution)/shard_map/all_gather | solution.py:490
  11.6 182.9 %all-gather.8.cloned.1.call-start = ((), (), s32[]{:S(2)}) async-start(), calls=%async_computation.11 | async-start | bytes 31850496 | tf_op jit(solution)/shard_map/all_gather | solution.py:493
  15.8 0.7 copy-start.5
  15.8 0.9 copy-start.6
  17.0 15.1 %copy-start.2 = (s32[4,1,256,2]{3,2,0,1:T(8,128)}, s32[4,1,256,2]{3,2,0,1:T(8,128)S(1)}, u32[]{:S(2)}) copy-start(s32[4,1,256,2]{3,2,0,1:T(8,128)S(1)} %copy.98) | copy-start | bytes 24580
  22.8 6.5 %copy-start.7 = (s32[4,1,256]{2,1,0:T(1,128)S(1)}, s32[4,1,256]{2,1,0:T(1,128)}, u32[]{:S(2)}) copy-start(s32[4,1,256]{2,1,0:T(1,128)} %row_ref.3) | copy-start | bytes 12292
  22.8 94.3 %all-to-all-start.1 = ((bf16[4,4,160,768]{3,2,1,0:T(8,128)(2,1)}), bf16[4,4,160,768]{3,2,1,0:T(8,128)(2,1)}, u32[]{:S(2)}, u32[]{:S(2)}) async-start(bf16[4,4,160,768]{3,2,1,0:T(8,128)(2,1)} %bitcast.61), calls=%async_computation.1 | async-start | bytes 7864320 | tf_op jit(solution)/shard_map/all_to_all | solution.py:512
  55.8 32.5 %copy-start.4 = (s32[4,2,256]{2,1,0:T(2,128)S(1)}, s32[4,2,256]{2,1,0:T(2,128)}, u32[]{:S(2)}) copy-start(s32[4,2,256]{2,1,0:T(2,128)} %copy.114.flat_ref) | copy-start | bytes 24580
  125.7 47.2 %all-to-all-start = ((bf16[4,2,160,768]{3,2,1,0:T(8,128)(2,1)}), bf16[4,2,160,768]{3,2,1,0:T(8,128)(2,1)S(1)}, u32[]{:S(2)}, u32[]{:S(2)}) async-start(bf16[4,2,160,768]{3,2,1,0:T(8,128)(2,1)} %bitcast.68), calls=%async_computation | async-start | bytes 3932160 | tf_op jit(solution)/shard_map/all_to_all | solution.py:512
  129.3 166.2 %all-gather.10.cloned.1.call-start = ((), (), s32[]{:S(2)}) async-start(), calls=%async_computation.12 | async-start | bytes 21233664 | tf_op jit(solution)/shard_map/all_gather | solution.py:493
  173.0 21.5 %copy-start.3 = (bf16[4,2,160,768]{3,2,1,0:T(8,128)(2,1)}, bf16[4,2,160,768]{3,2,1,0:T(8,128)(2,1)S(1)}, u32[]{:S(2)}) copy-start(bf16[4,2,160,768]{3,2,1,0:T(8,128)(2,1)S(1)} %all-to-all-done.refs_0_) | copy-start | bytes 5898244
  173.0 72.0 %all-to-all-start.3 = ((bf16[4,2,160,768]{3,2,1,0:T(8,128)(2,1)}), bf16[4,2,160,768]{3,2,1,0:T(8,128)(2,1)}, u32[]{:S(2)}, u32[]{:S(2)}) async-start(bf16[4,2,160,768]{3,2,1,0:T(8,128)(2,1)} %bitcast.17), calls=%async_computation.3 | async-start | bytes 3932160 | tf_op jit(solution)/shard_map/all_to_all | solution.py:512
  245.0 101.1 %all-to-all-start.4 = ((bf16[4,2,2,160,768]{4,3,2,1,0:T(8,128)(2,1)}), bf16[4,2,2,160,768]{4,3,2,1,0:T(8,128)(2,1)}, u32[]{:S(2)}, u32[]{:S(2)}) async-start(bf16[4,2,2,160,768]{4,3,2,1,0:T(8,128)(2,1)} %tie.5), calls=%async_computation.4 | async-start | bytes 7864320 | tf_op jit(solution)/shard_map/all_to_all | solution.py:587
  249.9 242.6 %reduce-scatter.3.cloned.1.call-start = ((), (), s32[]{:S(2)}) async-start(), calls=%async_computation.9 | async-start | bytes 31850496 | tf_op jit(solution)/shard_map/reduce_scatter | solution.py:656
  289.9 328.4 %reduce-scatter.5.cloned.1.call-start = ((), (), s32[]{:S(2)}) async-start(), calls=%async_computation.10 | async-start | bytes 21233664 | tf_op jit(solution)/shard_map/reduce_scatter | solution.py:656
  346.2 93.4 %all-to-all-start.5 = ((bf16[4,2,2,160,768]{4,3,2,1,0:T(8,128)(2,1)}), bf16[4,2,2,160,768]{4,3,2,1,0:T(8,128)(2,1)}, u32[]{:S(2)}, u32[]{:S(2)}) async-start(bf16[4,2,2,160,768]{4,3,2,1,0:T(8,128)(2,1)} %tie.6), calls=%async_computation.5 | async-start | bytes 7864320 | tf_op jit(solution)/shard_map/all_to_all | solution.py:587
  496.3 8.4 %collective-permute-start = (bf16[4,96,3200]{2,1,0:T(8,128)(2,1)}, bf16[4,96,3200]{2,1,0:T(8,128)(2,1)}, u32[]{:S(2)}, u32[]{:S(2)}) collective-permute-start(bf16[4,96,3200]{2,1,0:T(8,128)(2,1)} %dynamic-slice_bitcast_fusion), channel_id=1, source_target_pairs={{0,4},{4,0},{8,12},{12,8},{16,20},{20,16},{24,28},{28,24},{1,5},{5... | collective-permute-start | bytes 7372808 | tf_op jit(solution)/shard_map/ppermute | solution.py:60
  497.9 16.0 %collective-permute-start.5 = (bf16[2304,128]{1,0:T(8,128)(2,1)S(1)}, bf16[2304,128]{1,0:T(8,128)(2,1)}, u32[]{:S(2)}, u32[]{:S(2)}) collective-permute-start(bf16[2304,128]{1,0:T(8,128)(2,1)S(1)} %constant_dynamic-slice_fusion.1), channel_id=1, source_target_pairs={{0,1},{1,0},{2,3},{3,2},{4,5},{5,4},{6,7},{7,6},{8,9},{9,8},{10,11... | collective-permute-start | bytes 1769480 | tf_op jit(solution)/shard_map/ppermute | solution.py:640
  508.3 1.4 copy-start
  509.7 34.5 %collective-permute-start.1 = (bf16[2,96,3200]{2,1,0:T(8,128)(2,1)S(1)}, bf16[2,96,3200]{2,1,0:T(8,128)(2,1)}, u32[]{:S(2)}, u32[]{:S(2)}) collective-permute-start(bf16[2,96,3200]{2,1,0:T(8,128)(2,1)S(1)} %pad_maximum_fusion), channel_id=1, source_target_pairs={{0,8},{4,20},{8,0},{12,28},{16,24},{20,4},{24,16},{28,12},{1,9},{5... | collective-permute-start | bytes 3686408 | tf_op jit(solution)/shard_map/ppermute | solution.py:60
  515.9 31.8 %collective-permute-start.6 = (bf16[1152,128]{1,0:T(8,128)(2,1)}, bf16[1152,128]{1,0:T(8,128)(2,1)S(1)}, u32[]{:S(2)}, u32[]{:S(2)}) collective-permute-start(bf16[1152,128]{1,0:T(8,128)(2,1)} %constant_dynamic-slice_fusion), channel_id=1, source_target_pairs={{0,2},{1,3},{2,0},{3,1},{4,6},{5,7},{6,4},{7,5},{8,10},{9,11},{10,... | collective-permute-start | bytes 884744 | tf_op jit(solution)/shard_map/ppermute | solution.py:640
  547.6 23.8 %collective-permute-start.2 = (bf16[96,3200]{1,0:T(8,128)(2,1)}, bf16[96,3200]{1,0:T(8,128)(2,1)}, u32[]{:S(2)}, u32[]{:S(2)}) collective-permute-start(bf16[96,3200]{1,0:T(8,128)(2,1)} %fusion.5), channel_id=1, source_target_pairs={{0,16},{4,12},{8,24},{12,4},{16,0},{20,28},{24,8},{28,20},{1,17},{... | collective-permute-start | bytes 1843208 | tf_op jit(solution)/shard_map/ppermute | solution.py:60
  547.7 25.2 %collective-permute-start.7 = (bf16[1152,128]{1,0:T(8,128)(2,1)S(1)}, bf16[1152,128]{1,0:T(8,128)(2,1)S(1)}, u32[]{:S(2)}, u32[]{:S(2)}) collective-permute-start(bf16[1152,128]{1,0:T(8,128)(2,1)S(1)} %add_convert_fusion.2), channel_id=1, source_target_pairs={{0,2},{1,3},{2,0},{3,1},{4,6},{5,7},{6,4},{7,5},{8,10},{9,11},{10,... | collective-permute-start | bytes 884744 | tf_op jit(solution)/shard_map/ppermute | solution.py:640
  572.9 23.4 %collective-permute-start.3 = (bf16[96,3200]{1,0:T(8,128)(2,1)S(1)}, bf16[96,3200]{1,0:T(8,128)(2,1)S(1)}, u32[]{:S(2)}, u32[]{:S(2)}) collective-permute-start(bf16[96,3200]{1,0:T(8,128)(2,1)S(1)} %fusion.3), channel_id=1, source_target_pairs={{0,1},{1,0},{2,3},{3,2},{4,5},{5,4},{6,7},{7,6},{8,9},{9,8},{10,11... | collective-permute-start | bytes 1843208 | tf_op jit(solution)/shard_map/ppermute | solution.py:632
  573.1 30.7 %collective-permute-start.8 = (bf16[2304,128]{1,0:T(8,128)(2,1)S(1)}, bf16[2304,128]{1,0:T(8,128)(2,1)S(1)}, u32[]{:S(2)}, u32[]{:S(2)}) collective-permute-start(bf16[2304,128]{1,0:T(8,128)(2,1)S(1)} %pad_maximum_fusion.2), channel_id=1, source_target_pairs={{0,1},{1,0},{2,3},{3,2},{4,5},{5,4},{6,7},{7,6},{8,9},{9,8},{10,11... | collective-permute-start | bytes 1769480 | tf_op jit(solution)/shard_map/ppermute | solution.py:640
  596.4 21.9 %copy-start.1 = (bf16[96,3200]{1,0:T(8,128)(2,1)}, bf16[96,3200]{1,0:T(8,128)(2,1)S(1)}, u32[]{:S(2)}) copy-start(bf16[96,3200]{1,0:T(8,128)(2,1)S(1)} %add_convert_fusion.refs_2_) | copy-start | bytes 1843204
  596.4 28.9 %collective-permute-start.4 = (bf16[96,3200]{1,0:T(8,128)(2,1)S(1)}, bf16[96,3200]{1,0:T(8,128)(2,1)S(1)}, u32[]{:S(2)}, u32[]{:S(2)}) collective-permute-start(bf16[96,3200]{1,0:T(8,128)(2,1)S(1)} %add_convert_fusion.refs_2_), channel_id=1, source_target_pairs={{0,2},{1,3},{2,0},{3,1},{4,6},{5,7},{6,4},{7,5},{8,10},{9,11},{10,... | collective-permute-start | bytes 1843208 | tf_op jit(solution)/shard_map/ppermute | solution.py:632
Sparse Core Ops, SparseCore 0:
  11.7 42.3 all-gather.5
  55.9 138.4 all-gather.7
  196.9 98.5 all-gather.9
  299.1 175.4 reduce-scatter.2
  478.0 140.2 reduce-scatter.4

commit v6 on v5

--- a/solution.py
+++ b/solution.py
@@ -120,6 +120,10 @@
     return lax.rsqrt(jnp.mean(field * field, axis=-1, keepdims=True) + EPSILON)
 
 
+def pair_columns(pair, width):
+    return [pl.ds(pl.multiple_of(n * width + pair * PAIR, PAIR), PAIR) for n in range(3)]
+
+
 def forward_kernel(
     experts, tokens_ref, column_ref, row_ref, flat_ref, weight_ref, gain_one_ref, gain_two_ref, cosine_ref, sine_ref,
     hidden_ref, mixed_ref, attended_ref, qkv_ref, logsum_ref, router_ref, *outs,
@@ -132,14 +136,14 @@
     low = iota((x.shape[0], PAIR), 1) < HEAD_DIM
     lane = iota((x.shape[0], LANES), 1)
     logsum = jnp.zeros((x.shape[0], LANES), F32)
-    for pair in range(width // PAIR):
-        at = slice(pair * PAIR, (pair + 1) * PAIR)
+    def head_pair(pair, logsum):
+        at, key_at, value_at = pair_columns(pair, width)
         query = turn(mm(normed, weight_ref[:, at], NN), cosine, sine).astype(BF16) * BF16(0.125)
-        key = turn(mm(normed, weight_ref[:, width + at.start : width + at.stop], NN), cosine, sine).astype(BF16)
-        value = mm(normed, weight_ref[:, 2 * width + at.start : 2 * width + at.stop], NN).astype(BF16)
+        key = turn(mm(normed, weight_ref[:, key_at], NN), cosine, sine).astype(BF16)
+        value = mm(normed, weight_ref[:, value_at], NN).astype(BF16)
         qkv_ref[0, :, at] = query
-        qkv_ref[0, :, width + at.start : width + at.stop] = key
-        qkv_ref[0, :, 2 * width + at.start : 2 * width + at.stop] = value
+        qkv_ref[0, :, key_at] = key
+        qkv_ref[0, :, value_at] = value
         both = []
         for half in range(2):
             mine = low if half == 0 else jnp.logical_not(low)
@@ -150,6 +154,9 @@
             logsum = jnp.where(lane == 2 * pair + half, peak + jnp.log(total), logsum)
             both.append(mm((expo * (1.0 / total)).astype(BF16), value, NN))
         attended_ref[0, :, at] = jnp.where(low, both[0], both[1]).astype(BF16)
+        return logsum
+
+    logsum = lax.fori_loop(0, width // PAIR, head_pair, logsum)
     logsum_ref[0] = logsum
     hidden = x + mm(attended_ref[0], weight_ref[:, 3 * width : 4 * width], NN)
     hidden_ref[0] = hidden
@@ -174,7 +181,7 @@
     cosine_ref, sine_ref, hidden_ref, mixed_ref, attended_ref, qkv_ref, logsum_ref, router_ref, shared_ref, d_mixed_ref, *refs,
 ):
     backs = refs[:groups]
-    out_ref, grad_tokens_ref, grad_weight_ref, held_ref, sum_ref, gains_ref, d_qkv_ref = refs[groups:]
+    out_ref, grad_tokens_ref, grad_weight_ref, held_ref, sum_ref, gains_ref, d_qkv_ref, d_attended_ref = refs[groups:]
     width = tokens_ref.shape[2]
     step = pl.program_id(0)
 
@@ -216,32 +223,32 @@
     d_hidden = grad + inverse_two * (scaled - unit_two * jnp.mean(scaled * unit_two, axis=-1, keepdims=True))
     d_branch = d_hidden.astype(BF16)
     sum_ref[:, 3 * width : 4 * width] += mm(attended_ref[0], d_branch, TN)
-    d_attended = mm(d_branch, weight_ref[:, 3 * width : 4 * width], NT).astype(BF16)
+    d_attended_ref[...] = mm(d_branch, weight_ref[:, 3 * width : 4 * width], NT).astype(BF16)
 
     allowed = allowed_of(column_ref, row_ref)
     cosine, sine = cosine_ref[...], -sine_ref[...]
     low = iota((length, PAIR), 1) < HEAD_DIM
     logsum = logsum_ref[0]
-    for pair in range(width // PAIR):
-        at = slice(pair * PAIR, (pair + 1) * PAIR)
-        query = qkv_ref[0, :, at]
-        key = qkv_ref[0, :, width + at.start : width + at.stop]
-        value = qkv_ref[0, :, 2 * width + at.start : 2 * width + at.stop]
-        d_out = d_attended[:, at]
+    def head_pair(pair, carry):
+        at, key_at, value_at = pair_columns(pair, width)
+        query, key, value = qkv_ref[0, :, at], qkv_ref[0, :, key_at], qkv_ref[0, :, value_at]
+        d_out = d_attended_ref[:, at]
         parts = []
         for half in range(2):
             mine = low if half == 0 else jnp.logical_not(low)
             scores = jnp.where(allowed, mm(jnp.where(mine, query, BF16(0.0)), key, NT), -1e30)
-            head = 2 * pair + half
-            probs = jnp.exp(scores - logsum[:, head : head + 1])
+            head = jnp.sum(jnp.where(lane == 2 * pair + half, logsum, 0.0), axis=-1, keepdims=True)
+            probs = jnp.exp(scores - head)
             d_probs = mm(jnp.where(mine, d_out, BF16(0.0)), value, NT)
             d_scores = (probs * (d_probs - jnp.sum(probs * d_probs, axis=-1, keepdims=True))).astype(BF16)
             parts.append((mm(d_scores, key, NN), mm(d_scores, query, TN), mm(probs.astype(BF16), d_out, TN)))
         d_query, d_key, d_value = (jnp.where(low, a, b) for a, b in zip(*parts))
         d_qkv_ref[:, at] = turn(d_query * 0.125, cosine, sine).astype(BF16)
-        d_qkv_ref[:, width + at.start : width + at.stop] = turn(d_key, cosine, sine).astype(BF16)
-        d_qkv_ref[:, 2 * width + at.start : 2 * width + at.stop] = d_value.astype(BF16)
-
+        d_qkv_ref[:, key_at] = turn(d_key, cosine, sine).astype(BF16)
+        d_qkv_ref[:, value_at] = d_value.astype(BF16)
+        return carry
+
+    lax.fori_loop(0, width // PAIR, head_pair, 0)
     x = tokens_ref[0].astype(F32)
     inverse_one = inverse_rms(x)
     unit_one = x * inverse_one
@@ -262,17 +269,24 @@
         grad_weight_ref[:, 4 * width :] = (sum_ref[:, 4 * width :] + gains.T).astype(BF16)
 
 
-def pack_pieces(packed, gate, up, down):
+def for_pieces(move, packed, gate, up, down):
     steps, width = packed.shape[1], packed.shape[2]
     rows = gate.shape[0]
     for f in range(steps):
-        for j in range(width // rows):
-            at = slice((j * steps + f) * LANES, (j * steps + f + 1) * LANES)
-            yield packed.at[0, f, j * rows : (j + 1) * rows], gate.at[:, at]
-            yield packed.at[1, f, j * rows : (j + 1) * rows], up.at[:, at]
-        for c in range(width // LANES):
-            at = slice(c * LANES, (c + 1) * LANES)
-            yield packed.at[2, f, at], down.at[f * LANES : (f + 1) * LANES, at]
+        def block(j, carry):
+            own = pl.ds(pl.multiple_of(j * rows, rows), rows)
+            at = pl.ds(pl.multiple_of((j * steps + f) * LANES, LANES), LANES)
+            move(packed.at[0, f, own], gate.at[:, at])
+            move(packed.at[1, f, own], up.at[:, at])
+            return carry
+
+        def chunk(c, carry):
+            at = pl.ds(pl.multiple_of(c * LANES, LANES), LANES)
+            move(packed.at[2, f, at], down.at[f * LANES : (f + 1) * LANES, at])
+            return carry
+
+        lax.fori_loop(0, width // rows, block, 0)
+        lax.fori_loop(0, width // LANES, chunk, 0)
 
 
 def pack_kernel(count, *refs):
@@ -281,8 +295,10 @@
     for n in range((len(refs) - 1) // 3):
         @pl.when((step < count) if n == 0 else (step >= count))
         def _():
-            for to, source in pack_pieces(out, *refs[3 * n : 3 * n + 3]):
-                to[...] = source[...]
+            def move(piece, source):
+                piece[...] = source[...]
+
+            for_pieces(move, out, *refs[3 * n : 3 * n + 3])
 
 
 def pack(first, count, pool, shared, devices):
@@ -303,36 +319,27 @@
     )(*pool, *shared)
 
 
-def unpack_kernel(sizes, *refs):
-    packs, outs = refs[: len(sizes)], refs[len(sizes) :]
-    step = pl.program_id(0)
-    start = 0
-    for n, size in enumerate(sizes):
-        @pl.when(jnp.logical_and(step >= start, step < start + size))
-        def _(source=packs[n]):
-            for piece, to in pack_pieces(source, *outs):
-                to[...] = piece[...].astype(F32)
-        start += size
-
-
-def unpack(packs, sizes, rows, units, name, after=()):
+def unpack_kernel(packed, *outs):
+    def move(piece, to):
+        to[...] = piece[...].astype(F32)
+
+    for_pieces(move, packed, *outs)
+
+
+def unpack(packed, size, first, total, rows, units, name, after=(), carried=()):
     squeezed = pl.Squeezed()
-    specs, start = [], 0
-    for field, size in zip(packs, sizes):
-        specs.append(pl.BlockSpec(
-            (squeezed,) + field.shape[1:],
-            lambda l, start=start, size=size: (jnp.clip(l - start, 0, size - 1), 0, 0, 0, 0)))
-        start += size
-    width = packs[0].shape[3]
+    width = packed.shape[3]
     shapes = [(rows, units), (rows, units), (rows * units // width, width)]
+    unread = list(after) + list(carried)
     return pl.pallas_call(
-        skipping(functools.partial(unpack_kernel, tuple(sizes)), len(packs), len(after)),
-        grid=(start,),
-        in_specs=specs + [ANY] * len(after),
-        out_specs=[pl.BlockSpec((squeezed,) + shape, lambda l: (l, 0, 0)) for shape in shapes],
-        out_shape=[jax.ShapeDtypeStruct((start,) + shape, F32) for shape in shapes],
+        skipping(unpack_kernel, 1, len(unread)),
+        grid=(size,),
+        in_specs=[pl.BlockSpec((squeezed,) + packed.shape[1:], lambda l: (l, 0, 0, 0, 0))] + [ANY] * len(unread),
+        out_specs=[pl.BlockSpec((squeezed,) + shape, lambda l: (first + l, 0, 0)) for shape in shapes],
+        out_shape=[jax.ShapeDtypeStruct((total,) + shape, F32) for shape in shapes],
+        input_output_aliases={1 + len(after) + n: n for n in range(len(carried))},
         name=name,
-    )(*packs, *after)
+    )(packed, *unread)
 
 
 def feed_step(x, d, gate_weight, up_weight, down_weight, out, dx):
@@ -380,7 +387,7 @@
         field, total = weights[0], sums[0]
         devices = field.shape[0]
         rows = width // devices
-        size = min(devices, 4)
+        size = min(devices, 2)
         def half(n, carry):
             start = n * size
             chunks = [pl.ds(pl.multiple_of((start + j) * rows, rows), rows) for j in range(size)]
@@ -612,6 +619,7 @@
             pltpu.VMEM((width, columns), F32),
             pltpu.VMEM((8, width), F32),
             pltpu.VMEM((length, 3 * width), BF16),
+            pltpu.VMEM((length, width), BF16),
         ],
         compiler_params=params,
         cost_estimate=pl.CostEstimate(
@@ -656,7 +664,7 @@
             lax.psum_scatter(tie(field[0], *(backs[h - 1 : h] if h else arrived[1:])), "dp", scatter_dimension=0)
             for h, field in enumerate(sums)]
         shared_mine = unpack(
-            [over_owners_by_halves(mine[0][size].reshape(-1, LANES)).reshape(mine[0][size:].shape)], [1],
+            over_owners_by_halves(mine[0][size].reshape(-1, LANES)).reshape(mine[0][size:].shape), 1, 0, 1,
             width // devices, units, "unpack_shared")
         first_grad = tie(first_grad, mine[0])
         shared_mine = [field[0] for field in shared_mine]
@@ -672,7 +680,10 @@
     first_mine = scatter_rows(first_grad.reshape(devices, width // devices, columns))
     first_mine, before = over_owners(first_mine)
     if packed:
-        pool_mine = unpack(mine, [size] * groups, width // devices, units, "unpack_experts", [before] + shared_mine)
+        pool_mine = ()
+        for h, field in enumerate(mine):
+            pool_mine = unpack(
+                field, size, h * size, local_experts, width // devices, units, "unpack_experts", [before] + shared_mine, pool_mine)
     return (
         layer_out.reshape(tokens.shape),
         grad_tokens.reshape(tokens.shape),

time: 645 us -> 654 us (1.014); the launches traced: 636 us -> 652 us
  Pallas kernels: 247 us -> 275 us
  waiting for transfers between devices: 301 us -> 288 us
    pallas_call x3, Pallas kernels: 141 us -> 160 us  [feed(): pl.pallas_call(skipping(functools.partial(feed_kernel, gated, packed), in...]
    ppermute x4, waiting for transfers between devices: 9.84 us -> 24.5 us  [over_owners_by_halves(): lax.ppermute(part, 'expert', [(i, i ^ k) for i in range(owners)])]
    reduce_scatter x2, waiting for transfers between devices: 10.3 us -> 0.02 us  [on_device(): lax.psum_scatter(tie(field[0], *(backs[h - 1:h] if h else arrived[1:])),...]
    ppermute x2, waiting for transfers between devices: 21.1 us -> 14.5 us  [over_owners(): came = lax.ppermute(before, 'expert', [(i, i ^ k) for i in range(owners)])]
  transfers between devices with their start and end apart: 19 -> 19, of which waited for: 13 -> 11; matrix products, arithmetic and copies ran while one was open for 4% -> 4% of each run, Pallas kernels for 39% -> 42%
where the time goes in v6:
time: 654 us; the launch traced here: 652 us
  waiting for transfers between devices  288 us (44%)
  Pallas kernels  275 us (42%)
  starting transfers between devices  30.8 us (5%)
  local copies, waits for them, and re-layouts  20.4 us (3%)
  other arithmetic  15.4 us (2%)
  between operations  14.1 us (2%)
  blocking collectives  8.63 us (1%)
    pallas_call x3, Pallas kernels, feed(): pl.pallas_call(skipping(functools.partial(feed_kernel, gated, packed), in...  160 us
    all_to_all x2, waiting for transfers between devices, on_device(): lax.all_to_all(tie(results, *(backs[-1:] if h else arrived[1:])), 'expert...  88 us
    all_to_all x3, waiting for transfers between devices, trade(): lax.all_to_all(field.reshape(owners, field.shape[1], batch * CAP, width),...  63.6 us
    ppermute x3, waiting for transfers between devices, send(): return lax.ppermute(field, 'dp', [(i, step(i)) for i in range(8)])  58.8 us
    pallas_call x1, Pallas kernels, on_device(): pl.pallas_call(functools.partial(backward_kernel, experts, groups), grid=...  55.9 us
    pallas_call x1, Pallas kernels, on_device(): pl.pallas_call(functools.partial(forward_kernel, experts), grid=(batch,),...  36.3 us
    ppermute x4, waiting for transfers between devices, over_owners_by_halves(): lax.ppermute(part, 'expert', [(i, i ^ k) for i in range(owners)])  24.5 us
    all_gather x1, waiting for transfers between devices, on_device(): first_all = lax.all_gather(first_part, 'dp', axis=0, tiled=True)  21.4 us
  transfers between devices with their start and end apart: 19, of which 11 were waited for; matrix products, arithmetic and copies ran while one was open for 4% of the time, Pallas kernels for 42%

profile of v6, /device:TPU:0, one launch (start us, length us, event | category | flops | bytes accessed | tf_op | source)
XLA Modules:
  0.0 652.3 jit_solution(7514070999716213649)
XLA Ops:
  11.6 4.6 pack.2
  18.2 5.0 dispatch.1
  23.2 6.5 all-to-all-start.1
  32.6 21.4 %all-gather.6.cloned.1.call-done.weight_ref = bf16[768,3200]{1,0:T(8,128)(2,1)} async-done(((bf16[96,3200]{1,0:T(8,128)(2,1)}), bf16[768,3200]{1,0:T(8,128)(2,1)}) %all-gather.6.cloned.1.call-update) | async-done | bytes 4915216 | tf_op jit(solution)/shard_map/all_gather | solution.py:497
  55.8 36.3 %attention.1 = (f32[4,256,768]{2,1,0:T(8,128)}, bf16[4,256,768]{2,1,0:T(8,128)(2,1)}, bf16[4,256,768]{2,1,0:T(8,128)(2,1)}, bf16[4,256,2304]{2,1,0:T(8,128)(2,1)...) custom-call(bf16[4,256,768]{2,1,0:T(8,128)(2,1)} %bitcast.92, ...), custom_call_target="tpu_custom_call" | custom-call | flops 7650410496 | bytes 20643840 | tf_op jit(solution)/shard_map/attention/pallas_call | solution.py:565
  94.4 23.1 %all-to-all-done.1.refs_1_ = bf16[4,4,160,768]{3,2,1,0:T(8,128)(2,1)} async-done(((bf16[4,4,160,768]{3,2,1,0:T(8,128)(2,1)}), bf16[4,4,160,768]{3,2,1,0:T(8,128)(2,1)}, u32[]{:S(2)}, u32[]{:S(2)}) %all-to-all-start.1) | async-done | bytes 3932192 | tf_op jit(solution)/shard_map/all_to_all | solution.py:519
  117.5 8.6 %all_to_all.30.refs_2_ = f32[4,4,1,160]{3,2,1,0:T(1,128)} all-to-all(f32[4,4,1,160]{3,2,1,0:T(1,128)S(1)} %reshape.138), channel_id=1, replica_groups=mesh['dp'=8,'expert'=4] {'expert'}, dimensions={0} | all-to-all | bytes 20480 | tf_op jit(solution)/shard_map/all_to_all | solution.py:587
  126.1 3.6 all-to-all-start
  129.8 3.1 pack.3
  132.9 40.5 %all-to-all-done.refs_0_ = bf16[4,2,160,768]{3,2,1,0:T(8,128)(2,1)S(1)} async-done(((bf16[4,2,160,768]{3,2,1,0:T(8,128)(2,1)}), bf16[4,2,160,768]{3,2,1,0:T(8,128)(2,1)S(1)}, u32[]{:S(2)}, u32[]{:S(2)}) %all-to-all-start) | async-done | bytes 1966112 | tf_op jit(solution)/shard_map/all_to_all | solution.py:519
  173.3 4.4 all-to-all-start.3
  177.8 16.7 %all-gather.8.cloned.1.call-done = bf16[24,3,2,768,128]{4,3,2,1,0:T(8,128)(2,1)} async-done(((bf16[3,3,2,768,128]{4,3,2,1,0:T(8,128)(2,1)}), bf16[24,3,2,768,128]{4,3,2,1,0:T(8,128)(2,1)}) %all-gather.8.cloned.1.call-update) | async-done | bytes 28311568 | tf_op jit(solution)/shard_map/all_gather | solution.py:500
  194.5 57.5 %experts.2 = (bf16[4,2,2,160,768]{4,3,2,1,0:T(8,128)(2,1)}, bf16[8,3,3,2,768,128]{5,4,3,2,1,0:T(8,128)(2,1)}) custom-call(bf16[4,2,160,768]{3,2,1,0:T(8,128)(2,1)} %copy-done.2, bf16[4,4,160,768]{3,2,1,0:T(8,128)(2,1)} %all-to-all-done.1.refs_1_, f32[4,4,1,160]{3,2,1,0:T(1,128)} %all_to_all.30.refs_2_, bf16[8,3,3,2,768,128]{5,4,3,2,1,0:T(8,128)(2,1)} %bitcast.89), custom_call_target="tpu_custom_call" | custom-call | flops 724775731200 | bytes 45613056 | tf_op jit(solution)/shard_map/experts/pallas_call | solution.py:457
  252.0 4.8 all-to-all-start.4
  257.1 44.8 %shared.1 = (f32[1,1,1024,768]{3,2,1,0:T(8,128)}, f32[1,1,1024,768]{3,2,1,0:T(8,128)}, bf16[8,3,3,2,768,128]{5,4,3,2,1,0:T(8,128)(2,1)}) custom-call(bf16[1,1,1024,768]{3,2,1,0:T(8,128)(2,1)} %bitcast.98, bf16[1,1,1024,768]{3,2,1,0:T(8,128)(2,1)} %bitcast.79, bf16[8,3,3,2,768,128]{5,4,3,2,1,0:T(8,128)(2,1)} %bitcast.90, ...), custom_call_target="tpu_custom_call", output_to_operand_aliasing={{2}: (3, {})} | custom-call | flops 579820584960 | bytes 25165824 | tf_op jit(solution)/shard_map/shared/pallas_call | solution.py:457
  302.0 57.7 %experts.3 = (bf16[4,2,2,160,768]{4,3,2,1,0:T(8,128)(2,1)}, bf16[8,2,3,2,768,128]{5,4,3,2,1,0:T(8,128)(2,1)}) custom-call(bf16[4,2,160,768]{3,2,1,0:T(8,128)(2,1)} %all-to-all-done.3.refs_4_.refs_1_.refs_0_, bf16[4,4,160,768]{3,2,1,0:T(8,128)(2,1)} %all-to-all-done.1.refs_1_, f32[4,4,1,160]{3,2,1,0:T(1,128)} %all_to_all.30.refs_2_, ...), custom_call_target="tpu_custom_call" | custom-call | flops 724775731200 | bytes 45613056 | tf_op jit(solution)/shard_map/experts/pallas_call | solution.py:457
  359.7 5.1 all-to-all-start.5
  364.8 88.0 %all-to-all-done.5 = bf16[4,2,2,160,768]{4,3,2,1,0:T(8,128)(2,1)} async-done(((bf16[4,2,2,160,768]{4,3,2,1,0:T(8,128)(2,1)}), bf16[4,2,2,160,768]{4,3,2,1,0:T(8,128)(2,1)}, u32[]{:S(2)}, u32[]{:S(2)}) %all-to-all-start.5) | async-done | bytes 3932192 | tf_op jit(solution)/shard_map/all_to_all | solution.py:594
  452.8 55.9 %attention_back.1 = (bf16[4,256,768]{2,1,0:T(8,128)(2,1)}, f32[4,256,768]{2,1,0:T(8,128)}, bf16[768,3200]{1,0:T(8,128)(2,1)}) custom-call(bf16[4,256,768]{2,1,0:T(8,128)(2,1)} %bitcast.93, bf16[4,256,768]{2,1,0:T(8,128)(2,1)} %bitcast.80, s32[4,256,1]{2,1,0:T(8,128)} %broadcast_in_dim_reshape.5.column_ref, s32[4,1,256]{2,1,0:T(1,128)} %row_ref.3, ...), custom_call_target="tpu_custom_call" | custom-call | flops 15300820992 | bytes 34996224 | tf_op jit(solution)/shard_map/attention_back/pallas_call | solution.py:605
  508.7 3.5 dynamic-slice_bitcast_fusion
  513.7 3.5 collective-permute-done
  517.2 3.3 fusion
  523.5 6.1 collective-permute-done.5
  532.3 33.0 %collective-permute-done.1 = bf16[2,96,3200]{2,1,0:T(8,128)(2,1)} collective-permute-done((bf16[2,96,3200]{2,1,0:T(8,128)(2,1)S(1)}, bf16[2,96,3200]{2,1,0:T(8,128)(2,1)}, u32[]{:S(2)}, u32[]{:S(2)}) %collective-permute-start.1) | collective-permute-done | bytes 1228832 | tf_op jit(solution)/shard_map/ppermute | solution.py:60
  566.7 2.0 fusion.5
  569.4 22.3 %collective-permute-done.2 = bf16[96,3200]{1,0:T(8,128)(2,1)} collective-permute-done((bf16[96,3200]{1,0:T(8,128)(2,1)}, bf16[96,3200]{1,0:T(8,128)(2,1)}, u32[]{:S(2)}, u32[]{:S(2)}) %collective-permute-start.2) | collective-permute-done | bytes 614432 | tf_op jit(solution)/shard_map/ppermute | solution.py:60
  593.3 2.1 collective-permute-start.8
  595.4 14.5 %collective-permute-done.3 = bf16[96,3200]{1,0:T(8,128)(2,1)S(1)} collective-permute-done((bf16[96,3200]{1,0:T(8,128)(2,1)S(1)}, bf16[96,3200]{1,0:T(8,128)(2,1)S(1)}, u32[]{:S(2)}, u32[]{:S(2)}) %collective-permute-start.3) | collective-permute-done | bytes 614432 | tf_op jit(solution)/shard_map/ppermute | solution.py:640
  612.0 18.4 %collective-permute-done.8 = bf16[2304,128]{1,0:T(8,128)(2,1)S(1)} collective-permute-done((bf16[2304,128]{1,0:T(8,128)(2,1)S(1)}, bf16[2304,128]{1,0:T(8,128)(2,1)S(1)}, u32[]{:S(2)}, u32[]{:S(2)}) %collective-permute-start.8) | collective-permute-done | bytes 589856 | tf_op jit(solution)/shard_map/ppermute | solution.py:648
  631.7 2.9 unpack_shared.1
  634.7 3.7 unpack_experts.2
  638.4 3.7 unpack_experts.3
  (92 shorter events, 31.5 us)
Async XLA Ops:
  7.2 46.9 %all-gather.6.cloned.1.call-start = ((), (), s32[]{:S(2)}) async-start(), calls=%async_computation.8 | async-start | bytes 5529600 | tf_op jit(solution)/shard_map/all_gather | solution.py:497
  11.6 182.9 %all-gather.8.cloned.1.call-start = ((), (), s32[]{:S(2)}) async-start(), calls=%async_computation.11 | async-start | bytes 31850496 | tf_op jit(solution)/shard_map/all_gather | solution.py:500
  16.2 0.7 copy-start.4
  16.2 0.9 copy-start.5
  17.4 15.1 %copy-start.1 = (s32[4,1,256,2]{3,2,0,1:T(8,128)}, s32[4,1,256,2]{3,2,0,1:T(8,128)S(1)}, u32[]{:S(2)}) copy-start(s32[4,1,256,2]{3,2,0,1:T(8,128)S(1)} %copy.101) | copy-start | bytes 24580
  23.2 6.5 copy-start.6
  23.2 94.3 %all-to-all-start.1 = ((bf16[4,4,160,768]{3,2,1,0:T(8,128)(2,1)}), bf16[4,4,160,768]{3,2,1,0:T(8,128)(2,1)}, u32[]{:S(2)}, u32[]{:S(2)}) async-start(bf16[4,4,160,768]{3,2,1,0:T(8,128)(2,1)} %bitcast.61), calls=%async_computation.1 | async-start | bytes 7864320 | tf_op jit(solution)/shard_map/all_to_all | solution.py:519
  55.8 37.6 %copy-start.3 = (s32[4,2,256]{2,1,0:T(2,128)S(1)}, s32[4,2,256]{2,1,0:T(2,128)}, u32[]{:S(2)}) copy-start(s32[4,2,256]{2,1,0:T(2,128)} %copy.117.flat_ref) | copy-start | bytes 24580
  126.1 47.2 %all-to-all-start = ((bf16[4,2,160,768]{3,2,1,0:T(8,128)(2,1)}), bf16[4,2,160,768]{3,2,1,0:T(8,128)(2,1)S(1)}, u32[]{:S(2)}, u32[]{:S(2)}) async-start(bf16[4,2,160,768]{3,2,1,0:T(8,128)(2,1)} %bitcast.77), calls=%async_computation | async-start | bytes 3932160 | tf_op jit(solution)/shard_map/all_to_all | solution.py:519
  129.7 172.3 %all-gather.10.cloned.1.call-start = ((), (), s32[]{:S(2)}) async-start(), calls=%async_computation.12 | async-start | bytes 21233664 | tf_op jit(solution)/shard_map/all_gather | solution.py:500
  173.3 21.1 %copy-start.2 = (bf16[4,2,160,768]{3,2,1,0:T(8,128)(2,1)}, bf16[4,2,160,768]{3,2,1,0:T(8,128)(2,1)S(1)}, u32[]{:S(2)}) copy-start(bf16[4,2,160,768]{3,2,1,0:T(8,128)(2,1)S(1)} %all-to-all-done.refs_0_) | copy-start | bytes 5898244
  173.3 78.7 %all-to-all-start.3 = ((bf16[4,2,160,768]{3,2,1,0:T(8,128)(2,1)}), bf16[4,2,160,768]{3,2,1,0:T(8,128)(2,1)}, u32[]{:S(2)}, u32[]{:S(2)}) async-start(bf16[4,2,160,768]{3,2,1,0:T(8,128)(2,1)} %bitcast.17), calls=%async_computation.3 | async-start | bytes 3932160 | tf_op jit(solution)/shard_map/all_to_all | solution.py:519
  252.0 107.7 %all-to-all-start.4 = ((bf16[4,2,2,160,768]{4,3,2,1,0:T(8,128)(2,1)}), bf16[4,2,2,160,768]{4,3,2,1,0:T(8,128)(2,1)}, u32[]{:S(2)}, u32[]{:S(2)}) async-start(bf16[4,2,2,160,768]{4,3,2,1,0:T(8,128)(2,1)} %tie.5), calls=%async_computation.4 | async-start | bytes 7864320 | tf_op jit(solution)/shard_map/all_to_all | solution.py:594
  256.9 251.9 %reduce-scatter.3.cloned.1.call-start = ((), (), s32[]{:S(2)}) async-start(), calls=%async_computation.9 | async-start | bytes 31850496 | tf_op jit(solution)/shard_map/reduce_scatter | solution.py:664
  302.0 336.4 %reduce-scatter.5.cloned.1.call-start = ((), (), s32[]{:S(2)}) async-start(), calls=%async_computation.10 | async-start | bytes 21233664 | tf_op jit(solution)/shard_map/reduce_scatter | solution.py:664
  359.7 93.1 %all-to-all-start.5 = ((bf16[4,2,2,160,768]{4,3,2,1,0:T(8,128)(2,1)}), bf16[4,2,2,160,768]{4,3,2,1,0:T(8,128)(2,1)}, u32[]{:S(2)}, u32[]{:S(2)}) async-start(bf16[4,2,2,160,768]{4,3,2,1,0:T(8,128)(2,1)} %tie.6), calls=%async_computation.5 | async-start | bytes 7864320 | tf_op jit(solution)/shard_map/all_to_all | solution.py:594
  512.2 5.0 collective-permute-start
  513.6 15.9 %collective-permute-start.5 = (bf16[2304,128]{1,0:T(8,128)(2,1)S(1)}, bf16[2304,128]{1,0:T(8,128)(2,1)}, u32[]{:S(2)}, u32[]{:S(2)}) collective-permute-start(bf16[2304,128]{1,0:T(8,128)(2,1)S(1)} %constant_dynamic-slice_fusion.1), channel_id=1, source_target_pairs={{0,1},{1,0},{2,3},{3,2},{4,5},{5,4},{6,7},{7,6},{8,9},{9,8},{10,11... | collective-permute-start | bytes 1769480 | tf_op jit(solution)/shard_map/ppermute | solution.py:648
  520.5 1.4 copy-start
  522.0 43.3 %collective-permute-start.1 = (bf16[2,96,3200]{2,1,0:T(8,128)(2,1)S(1)}, bf16[2,96,3200]{2,1,0:T(8,128)(2,1)}, u32[]{:S(2)}, u32[]{:S(2)}) collective-permute-start(bf16[2,96,3200]{2,1,0:T(8,128)(2,1)S(1)} %pad_maximum_fusion), channel_id=1, source_target_pairs={{0,8},{4,20},{8,0},{12,28},{16,24},{20,4},{24,16},{28,12},{1,9},{5... | collective-permute-start | bytes 3686408 | tf_op jit(solution)/shard_map/ppermute | solution.py:60
  531.5 37.8 %collective-permute-start.6 = (bf16[1152,128]{1,0:T(8,128)(2,1)}, bf16[1152,128]{1,0:T(8,128)(2,1)S(1)}, u32[]{:S(2)}, u32[]{:S(2)}) collective-permute-start(bf16[1152,128]{1,0:T(8,128)(2,1)} %constant_dynamic-slice_fusion), channel_id=1, source_target_pairs={{0,2},{1,3},{2,0},{3,1},{4,6},{5,7},{6,4},{7,5},{8,10},{9,11},{10,... | collective-permute-start | bytes 884744 | tf_op jit(solution)/shard_map/ppermute | solution.py:648
  568.7 23.0 %collective-permute-start.2 = (bf16[96,3200]{1,0:T(8,128)(2,1)}, bf16[96,3200]{1,0:T(8,128)(2,1)}, u32[]{:S(2)}, u32[]{:S(2)}) collective-permute-start(bf16[96,3200]{1,0:T(8,128)(2,1)} %fusion.5), channel_id=1, source_target_pairs={{0,16},{4,12},{8,24},{12,4},{16,0},{20,28},{24,8},{28,20},{1,17},{... | collective-permute-start | bytes 1843208 | tf_op jit(solution)/shard_map/ppermute | solution.py:60
  569.4 23.9 %collective-permute-start.7 = (bf16[1152,128]{1,0:T(8,128)(2,1)S(1)}, bf16[1152,128]{1,0:T(8,128)(2,1)S(1)}, u32[]{:S(2)}, u32[]{:S(2)}) collective-permute-start(bf16[1152,128]{1,0:T(8,128)(2,1)S(1)} %add_convert_fusion.2), channel_id=1, source_target_pairs={{0,2},{1,3},{2,0},{3,1},{4,6},{5,7},{6,4},{7,5},{8,10},{9,11},{10,... | collective-permute-start | bytes 884744 | tf_op jit(solution)/shard_map/ppermute | solution.py:648
  593.2 16.8 %collective-permute-start.3 = (bf16[96,3200]{1,0:T(8,128)(2,1)S(1)}, bf16[96,3200]{1,0:T(8,128)(2,1)S(1)}, u32[]{:S(2)}, u32[]{:S(2)}) collective-permute-start(bf16[96,3200]{1,0:T(8,128)(2,1)S(1)} %fusion.3), channel_id=1, source_target_pairs={{0,1},{1,0},{2,3},{3,2},{4,5},{5,4},{6,7},{7,6},{8,9},{9,8},{10,11... | collective-permute-start | bytes 1843208 | tf_op jit(solution)/shard_map/ppermute | solution.py:640
  593.3 37.0 %collective-permute-start.8 = (bf16[2304,128]{1,0:T(8,128)(2,1)S(1)}, bf16[2304,128]{1,0:T(8,128)(2,1)S(1)}, u32[]{:S(2)}, u32[]{:S(2)}) collective-permute-start(bf16[2304,128]{1,0:T(8,128)(2,1)S(1)} %pad_maximum_fusion.2), channel_id=1, source_target_pairs={{0,1},{1,0},{2,3},{3,2},{4,5},{5,4},{6,7},{7,6},{8,9},{9,8},{10,11... | collective-permute-start | bytes 1769480 | tf_op jit(solution)/shard_map/ppermute | solution.py:648
  611.0 31.2 %collective-permute-start.4 = (bf16[96,3200]{1,0:T(8,128)(2,1)}, bf16[96,3200]{1,0:T(8,128)(2,1)S(1)}, u32[]{:S(2)}, u32[]{:S(2)}) collective-permute-start(bf16[96,3200]{1,0:T(8,128)(2,1)} %add_convert_fusion.refs_1_), channel_id=1, source_target_pairs={{0,2},{1,3},{2,0},{3,1},{4,6},{5,7},{6,4},{7,5},{8,10},{9,11},{10,... | collective-permute-start | bytes 1843208 | tf_op jit(solution)/shard_map/ppermute | solution.py:640
Sparse Core Ops, SparseCore 0:
  11.7 42.3 all-gather.5
  55.9 138.4 all-gather.7
  196.9 98.6 all-gather.9
  302.1 175.6 reduce-scatter.2
  481.2 146.1 reduce-scatter.4
